TPU v7x, 512 devices: a whole 4x4x16 slice. The times are simulated.
512 devices in a mesh: nodes: 128 (over x_lo, y, z), cols: 4 (over x_hi, core).
Axes of the slice: x: 4 (x_hi: 2, x_lo: 2; x = x_hi * 2 + x_lo), y: 4, z: 16, core: 2. Of those that a mesh axis runs over, the one named last changes fastest.
Arguments:
- vectors: bfloat16 [512, 4, 6, 16, 512], P('nodes', None, None, None, 'cols'), may hold values from -6 to 6
- node_shift: bfloat16 [512, 6, 16], P('nodes'), may hold values from 0.5 to 2
- coupling: float32 [4, 4], replicated, may hold values from -3 to 3
- dual_basis: bfloat16 [196608, 512], P(('nodes', 'cols')), may hold values from -0.013671875 to 0.013671875
Outputs:
- gram_matrix: float32 [512, 512], P('cols')
- rotated: bfloat16 [196608, 512], P(('nodes', 'cols'))
All inputs are finite; a program needn't handle non-finite values.
Results may differ from a plain program's by a relative error of at most 0.0064.
Values may be sent and summed in bfloat16 or wider, within the bound.
No kernel may reach another device: no remote copies, remote signals or barrier semaphores. Data moves between devices by JAX's collectives and lax.ppermute only.
A program may use at most 64 MiB of HBM per device.

v0:
```python
import jax
import jax.numpy as jnp
from jax import lax
from jax.sharding import Mesh
from jax.sharding import PartitionSpec as P

NODES = ("nodes_0", "nodes_1", "nodes_2")
COLS = ("cols_0", "cols_1")
NODES_COLS = ("nodes_0", "nodes_1", "nodes_2", "cols_0", "cols_1")


center_value = 10.0
half_width = 7.0


def with_halo(block, sides, width):
    for axis, dim in sides:
        count = lax.axis_size(axis)
        forward = [(i, i + 1) for i in range(count - 1)]
        backward = [(target, source) for source, target in forward]
        low = lax.ppermute(
            lax.slice_in_dim(block, block.shape[dim] - width, None, axis=dim), axis, forward
        )
        high = lax.ppermute(lax.slice_in_dim(block, 0, width, axis=dim), axis, backward)
        block = jnp.concatenate([low, block, high], axis=dim)
    return block


def rows_for(lines, devices):
    spare = -len(lines) % devices
    return jnp.pad(lines, [(0, spare)] + [(0, 0)] * (lines.ndim - 1))


def sum_in_order(blocks, axes, turns):
    inside = blocks.shape[1:]
    blocks = blocks.reshape(*(lax.axis_size(a) for a in axes), *inside)
    blocks = jnp.moveaxis(blocks, turns, range(len(axes))).reshape(-1, *inside)
    for k in turns:
        blocks = lax.psum_scatter(blocks, axes[k], scatter_dimension=0, tiled=True)
    return blocks[0]


def gather_in_order(array, axes, turns):
    blocks = array[None]
    for k in turns:
        blocks = lax.all_gather(blocks, axes[k], axis=0, tiled=True)
    current = [lax.axis_size(axes[k]) for k in reversed(turns)]
    blocks = blocks.reshape(*current, *array.shape)
    turned = sorted(range(len(turns)), key=lambda place: turns[len(turns) - 1 - place])
    return blocks.transpose(*turned, *range(len(turns), blocks.ndim)).reshape(-1, *array.shape)


def sum_all_axes(array, axes):
    devices, count = (lax.axis_size(axes), len(axes))
    lines = array.reshape(-1, *array.shape[1:][-1:])
    blocks = rows_for(lines, devices * count).reshape(count, devices, -1, *lines.shape[1:])
    outs = []
    for first in range(count):
        turns = [(first + k) % count for k in range(count)]
        own = sum_in_order(blocks[first], axes, turns)
        outs.append(gather_in_order(own, axes, turns[::-1]).reshape(-1, *lines.shape[1:]))
    return jnp.concatenate(outs)[: len(lines)].reshape(array.shape)


def operate_inner(padded, shift_part, coupling):
    middle = padded[1:-1]
    beside = padded[2:] + padded[:-2]
    spread = jnp.pad(middle, ((0, 0), (0, 0), (1, 1), (1, 1), (0, 0)))
    beside = beside + spread[:, :, 2:, 1:-1] + spread[:, :, :-2, 1:-1]
    beside = beside + spread[:, :, 1:-1, 2:] + spread[:, :, 1:-1, :-2]
    coupled = jnp.einsum("de,xeyzc->xdyzc", coupling, middle, precision=lax.Precision.HIGHEST)
    return (6.0 + shift_part[:, None, :, :, None]) * middle - beside + coupled


def shards(vectors, node_shift, coupling, dual_basis):
    layers = vectors.shape[0]
    wide_vectors, wide_shift = (
        with_halo(vectors, ((NODES, 0),), 3),
        with_halo(node_shift, ((NODES, 0),), 3),
    )
    shift_full = wide_shift.astype(jnp.float32)
    position = lax.axis_index(NODES) * layers - 3 + jnp.arange(layers + 6, dtype=jnp.int32)
    inside_mask = ((position >= 0) & (position < layers * lax.axis_size(NODES))).astype(jnp.float32)
    inside_mask = inside_mask[:, None, None, None, None]
    state_zero = wide_vectors.astype(jnp.float32)
    state_one = (
        operate_inner(state_zero, shift_full[1:-1], coupling) - center_value * state_zero[1:-1]
    ) / half_width
    state_one = state_one * inside_mask[1:-1]
    state_two = (
        2.0
        * (operate_inner(state_one, shift_full[2:-2], coupling) - center_value * state_one[1:-1])
        / half_width
        - state_zero[2:-2]
    )
    state_two = state_two * inside_mask[2:-2]
    state_three = (
        2.0
        * (operate_inner(state_two, shift_full[3:-3], coupling) - center_value * state_two[1:-1])
        / half_width
        - state_one[2:-2]
    )
    filtered = state_three.astype(jnp.bfloat16).reshape(-1, state_three.shape[-1])
    row_stack = lax.all_to_all(filtered, COLS, split_axis=0, concat_axis=1, tiled=True)
    partial_gram = lax.dot_general(
        dual_basis, row_stack, (((0,), (0,)), ((), ())), preferred_element_type=jnp.float32
    )
    vector_count = dual_basis.shape[1]
    share_rows = vector_count // lax.axis_size(COLS)
    gram_full = sum_all_axes(partial_gram, NODES_COLS)
    own_rows = lax.dynamic_slice_in_dim(gram_full, lax.axis_index(COLS) * share_rows, share_rows, 0)
    rotated_sum = jnp.dot(
        row_stack, gram_full.astype(jnp.bfloat16), preferred_element_type=jnp.float32
    )
    rotated = (rotated_sum * vector_count ** (-0.5)).astype(jnp.bfloat16)
    return (own_rows, rotated)


def solution(mesh):
    torus = Mesh(
        mesh.devices.reshape(2, 4, 16, 2, 2), ("nodes_0", "nodes_1", "nodes_2", "cols_0", "cols_1")
    )
    placed = (P(NODES, None, None, None, COLS), P(NODES, None, None), P(), P(NODES_COLS, None))
    return jax.shard_map(
        shards,
        mesh=torus,
        in_specs=placed,
        out_specs=(P(COLS, None), P(NODES_COLS, None)),
        check_vma=False,
    )
```

profile of v0, /device:TPU:1, one launch (start us, length us, event | category | flops | bytes accessed | tf_op | source)
XLA Modules:
  0.0 391.4 jit_solution(9766292862398771426)
XLA Ops:
  7.2 0.8 fusion.35
  8.0 4.4 %collective-permute-start = (bf16[3,6,16]{2,0,1:T(4,128)(2,1)S(1)}, bf16[3,6,16]{2,0,1:T(4,128)(2,1)S(1)}, u32[]{:S(2)}, u32[]{:S(2)}) collective-permute-start(bf16[3,6,16]{2,0,1:T(4,128)(2,1)S(1)} %get-tuple-element.4), channel_id=1, source_target_pairs={{0,4},{4,8},{8,12},{12,16},{16,20},{20,24},{24,28},{28,32},{32,36}... | collective-permute-start | bytes 1736 | tf_op jit(solution)/shard_map/ppermute | solution.py:21
  12.4 1.4 collective-permute-start.1
  13.8 1.1 fusion.34
  15.1 4.2 %collective-permute-start.2 = (bf16[3,4,6,16,128]{4,1,3,2,0:T(4,128)(2,1)S(1)}, bf16[3,4,6,16,128]{4,1,3,2,0:T(4,128)(2,1)S(1)}, u32[]{:S(2)}, u32[]{:S(2)}) collective-permute-start(bf16[3,4,6,16,128]{4,1,3,2,0:T(4,128)(2,1)S(1)} %copy.33), channel_id=1, source_target_pairs={{0,4},{4,8},{8,12},{12,16},{16,20},{20,24},{24,28},{28,32},{32,36}... | collective-permute-start | bytes 884744 | tf_op jit(solution)/shard_map/ppermute | solution.py:21
  19.4 1.3 collective-permute-start.3
  21.0 1.9 collective-permute-done.2
  23.3 3.8 collective-permute-done.3
  28.1 3.3 fusion.7
  31.5 4.2 %fusion.19 = f32[6,4,6,16,128]{4,1,3,2,0:T(4,128)S(1)} fusion(f32[10,4,6,16,128]{4,1,3,2,0:T(4,128)S(1)} %convert_element_type.30, f32[6,4,6,16,128]{4,1,3,2,0:T(4,128)S(1)} %slice.149, f32[8,4,6,16,128]{4,1,3,2,0:T(4,128)S(1)} %fusion.7, f32[6]{0:T(128)S(1)} %slice.133, f32[6,6,16]{2,1,0:T(8,128)S(1)} %copy.22, f32[4,4]{1,0:T(4,128)S(1)} %copy-done.3), kind=kOutput, calls=%fused_computation.37 | convolution fusion | flops 17989632 | bytes 7498240 | tf_op jit(solution)/shard_map/de,xeyzc->xdyzc/dot_general | solution.py:71
  35.8 2.8 fusion.26
  38.7 15.8 %all_to_all.19 = bf16[4,384,128]{2,1,0:T(8,128)(2,1)S(1)} all-to-all(bf16[4,384,128]{2,1,0:T(8,128)(2,1)S(1)} %bitcast.55), channel_id=1, replica_groups=mesh['nodes_0'=2,'nodes_1'=4,'nodes_2'=16,'cols_0'=2,'cols_1'=2] {'cols_..., dimensions={0} | all-to-all | bytes 786432 | tf_op jit(solution)/shard_map/all_to_all | solution.py:104
  54.7 1.4 convolution_bitcast_fusion.1
  56.2 34.9 %reduce-scatter.2.cloned.1.call-done = f32[256,1,512]{0,2,1:T(8,128)} async-done(((f32[512,1,512]{0,2,1:T(8,128)}), f32[256,1,512]{0,2,1:T(8,128)}) %reduce-scatter.2.cloned.1.call-update) | async-done | bytes 524304 | tf_op jit(solution)/shard_map/reduce_scatter | solution.py:39
  91.0 1.9 copy.29
  93.1 1.3 dynamic-slice.1
  95.0 55.9 %all-reduce.10.cloned.1.call-done = f32[256,1,512]{2,1,0:T(1,128)} async-done(((f32[256,1,512]{2,1,0:T(1,128)}), f32[256,1,512]{2,1,0:T(1,128)}) %all-reduce.10.cloned.1.call-update) | async-done | bytes 524304
  150.9 1.6 constant_dynamic-slice_fusion.3
  152.6 1.3 dynamic-slice.7
  153.9 1.3 dynamic-slice.5
  155.2 1.3 dynamic-slice.3
  157.7 126.2 %all-reduce.12.cloned.1.call-done = f32[64,1,512]{2,1,0:T(1,128)} async-done(((f32[64,1,512]{2,1,0:T(1,128)}), f32[64,1,512]{2,1,0:T(1,128)}) %all-reduce.12.cloned.1.call-update) | async-done | bytes 131088
  284.6 5.3 %all-reduce.5 = f32[4,1,512]{2,1,0:T(1,128)S(1)} all-reduce(f32[4,1,512]{2,1,0:T(1,128)S(1)} %constant_dynamic-slice_fusion.2), channel_id=5, replica_groups=mesh['nodes_0'=2,'nodes_1'=4,'nodes_2'=16,'cols_0'=2,'cols_1'=2] {'cols_0'}, use_global_device_ids=true, to_apply=%region_3.4.clone | all-reduce | flops 2048 | bytes 16384
  289.9 13.1 %all-reduce.6 = f32[2,1,512]{2,1,0:T(1,128)S(1)} all-reduce(f32[2,1,512]{2,1,0:T(1,128)S(1)} %constant_dynamic-slice_fusion.1), channel_id=6, replica_groups=mesh['nodes_0'=2,'nodes_1'=4,'nodes_2'=16,'cols_0'=2,'cols_1'=2] {'cols_1'}, use_global_device_ids=true, to_apply=%region_4.5.clone | all-reduce | flops 1024 | bytes 8192
  303.7 1.8 all_gather.10
  305.5 4.7 %all_gather.11 = f32[4,1,512]{2,1,0:T(1,128)S(1)} all-gather(f32[2,1,512]{2,1,0:T(1,128)S(1)} %all_gather.10), channel_id=1, replica_groups=mesh['nodes_0'=2,'nodes_1'=4,'nodes_2'=16,'cols_0'=2,'cols_1'=2] {'cols_0'}, dimensions={0}, use_global_device_ids=true | all-gather | bytes 12288 | tf_op jit(solution)/shard_map/all_gather | solution.py:46
  310.2 22.0 %all_gather.12 = f32[64,1,512]{2,1,0:T(1,128)S(1)} all-gather(f32[4,1,512]{2,1,0:T(1,128)S(1)} %all_gather.11), channel_id=1, replica_groups=mesh['nodes_0'=2,'nodes_1'=4,'nodes_2'=16,'cols_0'=2,'cols_1'=2] {'nodes..., dimensions={0}, use_global_device_ids=true | all-gather | bytes 139264 | tf_op jit(solution)/shard_map/all_gather | solution.py:46
  332.2 10.2 %all_gather.13 = f32[256,1,512]{2,1,0:T(1,128)S(1)} all-gather(f32[64,1,512]{2,1,0:T(1,128)S(1)} %all_gather.12), channel_id=1, replica_groups=mesh['nodes_0'=2,'nodes_1'=4,'nodes_2'=16,'cols_0'=2,'cols_1'=2] {'nodes..., dimensions={0}, use_global_device_ids=true | all-gather | bytes 655360 | tf_op jit(solution)/shard_map/all_gather | solution.py:46
  342.5 0.8 copy.30
  343.3 37.5 %all-gather.2.cloned.1.call-done = f32[512,1,512]{2,0,1:T(8,128)} async-done(((f32[256,1,512]{2,0,1:T(8,128)}), f32[512,1,512]{2,0,1:T(8,128)}) %all-gather.2.cloned.1.call-update) | async-done | bytes 1048592 | tf_op jit(solution)/shard_map/all_gather | solution.py:46
  380.8 2.4 fusion.11
  383.2 1.7 dynamic-slice_bitcast_fusion
  (42 shorter events, 3.9 us)
Async XLA Ops:
  7.2 47.5 %copy-start = (bf16[384,512]{1,0:T(8,128)(2,1)S(1)}, bf16[384,512]{1,0:T(8,128)(2,1)}, u32[]{:S(2)}) copy-start(bf16[384,512]{1,0:T(8,128)(2,1)} %param.7) | copy-start | bytes 1179652
  7.2 13.7 %copy-start.2 = (bf16[4,6,16]{2,0,1:T(4,128)(2,1)S(1)}, bf16[4,6,16]{2,0,1:T(4,128)(2,1)}, u32[]{:S(2)}) copy-start(bf16[4,6,16]{2,0,1:T(4,128)(2,1)} %param.5) | copy-start | bytes 2308
  7.2 83.9 %reduce-scatter.2.cloned.1.call-start = ((), (), s32[]{:S(2)}) async-start(), calls=%async_computation.2 | async-start | bytes 1572864 | tf_op jit(solution)/shard_map/reduce_scatter | solution.py:39
  8.0 12.9 %collective-permute-start = (bf16[3,6,16]{2,0,1:T(4,128)(2,1)S(1)}, bf16[3,6,16]{2,0,1:T(4,128)(2,1)S(1)}, u32[]{:S(2)}, u32[]{:S(2)}) collective-permute-start(bf16[3,6,16]{2,0,1:T(4,128)(2,1)S(1)} %get-tuple-element.4), channel_id=1, source_target_pairs={{0,4},{4,8},{8,12},{12,16},{16,20},{20,24},{24,28},{28,32},{32,36}... | collective-permute-start | bytes 1736 | tf_op jit(solution)/shard_map/ppermute | solution.py:21
  12.4 10.7 %copy-start.1 = (bf16[4,4,6,16,128]{4,3,2,1,0:T(8,128)(2,1)S(1)}, bf16[4,4,6,16,128]{4,3,2,1,0:T(8,128)(2,1)}, u32[]{:S(2)}) copy-start(bf16[4,4,6,16,128]{4,3,2,1,0:T(8,128)(2,1)} %param.4) | copy-start | bytes 1179652
  12.4 8.5 %collective-permute-start.1 = (bf16[3,6,16]{2,0,1:T(4,128)(2,1)S(1)}, bf16[3,6,16]{2,0,1:T(4,128)(2,1)S(1)}, u32[]{:S(2)}, u32[]{:S(2)}) collective-permute-start(bf16[3,6,16]{2,0,1:T(4,128)(2,1)S(1)} %get-tuple-element.5), channel_id=1, source_target_pairs={{4,0},{8,4},{12,8},{16,12},{20,16},{24,20},{28,24},{32,28},{36,32}... | collective-permute-start | bytes 1736 | tf_op jit(solution)/shard_map/ppermute | solution.py:24
  15.1 7.8 %collective-permute-start.2 = (bf16[3,4,6,16,128]{4,1,3,2,0:T(4,128)(2,1)S(1)}, bf16[3,4,6,16,128]{4,1,3,2,0:T(4,128)(2,1)S(1)}, u32[]{:S(2)}, u32[]{:S(2)}) collective-permute-start(bf16[3,4,6,16,128]{4,1,3,2,0:T(4,128)(2,1)S(1)} %copy.33), channel_id=1, source_target_pairs={{0,4},{4,8},{8,12},{12,16},{16,20},{20,24},{24,28},{28,32},{32,36}... | collective-permute-start | bytes 884744 | tf_op jit(solution)/shard_map/ppermute | solution.py:21
  19.4 7.6 %collective-permute-start.3 = (bf16[3,4,6,16,128]{4,1,3,2,0:T(4,128)(2,1)S(1)}, bf16[3,4,6,16,128]{4,1,3,2,0:T(4,128)(2,1)S(1)}, u32[]{:S(2)}, u32[]{:S(2)}) collective-permute-start(bf16[3,4,6,16,128]{4,1,3,2,0:T(4,128)(2,1)S(1)} %copy.34), channel_id=1, source_target_pairs={{4,0},{8,4},{12,8},{16,12},{20,16},{24,20},{28,24},{32,28},{36,32}... | collective-permute-start | bytes 884744 | tf_op jit(solution)/shard_map/ppermute | solution.py:24
  27.4 0.7 copy-start.3
  56.1 94.8 %all-reduce.10.cloned.1.call-start = ((), (), s32[]{:S(2)}) async-start(), calls=%async_computation.4 | async-start | bytes 1048576
  93.0 190.9 %all-reduce.12.cloned.1.call-start = ((), (), s32[]{:S(2)}) async-start(), calls=%async_computation.5 | async-start | bytes 262144
  152.5 228.3 %all-gather.2.cloned.1.call-start = ((), (), s32[]{:S(2)}) async-start(), calls=%async_computation.3 | async-start | bytes 1572864 | tf_op jit(solution)/shard_map/all_gather | solution.py:46
Sparse Core Ops, SparseCore 0:
  56.2 34.7 reduce-scatter.1
  93.4 57.4 all-reduce.9
  153.8 130.0 all-reduce.11
  343.5 37.3 all-gather.1
where the time goes:
time: 392 us; the launch traced here: 391 us
  waiting for transfers between devices  260 us (66%)
  blocking collectives  73 us (19%)
  local copies, waits for them, and re-layouts  16.3 us (4%)
  between operations  16 us (4%)
  matrix products  14.1 us (4%)
  starting transfers between devices  11.4 us (3%)
    unnamed x6, waiting for transfers between devices  182 us
    all_gather x4, blocking collectives, gather_in_order(): blocks = lax.all_gather(blocks, axes[k], axis=0, tiled=True)  38.8 us
    all_gather x1, waiting for transfers between devices, gather_in_order(): blocks = lax.all_gather(blocks, axes[k], axis=0, tiled=True)  37.5 us
    reduce_scatter x1, waiting for transfers between devices, sum_in_order(): blocks = lax.psum_scatter(blocks, axes[k], scatter_dimension=0, tiled=True)  34.9 us
    unnamed x2, blocking collectives  18.4 us
    all_to_all x1, blocking collectives, shards(): lax.all_to_all(filtered, COLS, split_axis=0, concat_axis=1, tiled=True)  15.8 us
    dot_general x3, matrix products, operate_inner(): jnp.einsum('de,xeyzc->xdyzc', coupling, middle, precision=lax.Precision.H...  10.3 us
    unnamed x20, local copies, waits for them, and re-layouts  9.17 us
  transfers between devices with their start and end apart: 8, of which 6 were waited for; matrix products, arithmetic and copies ran while one was open for 2% of the time, Pallas kernels for 0%

commit v1 on v0

v1 whole, which is shorter than its diff:
```python
import functools

import jax
import jax.numpy as jnp
from jax import lax
from jax.experimental import pallas as pl
from jax.experimental.pallas import tpu as pltpu
from jax.sharding import Mesh
from jax.sharding import PartitionSpec as P

NODES = ("x_lo", "y", "z_hi", "z_lo")
COLS = ("x_hi", "core")
NEAR = ("x_lo", "y", "z_lo", "x_hi", "core")
FAR = "z_hi"
REACH = 3
TILE_ROWS = 16
LANES = 128

bf16 = jnp.bfloat16
f32 = jnp.float32


def vmem(count):
    return [pl.BlockSpec(memory_space=pltpu.VMEM)] * count


def smem(count):
    return [pl.BlockSpec(memory_space=pltpu.SMEM)] * count


def room(mebibytes):
    return pltpu.CompilerParams(vmem_limit_bytes=mebibytes << 20)


def pack_kernel(v_ref, shift_ref, up_ref, down_ref):
    layers, rows = v_ref.shape[0], v_ref.shape[1]
    for k in range(REACH):
        up_ref[k * rows : (k + 1) * rows, :] = v_ref[layers - REACH + k]
        down_ref[k * rows : (k + 1) * rows, :] = v_ref[k]
    up_ref[REACH * rows :, :] = shift_ref[...]
    down_ref[REACH * rows :, :] = shift_ref[...]


def filter_kernel(
    gy, dofs, coup_ref, place_ref, v_ref, low_ref, high_ref, shift_ref, out_ref, s0, s1, s2, diag
):
    layers = v_ref.shape[0]
    gz = TILE_ROWS
    rows = dofs * gy * gz
    tiles = dofs * gy
    low_in = place_ref[0].astype(f32)
    high_in = place_ref[1].astype(f32)

    def shift_cols(ref, first, layer, slot):
        tile = ref[first : first + gz, :].astype(f32)
        for y in range(gy):
            k = layer * gy + y
            diag[slot, y] = jnp.broadcast_to(tile[:, k : k + 1], (gz, LANES)) - 4.0

    for k in range(2):
        shift_cols(low_ref, REACH * rows, layers - 2 + k, k)
        shift_cols(high_ref, REACH * rows, k, 2 + layers + k)
    for k in range(layers):
        shift_cols(shift_ref, 0, k, 2 + k)

    for t in range(tiles):
        for k in range(REACH):
            at = k * rows + t * gz
            s0[k, t] = low_ref[at : at + gz, :].astype(f32)
            s0[REACH + layers + k, t] = high_ref[at : at + gz, :].astype(f32)
        for k in range(layers):
            s0[REACH + k, t] = v_ref[k, t * gz : (t + 1) * gz, :].astype(f32)

    row = lax.broadcasted_iota(jnp.int32, (gz, LANES), 0)
    top, bottom = row == 0, row == gz - 1
    coup = [[coup_ref[d, e] for e in range(dofs)] for d in range(dofs)]

    def apply(src, at, dslot, emit):
        for y in range(gy):
            mid = [src[at, d * gy + y] for d in range(dofs)]
            dg = diag[dslot, y]
            for d in range(dofs):
                t = d * gy + y
                near = src[at - 1, t] + src[at + 1, t]
                if y > 0:
                    near = near + src[at, t - 1]
                if y < gy - 1:
                    near = near + src[at, t + 1]
                near = near + jnp.where(top, 0.0, pltpu.roll(mid[d], 1, 0))
                near = near + jnp.where(bottom, 0.0, pltpu.roll(mid[d], gz - 1, 0))
                total = (dg + coup[d][d]) * mid[d] - near
                for e in range(dofs):
                    if e != d:
                        total = total + coup[d][e] * mid[e]
                emit(t, total)

    def outside(layer):
        keep = jnp.where(layer < 0, low_in, jnp.where(layer >= layers, high_in, 1.0))
        return keep

    @pl.loop(0, layers + 4)
    def _(i):
        keep = outside(i - 2)

        def emit(t, total):
            s1[i, t] = total * keep

        apply(s0, i + 1, i, emit)

    @pl.loop(0, layers + 2)
    def _(i):
        keep = outside(i - 1)

        def emit(t, total):
            s2[i, t] = (total - 24.5 * s0[i + 2, t]) * keep

        apply(s1, i + 1, i + 1, emit)

    @pl.loop(0, layers)
    def _(i):
        def emit(t, total):
            last = (total - 12.25 * s1[i + 2, t]) * (4.0 / 343.0)
            out_ref[i, t * gz : (t + 1) * gz, :] = last.astype(bf16)

        apply(s2, i + 1, i + 2, emit)


def side_by_side(parts):
    return jnp.concatenate(parts, axis=1)


def gram_kernel(dual_ref, f_ref, out_ref):
    blocks = f_ref.shape[0]
    pieces, height, _ = out_ref.shape
    each = pieces // blocks
    dual = dual_ref[...]
    for b in range(0, blocks, 2):
        pair = side_by_side([f_ref[b], f_ref[b + 1]])
        part = lax.dot_general(dual, pair, (((0,), (0,)), ((), ())), preferred_element_type=f32)
        for k in range(2):
            cut = part[:, k * LANES : (k + 1) * LANES].astype(bf16)
            out_ref[(b + k) * each : (b + k + 1) * each] = cut.reshape(each, height, LANES)


def sum_kernel(in_ref, out_ref):
    count = in_ref.shape[0]
    total = in_ref[0].astype(f32)
    for k in range(1, count):
        total = total + in_ref[k].astype(f32)
    piece = total.astype(bf16)
    for k in range(out_ref.shape[0]):
        out_ref[k] = piece


def rotate_kernel(scale, place_ref, f_ref, g_ref, gram_ref, out_ref):
    blocks, rows, _ = f_ref.shape
    pieces, height, _ = g_ref.shape
    each = pieces // blocks
    own = each // blocks
    cols = side_by_side([f_ref[b] for b in range(blocks)])
    first = place_ref[2] * own
    for b in range(0, blocks, 2):
        pair = side_by_side(
            [g_ref[k * each : (k + 1) * each].reshape(each * height, LANES) for k in (b, b + 1)]
        )
        turned = jnp.dot(cols, pair, preferred_element_type=f32) * scale
        out_ref[:, b * LANES : (b + 2) * LANES] = turned.astype(bf16)
        for k in (b, b + 1):
            mine = g_ref[pl.ds(k * each + first, own)].reshape(own * height, LANES)
            gram_ref[:, k * LANES : (k + 1) * LANES] = mine.astype(f32)


def shards(vectors, node_shift, coupling, dual_basis):
    layers, dofs, gy, gz, width = vectors.shape
    rows = dofs * gy * gz
    count = lax.axis_size(NODES)
    near = lax.axis_size(NEAR)
    far = lax.axis_size(FAR)
    blocks = lax.axis_size(COLS)
    cols = blocks * width
    height = cols * blocks // near
    v = vectors.reshape(layers, rows, width)
    shift_tile = jnp.pad(
        node_shift.transpose(2, 0, 1).reshape(gz, layers * gy), ((0, 0), (0, LANES - layers * gy))
    )
    message = jax.ShapeDtypeStruct((REACH * rows + gz, width), bf16)
    up, down = pl.pallas_call(
        pack_kernel, out_shape=(message, message), in_specs=vmem(2), out_specs=tuple(vmem(2)),
        compiler_params=room(8), name="pack",
    )(v, shift_tile)
    low = lax.ppermute(up, NODES, [(i, i + 1) for i in range(count - 1)])
    high = lax.ppermute(down, NODES, [(i + 1, i) for i in range(count - 1)])
    node = lax.axis_index(NODES)
    place = jnp.stack([node > 0, node < count - 1, lax.axis_index(COLS)]).astype(jnp.int32)
    tiles = dofs * gy
    own = pl.pallas_call(
        functools.partial(filter_kernel, gy, dofs),
        out_shape=jax.ShapeDtypeStruct((layers, rows, width), bf16),
        in_specs=smem(2) + vmem(4),
        out_specs=vmem(1)[0],
        scratch_shapes=[
            pltpu.VMEM((layers + 6, tiles, gz, width), f32),
            pltpu.VMEM((layers + 4, tiles, gz, width), f32),
            pltpu.VMEM((layers + 2, tiles, gz, width), f32),
            pltpu.VMEM((layers + 4, gy, gz, width), f32),
        ],
        compiler_params=room(16), name="filter",
    )(coupling, place, v, low, high, shift_tile)
    mine = lax.all_to_all(own, COLS, split_axis=0, concat_axis=0, tiled=True)
    terms = pl.pallas_call(
        gram_kernel,
        out_shape=jax.ShapeDtypeStruct((near, height, LANES), bf16),
        in_specs=vmem(2), out_specs=vmem(1)[0], compiler_params=room(8), name="gram",
    )(dual_basis, mine)

    def summed(pieces, copies, name):
        return pl.pallas_call(
            sum_kernel,
            out_shape=jax.ShapeDtypeStruct((copies, height, LANES), bf16),
            in_specs=vmem(1), out_specs=vmem(1)[0], compiler_params=room(8), name=name,
        )(pieces)

    pieces = lax.all_to_all(terms, NEAR, split_axis=0, concat_axis=0, tiled=True)
    pieces = lax.all_to_all(summed(pieces, far, "near_sum"), FAR, split_axis=0, concat_axis=0, tiled=True)
    pieces = lax.all_to_all(summed(pieces, near, "far_sum"), NEAR, split_axis=0, concat_axis=0, tiled=True)
    gram, rotated = pl.pallas_call(
        functools.partial(rotate_kernel, cols ** (-0.5)),
        out_shape=(
            jax.ShapeDtypeStruct((cols // blocks, cols), f32),
            jax.ShapeDtypeStruct((rows, cols), bf16),
        ),
        in_specs=smem(1) + vmem(2), out_specs=tuple(vmem(2)), compiler_params=room(12), name="rotate",
    )(place, mine, pieces)
    return gram, rotated


SIZES = (2, 4, 8, 2, 2, 2)


def solution(mesh):
    torus = Mesh(mesh.devices.reshape(SIZES), NODES + COLS)
    placed = (P(NODES, None, None, None, COLS), P(NODES, None, None), P(), P(NODES + COLS, None))
    return jax.shard_map(
        shards,
        mesh=torus,
        in_specs=placed,
        out_specs=(P(COLS, None), P(NODES + COLS, None)),
        check_vma=False,
    )
```

time: 392 us -> 100 us (0.26)
  waiting for transfers between devices: 260 us -> 6.27 us
  between operations: 16 us -> 0.71 us
  local copies, waits for them, and re-layouts: 16.3 us -> 1.92 us
  matrix products: 14.1 us -> 0 us
  blocking collectives: 73 us -> 79.2 us
  Pallas kernels: 0 us -> 5.72 us
  starting transfers between devices: 11.4 us -> 5.8 us
    unnamed x6 -> x0, waiting for transfers between devices: 182 us -> none
    all_to_all x1 -> x4, blocking collectives: 15.8 us -> 79.2 us  [the longest x1 23.6 us: shards(): lax.all_to_all(terms, NEAR, split_axis=0, concat_axis=0, tiled=True)]
    all_gather x4 -> x0, blocking collectives: 38.8 us -> none  [gather_in_order(): blocks = lax.all_gather(blocks, axes[k], axis=0, tiled=True)]
    all_gather x1 -> x0, waiting for transfers between devices: 37.5 us -> none  [gather_in_order(): blocks = lax.all_gather(blocks, axes[k], axis=0, tiled=True)]
    reduce_scatter x1 -> x0, waiting for transfers between devices: 34.9 us -> none  [sum_in_order(): blocks = lax.psum_scatter(blocks, axes[k], scatter_dimension=0, tiled=True)]
    unnamed x2 -> x0, blocking collectives: 18.4 us -> none
    dot_general x5 -> x0, matrix products: 14.1 us -> none  [the longest x3 10.3 us: operate_inner(): jnp.einsum('de,xeyzc->xdyzc', coupling, middle, precision=lax.Precision.H...]
    unnamed x20 -> x8, local copies, waits for them, and re-layouts: 9.17 us -> 1.01 us
  transfers between devices with their start and end apart: 8 -> 2, of which waited for: 6 -> 2; matrix products, arithmetic and copies ran while one was open for 2% -> 0% of each run, Pallas kernels for 0% -> 0%
where the time goes in v1:
time: 100 us; the launch traced here: 99.7 us
  blocking collectives  79.2 us (79%)
  waiting for transfers between devices  6.27 us (6%)
  starting transfers between devices  5.8 us (6%)
  Pallas kernels  5.72 us (6%)
  local copies, waits for them, and re-layouts  1.92 us (2%)
    all_to_all x1, blocking collectives, shards(): lax.all_to_all(terms, NEAR, split_axis=0, concat_axis=0, tiled=True)  23.6 us
    all_to_all x1, blocking collectives, shards(): lax.all_to_all(summed(pieces, far, 'near_sum'), FAR, split_axis=0, concat...  21 us
    all_to_all x1, blocking collectives, shards(): lax.all_to_all(summed(pieces, near, 'far_sum'), NEAR, split_axis=0, conca...  18.6 us
    all_to_all x1, blocking collectives, shards(): mine = lax.all_to_all(own, COLS, split_axis=0, concat_axis=0, tiled=True)  16 us
    ppermute x1, starting transfers between devices, shards(): low = lax.ppermute(up, NODES, [(i, i + 1) for i in range(count - 1)])  4.51 us
    ppermute x1, waiting for transfers between devices, shards(): high = lax.ppermute(down, NODES, [(i + 1, i) for i in range(count - 1)])  4 us
    pallas_call x1, Pallas kernels, shards(): pl.pallas_call(functools.partial(filter_kernel, gy, dofs), out_shape=jax....  3.34 us
    ppermute x1, waiting for transfers between devices, shards(): low = lax.ppermute(up, NODES, [(i, i + 1) for i in range(count - 1)])  2.27 us
  transfers between devices with their start and end apart: 2, of which 2 were waited for; matrix products, arithmetic and copies ran while one was open for 0% of the time, Pallas kernels for 0%

profile of v1, /device:TPU:1, one launch (start us, length us, event | category | flops | bytes accessed | tf_op | source)
XLA Modules:
  0.0 99.7 jit_solution(7850777345261381444)
XLA Ops:
  0.6 0.8 copy.9
  1.4 0.1 reshape.14
  1.5 0.0 copy-start
  1.5 1.0 copy-done
  2.5 0.0 copy-start.1
  2.5 0.1 pack.1
  2.6 4.5 %collective-permute-start = (bf16[1168,128]{1,0:T(8,128)(2,1)S(1)}, bf16[1168,128]{1,0:T(8,128)(2,1)S(1)}, u32[]{:S(2)}, u32[]{:S(2)}) collective-permute-start(bf16[1168,128]{1,0:T(8,128)(2,1)S(1)} %get-tuple-element.4), channel_id=1, source_target_pairs={{0,4},{4,8},{8,12},{12,16},{16,20},{20,24},{24,28},{28,32},{32,36}... | collective-permute-start | bytes 897032 | tf_op jit(solution)/shard_map/ppermute | solution.py:191
  7.1 1.3 %collective-permute-start.1 = (bf16[1168,128]{1,0:T(8,128)(2,1)S(1)}, bf16[1168,128]{1,0:T(8,128)(2,1)S(1)}, u32[]{:S(2)}, u32[]{:S(2)}) collective-permute-start(bf16[1168,128]{1,0:T(8,128)(2,1)S(1)} %get-tuple-element.5), channel_id=1, source_target_pairs={{4,0},{8,4},{12,8},{16,12},{20,16},{24,20},{28,24},{32,28},{36,32}... | collective-permute-start | bytes 897032 | tf_op jit(solution)/shard_map/ppermute | solution.py:192
  8.4 0.0 copy-start.3
  8.5 0.1 pad_add_fusion.place_ref
  8.5 2.3 %collective-permute-done.low_ref = bf16[1168,128]{1,0:T(8,128)(2,1)S(1)} collective-permute-done((bf16[1168,128]{1,0:T(8,128)(2,1)S(1)}, bf16[1168,128]{1,0:T(8,128)(2,1)S(1)}, u32[]{:S(2)}, u32[]{:S(2)}) %collective-permute-start) | collective-permute-done | bytes 299040 | tf_op jit(solution)/shard_map/ppermute | solution.py:191
  10.8 4.0 %collective-permute-done.1.high_ref = bf16[1168,128]{1,0:T(8,128)(2,1)S(1)} collective-permute-done((bf16[1168,128]{1,0:T(8,128)(2,1)S(1)}, bf16[1168,128]{1,0:T(8,128)(2,1)S(1)}, u32[]{:S(2)}, u32[]{:S(2)}) %collective-permute-start.1) | collective-permute-done | bytes 299040 | tf_op jit(solution)/shard_map/ppermute | solution.py:192
  14.8 0.0 copy-done.1
  14.8 0.0 copy-done.3
  14.8 3.3 %filter.1 = bf16[4,384,128]{2,1,0:T(8,128)(2,1)S(1)} custom-call(f32[4,4]{1,0:T(4,128)S(1)} %copy-done.3, s32[3]{0:T(128)S(1)} %pad_add_fusion.place_ref, bf16[4,384,128]{2,1,0:T(8,128)(2,1)S(1)} %bitcast.6, bf16[1168,128]{1,0:T(8,128)(2,1)S(1)} %collective-permute-done.low_ref, bf16[1168,128]{1,0:T(8,128)(2,1)S(1)} %collective-permute-done.1.high_ref, ...), custom_call_target="tpu_custom_call" | custom-call | tf_op jit(solution)/shard_map/filter/pallas_call | solution.py:196
  18.2 0.0 copy-start.2
  18.2 16.0 %all_to_all.20.f_ref = bf16[4,384,128]{2,1,0:T(8,128)(2,1)S(1)} all-to-all(bf16[4,384,128]{2,1,0:T(8,128)(2,1)S(1)} %filter.1), channel_id=1, replica_groups=mesh['x_lo'=2,'y'=4,'z_hi'=8,'z_lo'=2,'x_hi'=2,'core'=2] {'x_hi','core'}, dimensions={0} | all-to-all | bytes 786432 | tf_op jit(solution)/shard_map/all_to_all | solution.py:209
  34.2 0.0 copy-done.2
  34.2 0.5 gram.1
  34.6 23.6 %all_to_all.21.in_ref = bf16[64,32,128]{2,1,0:T(8,128)(2,1)S(1)} all-to-all(bf16[64,32,128]{2,1,0:T(8,128)(2,1)S(1)} %gram.1), channel_id=1, replica_groups=mesh['x_lo'=2,'y'=4,'z_hi'=8,'z_lo'=2,'x_hi'=2,'core'=2] {'x_lo','y','z_..., dimensions={0} | all-to-all | bytes 1048576 | tf_op jit(solution)/shard_map/all_to_all | solution.py:223
  58.3 0.1 near_sum.1
  58.4 21.0 %all_to_all.22.in_ref = bf16[8,32,128]{2,1,0:T(8,128)(2,1)S(1)} all-to-all(bf16[8,32,128]{2,1,0:T(8,128)(2,1)S(1)} %near_sum.1), channel_id=1, replica_groups=mesh['x_lo'=2,'y'=4,'z_hi'=8,'z_lo'=2,'x_hi'=2,'core'=2] {'z_hi'}, dimensions={0} | all-to-all | bytes 131072 | tf_op jit(solution)/shard_map/all_to_all | solution.py:224
  79.4 18.6 %all_to_all.23.g_ref = bf16[64,32,128]{2,1,0:T(8,128)(2,1)S(1)} all-to-all(bf16[64,32,128]{2,1,0:T(8,128)(2,1)S(1)} %far_sum.1), channel_id=1, replica_groups=mesh['x_lo'=2,'y'=4,'z_hi'=8,'z_lo'=2,'x_hi'=2,'core'=2] {'x_lo','y','z_..., dimensions={0} | all-to-all | bytes 1048576 | tf_op jit(solution)/shard_map/all_to_all | solution.py:225
  98.0 1.7 %rotate.1 = (f32[128,512]{1,0:T(8,128)}, bf16[384,512]{1,0:T(8,128)(2,1)}) custom-call(s32[3]{0:T(128)S(1)} %pad_add_fusion.place_ref, bf16[4,384,128]{2,1,0:T(8,128)(2,1)S(1)} %all_to_all.20.f_ref, bf16[64,32,128]{2,1,0:T(8,128)(2,1)S(1)} %all_to_all.23.g_ref), custom_call_target="tpu_custom_call" | custom-call | tf_op jit(solution)/shard_map/rotate/pallas_call | solution.py:226
  (2 shorter events, 0.1 us)
Async XLA Ops:
  1.5 1.0 %copy-start = (bf16[4,4,6,16,128]{4,3,2,1,0:T(8,128)(2,1)S(1)}, bf16[4,4,6,16,128]{4,3,2,1,0:T(8,128)(2,1)}, u32[]{:S(2)}) copy-start(bf16[4,4,6,16,128]{4,3,2,1,0:T(8,128)(2,1)} %param.4) | copy-start | bytes 1179652
  2.5 12.3 %copy-start.1 = (bf16[4,4,6,16,128]{4,3,2,1,0:T(8,128)(2,1)S(1)}, bf16[4,4,6,16,128]{4,3,2,1,0:T(8,128)(2,1)}, u32[]{:S(2)}) copy-start(bf16[4,4,6,16,128]{4,3,2,1,0:T(8,128)(2,1)} %param.4) | copy-start | bytes 1179652
  2.6 8.2 %collective-permute-start = (bf16[1168,128]{1,0:T(8,128)(2,1)S(1)}, bf16[1168,128]{1,0:T(8,128)(2,1)S(1)}, u32[]{:S(2)}, u32[]{:S(2)}) collective-permute-start(bf16[1168,128]{1,0:T(8,128)(2,1)S(1)} %get-tuple-element.4), channel_id=1, source_target_pairs={{0,4},{4,8},{8,12},{12,16},{16,20},{20,24},{24,28},{28,32},{32,36}... | collective-permute-start | bytes 897032 | tf_op jit(solution)/shard_map/ppermute | solution.py:191
  7.1 7.7 %collective-permute-start.1 = (bf16[1168,128]{1,0:T(8,128)(2,1)S(1)}, bf16[1168,128]{1,0:T(8,128)(2,1)S(1)}, u32[]{:S(2)}, u32[]{:S(2)}) collective-permute-start(bf16[1168,128]{1,0:T(8,128)(2,1)S(1)} %get-tuple-element.5), channel_id=1, source_target_pairs={{4,0},{8,4},{12,8},{16,12},{20,16},{24,20},{28,24},{32,28},{36,32}... | collective-permute-start | bytes 897032 | tf_op jit(solution)/shard_map/ppermute | solution.py:192
  8.4 6.4 %copy-start.3 = (f32[4,4]{1,0:T(4,128)S(1)}, f32[4,4]{1,0:T(4,128)}, u32[]{:S(2)}) copy-start(f32[4,4]{1,0:T(4,128)} %coup_ref.1) | copy-start | bytes 196
  18.2 16.0 %copy-start.2 = (bf16[384,512]{1,0:T(8,128)(2,1)S(1)}, bf16[384,512]{1,0:T(8,128)(2,1)}, u32[]{:S(2)}) copy-start(bf16[384,512]{1,0:T(8,128)(2,1)} %dual_ref.1) | copy-start | bytes 1179652

commit v2 on v1

--- a/solution.py
+++ b/solution.py
@@ -8,9 +8,11 @@
 from jax.sharding import Mesh
 from jax.sharding import PartitionSpec as P
 
+
 NODES = ("x_lo", "y", "z_hi", "z_lo")
 COLS = ("x_hi", "core")
-NEAR = ("x_lo", "y", "z_lo", "x_hi", "core")
+NEAR = ("x_lo", "y", "z_lo")
+HALVES = "x_hi"
 FAR = "z_hi"
 REACH = 3
 TILE_ROWS = 16
@@ -129,17 +131,24 @@
     return jnp.concatenate(parts, axis=1)
 
 
-def gram_kernel(dual_ref, f_ref, out_ref):
-    blocks = f_ref.shape[0]
+def gram_kernel(
+    place_ref, own_ref, core_ref, half_ref, both_ref, f_ref, out_ref, to_core, to_half, to_both
+):
     pieces, height, _ = out_ref.shape
-    each = pieces // blocks
-    dual = dual_ref[...]
-    for b in range(0, blocks, 2):
-        pair = side_by_side([f_ref[b], f_ref[b + 1]])
-        part = lax.dot_general(dual, pair, (((0,), (0,)), ((), ())), preferred_element_type=f32)
-        for k in range(2):
-            cut = part[:, k * LANES : (k + 1) * LANES].astype(bf16)
-            out_ref[(b + k) * each : (b + k + 1) * each] = cut.reshape(each, height, LANES)
+    here, core = place_ref[2], place_ref[3]
+    layers = [2 * a + b for a, b in spots(here, core)]
+    part = 0.0
+    for at, dual in zip(layers, (own_ref, core_ref, half_ref, both_ref)):
+        part = part + lax.dot_general(
+            f_ref[at], dual[...], (((0,), (0,)), ((), ())), preferred_element_type=f32
+        )
+    out_ref[...] = part.T.astype(bf16).reshape(pieces, height, LANES)
+    for at, send in zip(layers[1:], (to_core, to_half, to_both)):
+        send[...] = f_ref[at]
+
+
+def spots(here, core):
+    return (here, core), (here, 1 - core), (1 - here, core), (1 - here, 1 - core)
 
 
 def sum_kernel(in_ref, out_ref):
@@ -152,22 +161,26 @@
         out_ref[k] = piece
 
 
-def rotate_kernel(scale, place_ref, f_ref, g_ref, gram_ref, out_ref):
-    blocks, rows, _ = f_ref.shape
+def rotate_kernel(scale, place_ref, f_ref, core_ref, half_ref, both_ref, g_ref, gram_ref, out_ref):
+    blocks = out_ref.shape[1] // LANES
     pieces, height, _ = g_ref.shape
     each = pieces // blocks
     own = each // blocks
-    cols = side_by_side([f_ref[b] for b in range(blocks)])
-    first = place_ref[2] * own
+    here, core = place_ref[2], place_ref[3]
+    places = [2 * a + b for a, b in spots(here, core)]
+    cols = side_by_side([f_ref[places[0]], core_ref[...], half_ref[...], both_ref[...]])
+
+    def rows_of(k, at):
+        return g_ref[pl.ds(k * each + at * own, own)].reshape(own * height, LANES)
+
     for b in range(0, blocks, 2):
-        pair = side_by_side(
-            [g_ref[k * each : (k + 1) * each].reshape(each * height, LANES) for k in (b, b + 1)]
+        turn = side_by_side(
+            [jnp.concatenate([rows_of(k, at) for at in places], axis=0) for k in (b, b + 1)]
         )
-        turned = jnp.dot(cols, pair, preferred_element_type=f32) * scale
+        turned = jnp.dot(cols, turn, preferred_element_type=f32) * scale
         out_ref[:, b * LANES : (b + 2) * LANES] = turned.astype(bf16)
         for k in (b, b + 1):
-            mine = g_ref[pl.ds(k * each + first, own)].reshape(own * height, LANES)
-            gram_ref[:, k * LANES : (k + 1) * LANES] = mine.astype(f32)
+            gram_ref[:, k * LANES : (k + 1) * LANES] = rows_of(k, places[0]).astype(f32)
 
 
 def shards(vectors, node_shift, coupling, dual_basis):
@@ -178,11 +191,21 @@
     far = lax.axis_size(FAR)
     blocks = lax.axis_size(COLS)
     cols = blocks * width
-    height = cols * blocks // near
+    height = cols // near
     v = vectors.reshape(layers, rows, width)
     shift_tile = jnp.pad(
         node_shift.transpose(2, 0, 1).reshape(gz, layers * gy), ((0, 0), (0, LANES - layers * gy))
     )
+
+    def swap(array, axes):
+        many = lax.axis_size(axes)
+        return lax.ppermute(array, axes, [(i, many - 1 - i) for i in range(many)])
+
+    def spread(array, axes):
+        return lax.all_to_all(array, axes, split_axis=0, concat_axis=0, tiled=True)
+
+    dual_half = swap(dual_basis, HALVES)
+    dual_core = swap(dual_basis, "core")
     message = jax.ShapeDtypeStruct((REACH * rows + gz, width), bf16)
     up, down = pl.pallas_call(
         pack_kernel, out_shape=(message, message), in_specs=vmem(2), out_specs=tuple(vmem(2)),
@@ -190,8 +213,11 @@
     )(v, shift_tile)
     low = lax.ppermute(up, NODES, [(i, i + 1) for i in range(count - 1)])
     high = lax.ppermute(down, NODES, [(i + 1, i) for i in range(count - 1)])
+    dual_both = swap(dual_half, "core")
     node = lax.axis_index(NODES)
-    place = jnp.stack([node > 0, node < count - 1, lax.axis_index(COLS)]).astype(jnp.int32)
+    place = jnp.stack(
+        [node > 0, node < count - 1, lax.axis_index(HALVES), lax.axis_index("core")]
+    ).astype(jnp.int32)
     tiles = dofs * gy
     own = pl.pallas_call(
         functools.partial(filter_kernel, gy, dofs),
@@ -206,31 +232,35 @@
         ],
         compiler_params=room(16), name="filter",
     )(coupling, place, v, low, high, shift_tile)
-    mine = lax.all_to_all(own, COLS, split_axis=0, concat_axis=0, tiled=True)
-    terms = pl.pallas_call(
+    layer = jax.ShapeDtypeStruct((rows, width), bf16)
+    terms, to_core, to_half, to_both = pl.pallas_call(
         gram_kernel,
-        out_shape=jax.ShapeDtypeStruct((near, height, LANES), bf16),
-        in_specs=vmem(2), out_specs=vmem(1)[0], compiler_params=room(8), name="gram",
-    )(dual_basis, mine)
-
-    def summed(pieces, copies, name):
+        out_shape=(jax.ShapeDtypeStruct((near, height, LANES), bf16), layer, layer, layer),
+        in_specs=smem(1) + vmem(5), out_specs=tuple(vmem(4)), compiler_params=room(12), name="gram",
+    )(place, dual_basis, dual_core, dual_half, dual_both, own)
+    from_core = swap(to_core, "core")
+    from_half = swap(to_half, HALVES)
+    from_both = swap(to_both, COLS)
+
+    def summed(pieces, copies):
         return pl.pallas_call(
             sum_kernel,
             out_shape=jax.ShapeDtypeStruct((copies, height, LANES), bf16),
-            in_specs=vmem(1), out_specs=vmem(1)[0], compiler_params=room(8), name=name,
+            in_specs=vmem(1), out_specs=vmem(1)[0], compiler_params=room(8),
         )(pieces)
 
-    pieces = lax.all_to_all(terms, NEAR, split_axis=0, concat_axis=0, tiled=True)
-    pieces = lax.all_to_all(summed(pieces, far, "near_sum"), FAR, split_axis=0, concat_axis=0, tiled=True)
-    pieces = lax.all_to_all(summed(pieces, near, "far_sum"), NEAR, split_axis=0, concat_axis=0, tiled=True)
+    pieces = spread(terms, NEAR)
+    part = summed(pieces, far)
+    pieces = spread(part, FAR)
+    pieces = spread(summed(pieces, near * blocks), COLS + NEAR)
     gram, rotated = pl.pallas_call(
         functools.partial(rotate_kernel, cols ** (-0.5)),
         out_shape=(
             jax.ShapeDtypeStruct((cols // blocks, cols), f32),
             jax.ShapeDtypeStruct((rows, cols), bf16),
         ),
-        in_specs=smem(1) + vmem(2), out_specs=tuple(vmem(2)), compiler_params=room(12), name="rotate",
-    )(place, mine, pieces)
+        in_specs=smem(1) + vmem(5), out_specs=tuple(vmem(2)), compiler_params=room(12), name="rotate",
+    )(place, own, from_core, from_half, from_both, pieces)
     return gram, rotated
 
 

time: 100 us -> 105 us (1.050)
  blocking collectives: 79.2 us -> 37.5 us
  starting transfers between devices: 5.8 us -> 41.7 us
  waiting for transfers between devices: 6.27 us -> 15.9 us
  Pallas kernels: 5.72 us -> 7.05 us
    all_to_all x4 -> x2, blocking collectives: 79.2 us -> 37.5 us  [spread(): return lax.all_to_all(array, axes, split_axis=0, concat_axis=0, tiled=True)]
    ppermute x0 -> x6, starting transfers between devices: none -> 28.9 us  [swap(): return lax.ppermute(array, axes, [(i, many - 1 - i) for i in range(many)])]
    all_to_all x0 -> x1, starting transfers between devices: none -> 10 us  [spread(): return lax.all_to_all(array, axes, split_axis=0, concat_axis=0, tiled=True)]
    ppermute x0 -> x6, waiting for transfers between devices: none -> 6.74 us  [swap(): return lax.ppermute(array, axes, [(i, many - 1 - i) for i in range(many)])]
    ppermute x1, starting transfers between devices: 4.51 us -> 1.44 us  [shards(): low = lax.ppermute(up, NODES, [(i, i + 1) for i in range(count - 1)])]
    ppermute x1, waiting for transfers between devices: 2.27 us -> 5.01 us  [shards(): low = lax.ppermute(up, NODES, [(i, i + 1) for i in range(count - 1)])]
  transfers between devices with their start and end apart: 2 -> 9, of which waited for: 2 -> 5; matrix products, arithmetic and copies ran while one was open for 0% -> 1% of each run, Pallas kernels for 0% -> 3%
where the time goes in v2:
time: 105 us
  starting transfers between devices  41.7 us (40%)
  blocking collectives  37.5 us (36%)
  waiting for transfers between devices  15.9 us (15%)
  Pallas kernels  7.05 us (7%)
  local copies, waits for them, and re-layouts  1.91 us (2%)
    all_to_all x2, blocking collectives, spread(): return lax.all_to_all(array, axes, split_axis=0, concat_axis=0, tiled=True)  37.5 us
    ppermute x6, starting transfers between devices, swap(): return lax.ppermute(array, axes, [(i, many - 1 - i) for i in range(many)])  28.9 us
    all_to_all x1, starting transfers between devices, spread(): return lax.all_to_all(array, axes, split_axis=0, concat_axis=0, tiled=True)  10 us
    ppermute x6, waiting for transfers between devices, swap(): return lax.ppermute(array, axes, [(i, many - 1 - i) for i in range(many)])  6.74 us
    ppermute x1, waiting for transfers between devices, shards(): low = lax.ppermute(up, NODES, [(i, i + 1) for i in range(count - 1)])  5.01 us
    ppermute x1, waiting for transfers between devices, shards(): high = lax.ppermute(down, NODES, [(i + 1, i) for i in range(count - 1)])  4.16 us
    pallas_call x1, Pallas kernels, shards(): pl.pallas_call(functools.partial(filter_kernel, gy, dofs), out_shape=jax....  3.34 us
  transfers between devices with their start and end apart: 9, of which 5 were waited for; matrix products, arithmetic and copies ran while one was open for 1% of the time, Pallas kernels for 3%

profile of v2, /device:TPU:1, one launch (start us, length us, event | category | flops | bytes accessed | tf_op | source)
XLA Modules:
  0.0 104.9 jit_solution(8842614043130262808)
XLA Ops:
  0.6 5.5 %collective-permute-start.3 = (bf16[384,512]{1,0:T(8,128)(2,1)}, bf16[384,512]{1,0:T(8,128)(2,1)S(1)}, u32[]{:S(2)}, u32[]{:S(2)}) collective-permute-start(bf16[384,512]{1,0:T(8,128)(2,1)} %own_ref.1), channel_id=1, source_target_pairs={{0,2},{2,0},{1,3},{3,1},{4,6},{6,4},{5,7},{7,5},{8,10},{10,8},{9,1... | collective-permute-start | bytes 1179656 | tf_op jit(solution)/shard_map/ppermute | solution.py:202
  6.1 5.2 %collective-permute-start.2 = (bf16[384,512]{1,0:T(8,128)(2,1)}, bf16[384,512]{1,0:T(8,128)(2,1)S(1)}, u32[]{:S(2)}, u32[]{:S(2)}) collective-permute-start(bf16[384,512]{1,0:T(8,128)(2,1)} %own_ref.1), channel_id=1, source_target_pairs={{0,1},{1,0},{2,3},{3,2},{4,5},{5,4},{6,7},{7,6},{8,9},{9,8},{10,11... | collective-permute-start | bytes 1179656 | tf_op jit(solution)/shard_map/ppermute | solution.py:202
  11.3 0.5 collective-permute-done.3.half_ref
  11.9 8.9 %collective-permute-start.4 = (bf16[384,512]{1,0:T(8,128)(2,1)S(1)}, bf16[384,512]{1,0:T(8,128)(2,1)S(1)}, u32[]{:S(2)}, u32[]{:S(2)}) collective-permute-start(bf16[384,512]{1,0:T(8,128)(2,1)S(1)} %collective-permute-done.3.half_ref), channel_id=1, source_target_pairs={{0,1},{1,0},{2,3},{3,2},{4,5},{5,4},{6,7},{7,6},{8,9},{9,8},{10,11... | collective-permute-start | bytes 1179656 | tf_op jit(solution)/shard_map/ppermute | solution.py:202
  20.8 0.8 copy.9
  21.6 0.1 reshape.14
  21.7 1.0 copy-done
  22.7 0.1 pack.1
  22.7 1.4 %collective-permute-start = (bf16[1168,128]{1,0:T(8,128)(2,1)S(1)}, bf16[1168,128]{1,0:T(8,128)(2,1)S(1)}, u32[]{:S(2)}, u32[]{:S(2)}) collective-permute-start(bf16[1168,128]{1,0:T(8,128)(2,1)S(1)} %get-tuple-element.8), channel_id=1, source_target_pairs={{0,4},{4,8},{8,12},{12,16},{16,20},{20,24},{24,28},{28,32},{32,36}... | collective-permute-start | bytes 897032 | tf_op jit(solution)/shard_map/ppermute | solution.py:214
  24.2 1.3 %collective-permute-start.1 = (bf16[1168,128]{1,0:T(8,128)(2,1)S(1)}, bf16[1168,128]{1,0:T(8,128)(2,1)S(1)}, u32[]{:S(2)}, u32[]{:S(2)}) collective-permute-start(bf16[1168,128]{1,0:T(8,128)(2,1)S(1)} %get-tuple-element.9), channel_id=1, source_target_pairs={{4,0},{8,4},{12,8},{16,12},{20,16},{24,20},{28,24},{32,28},{36,32}... | collective-permute-start | bytes 897032 | tf_op jit(solution)/shard_map/ppermute | solution.py:215
  25.5 0.0 copy-start.3
  25.5 0.1 pad_add_fusion.place_ref
  25.6 5.0 %collective-permute-done.low_ref = bf16[1168,128]{1,0:T(8,128)(2,1)S(1)} collective-permute-done((bf16[1168,128]{1,0:T(8,128)(2,1)S(1)}, bf16[1168,128]{1,0:T(8,128)(2,1)S(1)}, u32[]{:S(2)}, u32[]{:S(2)}) %collective-permute-start) | collective-permute-done | bytes 299040 | tf_op jit(solution)/shard_map/ppermute | solution.py:214
  30.6 4.2 %collective-permute-done.1.high_ref = bf16[1168,128]{1,0:T(8,128)(2,1)S(1)} collective-permute-done((bf16[1168,128]{1,0:T(8,128)(2,1)S(1)}, bf16[1168,128]{1,0:T(8,128)(2,1)S(1)}, u32[]{:S(2)}, u32[]{:S(2)}) %collective-permute-start.1) | collective-permute-done | bytes 299040 | tf_op jit(solution)/shard_map/ppermute | solution.py:215
  34.8 0.0 copy-done.1
  34.8 0.0 copy-done.3
  34.8 3.3 %filter.1.f_ref = bf16[4,384,128]{2,1,0:T(8,128)(2,1)S(1)} custom-call(f32[4,4]{1,0:T(4,128)S(1)} %copy-done.3, s32[4]{0:T(128)S(1)} %pad_add_fusion.place_ref, bf16[4,384,128]{2,1,0:T(8,128)(2,1)S(1)} %bitcast.7, bf16[1168,128]{1,0:T(8,128)(2,1)S(1)} %collective-permute-done.low_ref, bf16[1168,128]{1,0:T(8,128)(2,1)S(1)} %collective-permute-done.1.high_ref, ...), custom_call_target="tpu_custom_call" | custom-call | tf_op jit(solution)/shard_map/filter/pallas_call | solution.py:222
  38.1 0.0 collective-permute-done.2.core_ref
  38.1 0.0 collective-permute-done.4.both_ref
  38.2 1.1 %gram.1 = (bf16[16,32,128]{2,1,0:T(8,128)(2,1)S(1)}, bf16[384,128]{1,0:T(8,128)(2,1)S(1)}, bf16[384,128]{1,0:T(8,128)(2,1)S(1)}, bf16[384,128]{1,0:T(8,128)(2,1)S(1)}) custom-call(s32[4]{0:T(128)S(1)} %pad_add_fusion.place_ref, bf16[384,512]{1,0:T(8,128)(2,1)S(1)} %copy-done.2, bf16[384,512]{1,0:T(8,128)(2,1)S(1)} %collective-permute-done.2.core_ref, ...), custom_call_target="tpu_custom_call" | custom-call | tf_op jit(solution)/shard_map/gram/pallas_call | solution.py:236
  39.2 16.3 %all_to_all.15.in_ref = bf16[16,32,128]{2,1,0:T(8,128)(2,1)S(1)} all-to-all(bf16[16,32,128]{2,1,0:T(8,128)(2,1)S(1)} %get-tuple-element.13), channel_id=1, replica_groups=mesh['x_lo'=2,'y'=4,'z_hi'=8,'z_lo'=2,'x_hi'=2,'core'=2] {'x_lo','y','z_..., dimensions={0} | all-to-all | bytes 262144 | tf_op jit(solution)/shard_map/all_to_all | solution.py:205
  55.6 21.1 %all_to_all.16.in_ref = bf16[8,32,128]{2,1,0:T(8,128)(2,1)S(1)} all-to-all(bf16[8,32,128]{2,1,0:T(8,128)(2,1)S(1)} %shard_map.59), channel_id=1, replica_groups=mesh['x_lo'=2,'y'=4,'z_hi'=8,'z_lo'=2,'x_hi'=2,'core'=2] {'z_hi'}, dimensions={0} | all-to-all | bytes 131072 | tf_op jit(solution)/shard_map/all_to_all | solution.py:205
  76.7 0.8 shard_map.60
  77.6 10.0 %all-to-all-start.2 = ((bf16[64,32,128]{2,1,0:T(8,128)(2,1)}), bf16[64,32,128]{2,1,0:T(8,128)(2,1)S(1)}, u32[]{:S(2)}, u32[]{:S(2)}) async-start(bf16[64,32,128]{2,1,0:T(8,128)(2,1)} %shard_map.60), calls=%async_computation.2 | async-start | bytes 1048576 | tf_op jit(solution)/shard_map/all_to_all | solution.py:205
  87.6 2.4 %collective-permute-start.5 = (bf16[384,128]{1,0:T(8,128)(2,1)S(1)}, bf16[384,128]{1,0:T(8,128)(2,1)S(1)}, u32[]{:S(2)}, u32[]{:S(2)}) collective-permute-start(bf16[384,128]{1,0:T(8,128)(2,1)S(1)} %get-tuple-element.10), channel_id=1, source_target_pairs={{0,1},{1,0},{2,3},{3,2},{4,5},{5,4},{6,7},{7,6},{8,9},{9,8},{10,11... | collective-permute-start | bytes 294920 | tf_op jit(solution)/shard_map/ppermute | solution.py:202
  90.0 4.8 %collective-permute-start.6 = (bf16[384,128]{1,0:T(8,128)(2,1)S(1)}, bf16[384,128]{1,0:T(8,128)(2,1)S(1)}, u32[]{:S(2)}, u32[]{:S(2)}) collective-permute-start(bf16[384,128]{1,0:T(8,128)(2,1)S(1)} %get-tuple-element.11), channel_id=1, source_target_pairs={{0,2},{2,0},{1,3},{3,1},{4,6},{6,4},{5,7},{7,5},{8,10},{10,8},{9,1... | collective-permute-start | bytes 294920 | tf_op jit(solution)/shard_map/ppermute | solution.py:202
  94.8 2.2 %collective-permute-start.7 = (bf16[384,128]{1,0:T(8,128)(2,1)S(1)}, bf16[384,128]{1,0:T(8,128)(2,1)S(1)}, u32[]{:S(2)}, u32[]{:S(2)}) collective-permute-start(bf16[384,128]{1,0:T(8,128)(2,1)S(1)} %get-tuple-element.12), channel_id=1, source_target_pairs={{0,3},{1,2},{2,1},{3,0},{4,7},{5,6},{6,5},{7,4},{8,11},{9,10},{10,... | collective-permute-start | bytes 294920 | tf_op jit(solution)/shard_map/ppermute | solution.py:202
  97.0 0.0 collective-permute-done.5.core_ref
  97.0 2.0 %collective-permute-done.6.half_ref = bf16[384,128]{1,0:T(8,128)(2,1)S(1)} collective-permute-done((bf16[384,128]{1,0:T(8,128)(2,1)S(1)}, bf16[384,128]{1,0:T(8,128)(2,1)S(1)}, u32[]{:S(2)}, u32[]{:S(2)}) %collective-permute-start.6) | collective-permute-done | bytes 98336 | tf_op jit(solution)/shard_map/ppermute | solution.py:202
  99.0 4.2 %collective-permute-done.7.both_ref = bf16[384,128]{1,0:T(8,128)(2,1)S(1)} collective-permute-done((bf16[384,128]{1,0:T(8,128)(2,1)S(1)}, bf16[384,128]{1,0:T(8,128)(2,1)S(1)}, u32[]{:S(2)}, u32[]{:S(2)}) %collective-permute-start.7) | collective-permute-done | bytes 98336 | tf_op jit(solution)/shard_map/ppermute | solution.py:202
  103.2 0.0 all-to-all-done.2.g_ref
  103.2 1.7 %rotate.1 = (f32[128,512]{1,0:T(8,128)}, bf16[384,512]{1,0:T(8,128)(2,1)}) custom-call(s32[4]{0:T(128)S(1)} %pad_add_fusion.place_ref, bf16[4,384,128]{2,1,0:T(8,128)(2,1)S(1)} %filter.1.f_ref, bf16[384,128]{1,0:T(8,128)(2,1)S(1)} %collective-permute-done.5.core_ref, bf16[384,128]{1,0:T(8,128)(2,1)S(1)} %collective-permute-done.6.half_ref, ...), custom_call_target="tpu_custom_call" | custom-call | tf_op jit(solution)/shard_map/rotate/pallas_call | solution.py:256
  (6 shorter events, 0.0 us)
Async XLA Ops:
  0.6 11.2 %collective-permute-start.3 = (bf16[384,512]{1,0:T(8,128)(2,1)}, bf16[384,512]{1,0:T(8,128)(2,1)S(1)}, u32[]{:S(2)}, u32[]{:S(2)}) collective-permute-start(bf16[384,512]{1,0:T(8,128)(2,1)} %own_ref.1), channel_id=1, source_target_pairs={{0,2},{2,0},{1,3},{3,1},{4,6},{6,4},{5,7},{7,5},{8,10},{10,8},{9,1... | collective-permute-start | bytes 1179656 | tf_op jit(solution)/shard_map/ppermute | solution.py:202
  6.1 32.0 %collective-permute-start.2 = (bf16[384,512]{1,0:T(8,128)(2,1)}, bf16[384,512]{1,0:T(8,128)(2,1)S(1)}, u32[]{:S(2)}, u32[]{:S(2)}) collective-permute-start(bf16[384,512]{1,0:T(8,128)(2,1)} %own_ref.1), channel_id=1, source_target_pairs={{0,1},{1,0},{2,3},{3,2},{4,5},{5,4},{6,7},{7,6},{8,9},{9,8},{10,11... | collective-permute-start | bytes 1179656 | tf_op jit(solution)/shard_map/ppermute | solution.py:202
  11.9 26.3 %collective-permute-start.4 = (bf16[384,512]{1,0:T(8,128)(2,1)S(1)}, bf16[384,512]{1,0:T(8,128)(2,1)S(1)}, u32[]{:S(2)}, u32[]{:S(2)}) collective-permute-start(bf16[384,512]{1,0:T(8,128)(2,1)S(1)} %collective-permute-done.3.half_ref), channel_id=1, source_target_pairs={{0,1},{1,0},{2,3},{3,2},{4,5},{5,4},{6,7},{7,6},{8,9},{9,8},{10,11... | collective-permute-start | bytes 1179656 | tf_op jit(solution)/shard_map/ppermute | solution.py:202
  21.7 1.0 copy-start
  22.7 12.1 %copy-start.1 = (bf16[4,4,6,16,128]{4,3,2,1,0:T(8,128)(2,1)S(1)}, bf16[4,4,6,16,128]{4,3,2,1,0:T(8,128)(2,1)}, u32[]{:S(2)}) copy-start(bf16[4,4,6,16,128]{4,3,2,1,0:T(8,128)(2,1)} %param.4) | copy-start | bytes 1179652
  22.7 7.9 %collective-permute-start = (bf16[1168,128]{1,0:T(8,128)(2,1)S(1)}, bf16[1168,128]{1,0:T(8,128)(2,1)S(1)}, u32[]{:S(2)}, u32[]{:S(2)}) collective-permute-start(bf16[1168,128]{1,0:T(8,128)(2,1)S(1)} %get-tuple-element.8), channel_id=1, source_target_pairs={{0,4},{4,8},{8,12},{12,16},{16,20},{20,24},{24,28},{28,32},{32,36}... | collective-permute-start | bytes 897032 | tf_op jit(solution)/shard_map/ppermute | solution.py:214
  24.2 10.6 %collective-permute-start.1 = (bf16[1168,128]{1,0:T(8,128)(2,1)S(1)}, bf16[1168,128]{1,0:T(8,128)(2,1)S(1)}, u32[]{:S(2)}, u32[]{:S(2)}) collective-permute-start(bf16[1168,128]{1,0:T(8,128)(2,1)S(1)} %get-tuple-element.9), channel_id=1, source_target_pairs={{4,0},{8,4},{12,8},{16,12},{20,16},{24,20},{28,24},{32,28},{36,32}... | collective-permute-start | bytes 897032 | tf_op jit(solution)/shard_map/ppermute | solution.py:215
  25.5 9.3 %copy-start.3 = (f32[4,4]{1,0:T(4,128)S(1)}, f32[4,4]{1,0:T(4,128)}, u32[]{:S(2)}) copy-start(f32[4,4]{1,0:T(4,128)} %coup_ref.1) | copy-start | bytes 196
  25.6 12.6 %copy-start.2 = (bf16[384,512]{1,0:T(8,128)(2,1)S(1)}, bf16[384,512]{1,0:T(8,128)(2,1)}, u32[]{:S(2)}) copy-start(bf16[384,512]{1,0:T(8,128)(2,1)} %own_ref.1) | copy-start | bytes 1179652
  77.6 25.6 %all-to-all-start.2 = ((bf16[64,32,128]{2,1,0:T(8,128)(2,1)}), bf16[64,32,128]{2,1,0:T(8,128)(2,1)S(1)}, u32[]{:S(2)}, u32[]{:S(2)}) async-start(bf16[64,32,128]{2,1,0:T(8,128)(2,1)} %shard_map.60), calls=%async_computation.2 | async-start | bytes 1048576 | tf_op jit(solution)/shard_map/all_to_all | solution.py:205
  87.6 9.4 %collective-permute-start.5 = (bf16[384,128]{1,0:T(8,128)(2,1)S(1)}, bf16[384,128]{1,0:T(8,128)(2,1)S(1)}, u32[]{:S(2)}, u32[]{:S(2)}) collective-permute-start(bf16[384,128]{1,0:T(8,128)(2,1)S(1)} %get-tuple-element.10), channel_id=1, source_target_pairs={{0,1},{1,0},{2,3},{3,2},{4,5},{5,4},{6,7},{7,6},{8,9},{9,8},{10,11... | collective-permute-start | bytes 294920 | tf_op jit(solution)/shard_map/ppermute | solution.py:202
  90.0 9.0 %collective-permute-start.6 = (bf16[384,128]{1,0:T(8,128)(2,1)S(1)}, bf16[384,128]{1,0:T(8,128)(2,1)S(1)}, u32[]{:S(2)}, u32[]{:S(2)}) collective-permute-start(bf16[384,128]{1,0:T(8,128)(2,1)S(1)} %get-tuple-element.11), channel_id=1, source_target_pairs={{0,2},{2,0},{1,3},{3,1},{4,6},{6,4},{5,7},{7,5},{8,10},{10,8},{9,1... | collective-permute-start | bytes 294920 | tf_op jit(solution)/shard_map/ppermute | solution.py:202
  94.8 8.4 %collective-permute-start.7 = (bf16[384,128]{1,0:T(8,128)(2,1)S(1)}, bf16[384,128]{1,0:T(8,128)(2,1)S(1)}, u32[]{:S(2)}, u32[]{:S(2)}) collective-permute-start(bf16[384,128]{1,0:T(8,128)(2,1)S(1)} %get-tuple-element.12), channel_id=1, source_target_pairs={{0,3},{1,2},{2,1},{3,0},{4,7},{5,6},{6,5},{7,4},{8,11},{9,10},{10,... | collective-permute-start | bytes 294920 | tf_op jit(solution)/shard_map/ppermute | solution.py:202

commit v3 on v2

--- a/solution.py
+++ b/solution.py
@@ -17,6 +17,7 @@
 REACH = 3
 TILE_ROWS = 16
 LANES = 128
+SHIFT_ROWS = 32
 
 bf16 = jnp.bfloat16
 f32 = jnp.float32
@@ -34,13 +35,25 @@
     return pltpu.CompilerParams(vmem_limit_bytes=mebibytes << 20)
 
 
-def pack_kernel(v_ref, shift_ref, up_ref, down_ref):
-    layers, rows = v_ref.shape[0], v_ref.shape[1]
-    for k in range(REACH):
-        up_ref[k * rows : (k + 1) * rows, :] = v_ref[layers - REACH + k]
-        down_ref[k * rows : (k + 1) * rows, :] = v_ref[k]
-    up_ref[REACH * rows :, :] = shift_ref[...]
-    down_ref[REACH * rows :, :] = shift_ref[...]
+def pack_kernel(rows, v_ref, shift_ref, up_ref, down_ref, tile_ref, spread, sems):
+    span = REACH * rows
+    total = v_ref.shape[0]
+    copies = [
+        pltpu.make_async_copy(v_ref.at[total - span : total], up_ref.at[0:span], sems.at[0]),
+        pltpu.make_async_copy(v_ref.at[0:span], down_ref.at[0:span], sems.at[1]),
+    ]
+    for copy in copies:
+        copy.start()
+    gy, layers, gz = shift_ref.shape
+    spread[...] = jnp.zeros_like(spread)
+    for y in range(gy):
+        spread[y * layers : (y + 1) * layers, 0:gz] = shift_ref[y].astype(f32)
+    tile = spread[...].astype(bf16)
+    tile_ref[...] = tile
+    up_ref[span:, :] = tile
+    down_ref[span:, :] = tile
+    for copy in copies:
+        copy.wait()
 
 
 def filter_kernel(
@@ -48,22 +61,25 @@
 ):
     layers = v_ref.shape[0]
     gz = TILE_ROWS
+    half = gz // 2
     rows = dofs * gy * gz
     tiles = dofs * gy
-    low_in = place_ref[0].astype(f32)
-    high_in = place_ref[1].astype(f32)
-
-    def shift_cols(ref, first, layer, slot):
-        tile = ref[first : first + gz, :].astype(f32)
+    span = REACH * rows
+
+    stiff = jnp.concatenate(
+        [low_ref[span:, :], shift_ref[...], high_ref[span:, :]]
+        + [jnp.zeros((LANES - 3 * SHIFT_ROWS, LANES), bf16)],
+        axis=0,
+    )
+    stiff = stiff.astype(f32).T
+    firsts = [layers - 2 + k for k in range(2)]
+    firsts += [SHIFT_ROWS + k for k in range(layers)]
+    firsts += [2 * SHIFT_ROWS + k for k in range(2)]
+    for slot, first in enumerate(firsts):
         for y in range(gy):
-            k = layer * gy + y
-            diag[slot, y] = jnp.broadcast_to(tile[:, k : k + 1], (gz, LANES)) - 4.0
-
-    for k in range(2):
-        shift_cols(low_ref, REACH * rows, layers - 2 + k, k)
-        shift_cols(high_ref, REACH * rows, k, 2 + layers + k)
-    for k in range(layers):
-        shift_cols(shift_ref, 0, k, 2 + k)
+            lane = first + y * layers
+            column = stiff[0:gz, lane : lane + 1]
+            diag[slot, y] = jnp.broadcast_to(column, (gz, LANES)) - 4.0
 
     for t in range(tiles):
         for k in range(REACH):
@@ -73,56 +89,72 @@
         for k in range(layers):
             s0[REACH + k, t] = v_ref[k, t * gz : (t + 1) * gz, :].astype(f32)
 
-    row = lax.broadcasted_iota(jnp.int32, (gz, LANES), 0)
-    top, bottom = row == 0, row == gz - 1
+    row = lax.broadcasted_iota(jnp.int32, (half, LANES), 0)
+    top, bottom = row == 0, row == half - 1
     coup = [[coup_ref[d, e] for e in range(dofs)] for d in range(dofs)]
+    halves = (slice(0, half), slice(half, gz))
 
     def apply(src, at, dslot, emit):
         for y in range(gy):
-            mid = [src[at, d * gy + y] for d in range(dofs)]
-            dg = diag[dslot, y]
+            mid = [[src[at, d * gy + y, part] for part in halves] for d in range(dofs)]
+            dg = [diag[dslot, y, part] for part in halves]
             for d in range(dofs):
                 t = d * gy + y
-                near = src[at - 1, t] + src[at + 1, t]
-                if y > 0:
-                    near = near + src[at, t - 1]
-                if y < gy - 1:
-                    near = near + src[at, t + 1]
-                near = near + jnp.where(top, 0.0, pltpu.roll(mid[d], 1, 0))
-                near = near + jnp.where(bottom, 0.0, pltpu.roll(mid[d], gz - 1, 0))
-                total = (dg + coup[d][d]) * mid[d] - near
-                for e in range(dofs):
-                    if e != d:
-                        total = total + coup[d][e] * mid[e]
-                emit(t, total)
-
-    def outside(layer):
-        keep = jnp.where(layer < 0, low_in, jnp.where(layer >= layers, high_in, 1.0))
-        return keep
+                up = [pltpu.roll(mid[d][k], 1, 0) for k in range(2)]
+                down = [pltpu.roll(mid[d][k], half - 1, 0) for k in range(2)]
+                shifted = (
+                    jnp.where(top, 0.0, up[0]) + jnp.where(bottom, down[1], down[0]),
+                    jnp.where(top, up[0], up[1]) + jnp.where(bottom, 0.0, down[1]),
+                )
+                for k, part in enumerate(halves):
+                    near = src[at - 1, t, part] + src[at + 1, t, part]
+                    if y > 0:
+                        near = near + src[at, t - 1, part]
+                    if y < gy - 1:
+                        near = near + src[at, t + 1, part]
+                    near = near + shifted[k]
+                    total = (dg[k] + coup[d][d]) * mid[d][k] - near
+                    for e in range(dofs):
+                        if e != d:
+                            total = total + coup[d][e] * mid[e][k]
+                    emit(t, k, part, total)
+
+    def clear(state, beyond):
+        @pl.when(place_ref[0] == 0)
+        def _():
+            state[0:beyond] = jnp.zeros((beyond, tiles, gz, LANES), f32)
+
+        @pl.when(place_ref[1] == 0)
+        def _():
+            state[layers + beyond :] = jnp.zeros((beyond, tiles, gz, LANES), f32)
 
     @pl.loop(0, layers + 4)
     def _(i):
-        keep = outside(i - 2)
-
-        def emit(t, total):
-            s1[i, t] = total * keep
+        def emit(t, k, part, total):
+            s1[i, t, part] = total
 
         apply(s0, i + 1, i, emit)
+
+    clear(s1, 2)
 
     @pl.loop(0, layers + 2)
     def _(i):
-        keep = outside(i - 1)
-
-        def emit(t, total):
-            s2[i, t] = (total - 24.5 * s0[i + 2, t]) * keep
+        def emit(t, k, part, total):
+            s2[i, t, part] = total - 24.5 * s0[i + 2, t, part]
 
         apply(s1, i + 1, i + 1, emit)
+
+    clear(s2, 1)
 
     @pl.loop(0, layers)
     def _(i):
-        def emit(t, total):
-            last = (total - 12.25 * s1[i + 2, t]) * (4.0 / 343.0)
-            out_ref[i, t * gz : (t + 1) * gz, :] = last.astype(bf16)
+        held = {}
+
+        def emit(t, k, part, total):
+            held[k] = (total - 12.25 * s1[i + 2, t, part]) * (4.0 / 343.0)
+            if k == 1:
+                both = jnp.concatenate([held[0], held[1]], axis=0)
+                out_ref[i, t * gz : (t + 1) * gz, :] = both.astype(bf16)
 
         apply(s2, i + 1, i + 2, emit)
 
@@ -193,9 +225,6 @@
     cols = blocks * width
     height = cols // near
     v = vectors.reshape(layers, rows, width)
-    shift_tile = jnp.pad(
-        node_shift.transpose(2, 0, 1).reshape(gz, layers * gy), ((0, 0), (0, LANES - layers * gy))
-    )
 
     def swap(array, axes):
         many = lax.axis_size(axes)
@@ -206,11 +235,14 @@
 
     dual_half = swap(dual_basis, HALVES)
     dual_core = swap(dual_basis, "core")
-    message = jax.ShapeDtypeStruct((REACH * rows + gz, width), bf16)
-    up, down = pl.pallas_call(
-        pack_kernel, out_shape=(message, message), in_specs=vmem(2), out_specs=tuple(vmem(2)),
+    message = jax.ShapeDtypeStruct((REACH * rows + SHIFT_ROWS, width), bf16)
+    up, down, shift_tile = pl.pallas_call(
+        functools.partial(pack_kernel, rows),
+        out_shape=(message, message, jax.ShapeDtypeStruct((SHIFT_ROWS, width), bf16)),
+        in_specs=[pl.BlockSpec(memory_space=pltpu.HBM)] + vmem(1), out_specs=tuple(vmem(3)),
+        scratch_shapes=[pltpu.VMEM((SHIFT_ROWS, width), f32), pltpu.SemaphoreType.DMA((2,))],
         compiler_params=room(8), name="pack",
-    )(v, shift_tile)
+    )(vectors.reshape(layers * rows, width), node_shift.transpose(1, 0, 2))
     low = lax.ppermute(up, NODES, [(i, i + 1) for i in range(count - 1)])
     high = lax.ppermute(down, NODES, [(i + 1, i) for i in range(count - 1)])
     dual_both = swap(dual_half, "core")

time: 105 us -> 105 us (level)
  transfers between devices with their start and end apart: 9 -> 9, of which waited for: 5 -> 5; matrix products, arithmetic and copies ran while one was open for 1% -> 0% of each run, Pallas kernels for 3% -> 3%
where the time goes in v3:
time: 105 us
  starting transfers between devices  41.5 us (40%)
  blocking collectives  37.5 us (36%)
  waiting for transfers between devices  16 us (15%)
  Pallas kernels  7.04 us (7%)
  local copies, waits for them, and re-layouts  1.69 us (2%)
    all_to_all x2, blocking collectives, spread(): return lax.all_to_all(array, axes, split_axis=0, concat_axis=0, tiled=True)  37.5 us
    ppermute x6, starting transfers between devices, swap(): return lax.ppermute(array, axes, [(i, many - 1 - i) for i in range(many)])  28.9 us
    all_to_all x1, starting transfers between devices, spread(): return lax.all_to_all(array, axes, split_axis=0, concat_axis=0, tiled=True)  9.99 us
    ppermute x6, waiting for transfers between devices, swap(): return lax.ppermute(array, axes, [(i, many - 1 - i) for i in range(many)])  6.74 us
    ppermute x1, waiting for transfers between devices, shards(): low = lax.ppermute(up, NODES, [(i, i + 1) for i in range(count - 1)])  5.11 us
    ppermute x1, waiting for transfers between devices, shards(): high = lax.ppermute(down, NODES, [(i + 1, i) for i in range(count - 1)])  4.16 us
    pallas_call x1, Pallas kernels, shards(): pl.pallas_call(functools.partial(filter_kernel, gy, dofs), out_shape=jax....  3.24 us
  transfers between devices with their start and end apart: 9, of which 5 were waited for; matrix products, arithmetic and copies ran while one was open for 0% of the time, Pallas kernels for 3%

profile of v3, /device:TPU:1, one launch (start us, length us, event | category | flops | bytes accessed | tf_op | source)
XLA Modules:
  0.0 104.6 jit_solution(112143564660726193)
XLA Ops:
  0.6 5.5 %collective-permute-start.3 = (bf16[384,512]{1,0:T(8,128)(2,1)}, bf16[384,512]{1,0:T(8,128)(2,1)S(1)}, u32[]{:S(2)}, u32[]{:S(2)}) collective-permute-start(bf16[384,512]{1,0:T(8,128)(2,1)} %own_ref.1), channel_id=1, source_target_pairs={{0,2},{2,0},{1,3},{3,1},{4,6},{6,4},{5,7},{7,5},{8,10},{10,8},{9,1... | collective-permute-start | bytes 1179656 | tf_op jit(solution)/shard_map/ppermute | solution.py:231
  6.1 5.2 %collective-permute-start.2 = (bf16[384,512]{1,0:T(8,128)(2,1)}, bf16[384,512]{1,0:T(8,128)(2,1)S(1)}, u32[]{:S(2)}, u32[]{:S(2)}) collective-permute-start(bf16[384,512]{1,0:T(8,128)(2,1)} %own_ref.1), channel_id=1, source_target_pairs={{0,1},{1,0},{2,3},{3,2},{4,5},{5,4},{6,7},{7,6},{8,9},{9,8},{10,11... | collective-permute-start | bytes 1179656 | tf_op jit(solution)/shard_map/ppermute | solution.py:231
  11.3 0.5 collective-permute-done.3.half_ref
  11.9 8.9 %collective-permute-start.4 = (bf16[384,512]{1,0:T(8,128)(2,1)S(1)}, bf16[384,512]{1,0:T(8,128)(2,1)S(1)}, u32[]{:S(2)}, u32[]{:S(2)}) collective-permute-start(bf16[384,512]{1,0:T(8,128)(2,1)S(1)} %collective-permute-done.3.half_ref), channel_id=1, source_target_pairs={{0,1},{1,0},{2,3},{3,2},{4,5},{5,4},{6,7},{7,6},{8,9},{9,8},{10,11... | collective-permute-start | bytes 1179656 | tf_op jit(solution)/shard_map/ppermute | solution.py:231
  20.8 0.0 copy-start
  20.8 1.0 copy-done
  21.8 0.7 copy-done.3
  22.5 0.1 pack.1
  22.6 1.3 %collective-permute-start = (bf16[1184,128]{1,0:T(8,128)(2,1)S(1)}, bf16[1184,128]{1,0:T(8,128)(2,1)S(1)}, u32[]{:S(2)}, u32[]{:S(2)}) collective-permute-start(bf16[1184,128]{1,0:T(8,128)(2,1)S(1)} %get-tuple-element.9), channel_id=1, source_target_pairs={{0,4},{4,8},{8,12},{12,16},{16,20},{20,24},{24,28},{28,32},{32,36}... | collective-permute-start | bytes 909320 | tf_op jit(solution)/shard_map/ppermute | solution.py:246
  23.9 1.3 %collective-permute-start.1 = (bf16[1184,128]{1,0:T(8,128)(2,1)S(1)}, bf16[1184,128]{1,0:T(8,128)(2,1)S(1)}, u32[]{:S(2)}, u32[]{:S(2)}) collective-permute-start(bf16[1184,128]{1,0:T(8,128)(2,1)S(1)} %get-tuple-element.10), channel_id=1, source_target_pairs={{4,0},{8,4},{12,8},{16,12},{20,16},{24,20},{28,24},{32,28},{36,32}... | collective-permute-start | bytes 909320 | tf_op jit(solution)/shard_map/ppermute | solution.py:247
  25.2 0.1 pad_add_fusion.place_ref
  25.3 5.1 %collective-permute-done.low_ref = bf16[1184,128]{1,0:T(8,128)(2,1)S(1)} collective-permute-done((bf16[1184,128]{1,0:T(8,128)(2,1)S(1)}, bf16[1184,128]{1,0:T(8,128)(2,1)S(1)}, u32[]{:S(2)}, u32[]{:S(2)}) %collective-permute-start) | collective-permute-done | bytes 303136 | tf_op jit(solution)/shard_map/ppermute | solution.py:246
  30.4 4.2 %collective-permute-done.1.high_ref = bf16[1184,128]{1,0:T(8,128)(2,1)S(1)} collective-permute-done((bf16[1184,128]{1,0:T(8,128)(2,1)S(1)}, bf16[1184,128]{1,0:T(8,128)(2,1)S(1)}, u32[]{:S(2)}, u32[]{:S(2)}) %collective-permute-start.1) | collective-permute-done | bytes 303136 | tf_op jit(solution)/shard_map/ppermute | solution.py:247
  34.6 0.0 copy-done.1
  34.6 0.0 copy-done.4
  34.6 3.2 %filter.1.f_ref = bf16[4,384,128]{2,1,0:T(8,128)(2,1)S(1)} custom-call(f32[4,4]{1,0:T(4,128)S(1)} %copy-done.4, s32[4]{0:T(128)S(1)} %pad_add_fusion.place_ref, bf16[4,384,128]{2,1,0:T(8,128)(2,1)S(1)} %bitcast.8, bf16[1184,128]{1,0:T(8,128)(2,1)S(1)} %collective-permute-done.low_ref, bf16[1184,128]{1,0:T(8,128)(2,1)S(1)} %collective-permute-done.1.high_ref, ...), custom_call_target="tpu_custom_call" | custom-call | tf_op jit(solution)/shard_map/filter/pallas_call | solution.py:254
  37.8 0.0 collective-permute-done.2.core_ref
  37.9 0.0 collective-permute-done.4.both_ref
  37.9 0.0 copy-done.2
  37.9 1.1 %gram.1 = (bf16[16,32,128]{2,1,0:T(8,128)(2,1)S(1)}, bf16[384,128]{1,0:T(8,128)(2,1)S(1)}, bf16[384,128]{1,0:T(8,128)(2,1)S(1)}, bf16[384,128]{1,0:T(8,128)(2,1)S(1)}) custom-call(s32[4]{0:T(128)S(1)} %pad_add_fusion.place_ref, bf16[384,512]{1,0:T(8,128)(2,1)S(1)} %copy-done.2, bf16[384,512]{1,0:T(8,128)(2,1)S(1)} %collective-permute-done.2.core_ref, ...), custom_call_target="tpu_custom_call" | custom-call | tf_op jit(solution)/shard_map/gram/pallas_call | solution.py:268
  39.0 16.3 %all_to_all.15.in_ref = bf16[16,32,128]{2,1,0:T(8,128)(2,1)S(1)} all-to-all(bf16[16,32,128]{2,1,0:T(8,128)(2,1)S(1)} %get-tuple-element.15), channel_id=1, replica_groups=mesh['x_lo'=2,'y'=4,'z_hi'=8,'z_lo'=2,'x_hi'=2,'core'=2] {'x_lo','y','z_..., dimensions={0} | all-to-all | bytes 262144 | tf_op jit(solution)/shard_map/all_to_all | solution.py:234
  55.3 21.1 %all_to_all.16.in_ref = bf16[8,32,128]{2,1,0:T(8,128)(2,1)S(1)} all-to-all(bf16[8,32,128]{2,1,0:T(8,128)(2,1)S(1)} %shard_map.59), channel_id=1, replica_groups=mesh['x_lo'=2,'y'=4,'z_hi'=8,'z_lo'=2,'x_hi'=2,'core'=2] {'z_hi'}, dimensions={0} | all-to-all | bytes 131072 | tf_op jit(solution)/shard_map/all_to_all | solution.py:234
  76.4 0.8 shard_map.60
  77.3 10.0 %all-to-all-start.2 = ((bf16[64,32,128]{2,1,0:T(8,128)(2,1)}), bf16[64,32,128]{2,1,0:T(8,128)(2,1)S(1)}, u32[]{:S(2)}, u32[]{:S(2)}) async-start(bf16[64,32,128]{2,1,0:T(8,128)(2,1)} %shard_map.60), calls=%async_computation.2 | async-start | bytes 1048576 | tf_op jit(solution)/shard_map/all_to_all | solution.py:234
  87.3 2.4 %collective-permute-start.5 = (bf16[384,128]{1,0:T(8,128)(2,1)S(1)}, bf16[384,128]{1,0:T(8,128)(2,1)S(1)}, u32[]{:S(2)}, u32[]{:S(2)}) collective-permute-start(bf16[384,128]{1,0:T(8,128)(2,1)S(1)} %get-tuple-element.12), channel_id=1, source_target_pairs={{0,1},{1,0},{2,3},{3,2},{4,5},{5,4},{6,7},{7,6},{8,9},{9,8},{10,11... | collective-permute-start | bytes 294920 | tf_op jit(solution)/shard_map/ppermute | solution.py:231
  89.6 4.8 %collective-permute-start.6 = (bf16[384,128]{1,0:T(8,128)(2,1)S(1)}, bf16[384,128]{1,0:T(8,128)(2,1)S(1)}, u32[]{:S(2)}, u32[]{:S(2)}) collective-permute-start(bf16[384,128]{1,0:T(8,128)(2,1)S(1)} %get-tuple-element.13), channel_id=1, source_target_pairs={{0,2},{2,0},{1,3},{3,1},{4,6},{6,4},{5,7},{7,5},{8,10},{10,8},{9,1... | collective-permute-start | bytes 294920 | tf_op jit(solution)/shard_map/ppermute | solution.py:231
  94.5 2.2 %collective-permute-start.7 = (bf16[384,128]{1,0:T(8,128)(2,1)S(1)}, bf16[384,128]{1,0:T(8,128)(2,1)S(1)}, u32[]{:S(2)}, u32[]{:S(2)}) collective-permute-start(bf16[384,128]{1,0:T(8,128)(2,1)S(1)} %get-tuple-element.14), channel_id=1, source_target_pairs={{0,3},{1,2},{2,1},{3,0},{4,7},{5,6},{6,5},{7,4},{8,11},{9,10},{10,... | collective-permute-start | bytes 294920 | tf_op jit(solution)/shard_map/ppermute | solution.py:231
  96.7 0.0 collective-permute-done.5.core_ref
  96.7 2.0 %collective-permute-done.6.half_ref = bf16[384,128]{1,0:T(8,128)(2,1)S(1)} collective-permute-done((bf16[384,128]{1,0:T(8,128)(2,1)S(1)}, bf16[384,128]{1,0:T(8,128)(2,1)S(1)}, u32[]{:S(2)}, u32[]{:S(2)}) %collective-permute-start.6) | collective-permute-done | bytes 98336 | tf_op jit(solution)/shard_map/ppermute | solution.py:231
  98.7 4.2 %collective-permute-done.7.both_ref = bf16[384,128]{1,0:T(8,128)(2,1)S(1)} collective-permute-done((bf16[384,128]{1,0:T(8,128)(2,1)S(1)}, bf16[384,128]{1,0:T(8,128)(2,1)S(1)}, u32[]{:S(2)}, u32[]{:S(2)}) %collective-permute-start.7) | collective-permute-done | bytes 98336 | tf_op jit(solution)/shard_map/ppermute | solution.py:231
  102.9 0.0 all-to-all-done.2.g_ref
  102.9 1.7 %rotate.1 = (f32[128,512]{1,0:T(8,128)}, bf16[384,512]{1,0:T(8,128)(2,1)}) custom-call(s32[4]{0:T(128)S(1)} %pad_add_fusion.place_ref, bf16[4,384,128]{2,1,0:T(8,128)(2,1)S(1)} %filter.1.f_ref, bf16[384,128]{1,0:T(8,128)(2,1)S(1)} %collective-permute-done.5.core_ref, bf16[384,128]{1,0:T(8,128)(2,1)S(1)} %collective-permute-done.6.half_ref, ...), custom_call_target="tpu_custom_call" | custom-call | tf_op jit(solution)/shard_map/rotate/pallas_call | solution.py:288
  (5 shorter events, 0.0 us)
Async XLA Ops:
  0.6 11.2 %collective-permute-start.3 = (bf16[384,512]{1,0:T(8,128)(2,1)}, bf16[384,512]{1,0:T(8,128)(2,1)S(1)}, u32[]{:S(2)}, u32[]{:S(2)}) collective-permute-start(bf16[384,512]{1,0:T(8,128)(2,1)} %own_ref.1), channel_id=1, source_target_pairs={{0,2},{2,0},{1,3},{3,1},{4,6},{6,4},{5,7},{7,5},{8,10},{10,8},{9,1... | collective-permute-start | bytes 1179656 | tf_op jit(solution)/shard_map/ppermute | solution.py:231
  6.1 31.7 %collective-permute-start.2 = (bf16[384,512]{1,0:T(8,128)(2,1)}, bf16[384,512]{1,0:T(8,128)(2,1)S(1)}, u32[]{:S(2)}, u32[]{:S(2)}) collective-permute-start(bf16[384,512]{1,0:T(8,128)(2,1)} %own_ref.1), channel_id=1, source_target_pairs={{0,1},{1,0},{2,3},{3,2},{4,5},{5,4},{6,7},{7,6},{8,9},{9,8},{10,11... | collective-permute-start | bytes 1179656 | tf_op jit(solution)/shard_map/ppermute | solution.py:231
  11.9 26.0 %collective-permute-start.4 = (bf16[384,512]{1,0:T(8,128)(2,1)S(1)}, bf16[384,512]{1,0:T(8,128)(2,1)S(1)}, u32[]{:S(2)}, u32[]{:S(2)}) collective-permute-start(bf16[384,512]{1,0:T(8,128)(2,1)S(1)} %collective-permute-done.3.half_ref), channel_id=1, source_target_pairs={{0,1},{1,0},{2,3},{3,2},{4,5},{5,4},{6,7},{7,6},{8,9},{9,8},{10,11... | collective-permute-start | bytes 1179656 | tf_op jit(solution)/shard_map/ppermute | solution.py:231
  20.8 1.0 copy-start
  21.8 0.7 copy-start.3
  22.4 12.1 %copy-start.1 = (bf16[4,4,6,16,128]{4,3,2,1,0:T(8,128)(2,1)S(1)}, bf16[4,4,6,16,128]{4,3,2,1,0:T(8,128)(2,1)}, u32[]{:S(2)}) copy-start(bf16[4,4,6,16,128]{4,3,2,1,0:T(8,128)(2,1)} %param.4) | copy-start | bytes 1179652
  22.6 7.8 %collective-permute-start = (bf16[1184,128]{1,0:T(8,128)(2,1)S(1)}, bf16[1184,128]{1,0:T(8,128)(2,1)S(1)}, u32[]{:S(2)}, u32[]{:S(2)}) collective-permute-start(bf16[1184,128]{1,0:T(8,128)(2,1)S(1)} %get-tuple-element.9), channel_id=1, source_target_pairs={{0,4},{4,8},{8,12},{12,16},{16,20},{20,24},{24,28},{28,32},{32,36}... | collective-permute-start | bytes 909320 | tf_op jit(solution)/shard_map/ppermute | solution.py:246
  23.9 10.7 %collective-permute-start.1 = (bf16[1184,128]{1,0:T(8,128)(2,1)S(1)}, bf16[1184,128]{1,0:T(8,128)(2,1)S(1)}, u32[]{:S(2)}, u32[]{:S(2)}) collective-permute-start(bf16[1184,128]{1,0:T(8,128)(2,1)S(1)} %get-tuple-element.10), channel_id=1, source_target_pairs={{4,0},{8,4},{12,8},{16,12},{20,16},{24,20},{28,24},{32,28},{36,32}... | collective-permute-start | bytes 909320 | tf_op jit(solution)/shard_map/ppermute | solution.py:247
  25.3 9.3 %copy-start.4 = (f32[4,4]{1,0:T(4,128)S(1)}, f32[4,4]{1,0:T(4,128)}, u32[]{:S(2)}) copy-start(f32[4,4]{1,0:T(4,128)} %coup_ref.1) | copy-start | bytes 196
  34.6 3.3 %copy-start.2 = (bf16[384,512]{1,0:T(8,128)(2,1)S(1)}, bf16[384,512]{1,0:T(8,128)(2,1)}, u32[]{:S(2)}) copy-start(bf16[384,512]{1,0:T(8,128)(2,1)} %own_ref.1) | copy-start | bytes 1179652
  77.3 25.6 %all-to-all-start.2 = ((bf16[64,32,128]{2,1,0:T(8,128)(2,1)}), bf16[64,32,128]{2,1,0:T(8,128)(2,1)S(1)}, u32[]{:S(2)}, u32[]{:S(2)}) async-start(bf16[64,32,128]{2,1,0:T(8,128)(2,1)} %shard_map.60), calls=%async_computation.2 | async-start | bytes 1048576 | tf_op jit(solution)/shard_map/all_to_all | solution.py:234
  87.3 9.4 %collective-permute-start.5 = (bf16[384,128]{1,0:T(8,128)(2,1)S(1)}, bf16[384,128]{1,0:T(8,128)(2,1)S(1)}, u32[]{:S(2)}, u32[]{:S(2)}) collective-permute-start(bf16[384,128]{1,0:T(8,128)(2,1)S(1)} %get-tuple-element.12), channel_id=1, source_target_pairs={{0,1},{1,0},{2,3},{3,2},{4,5},{5,4},{6,7},{7,6},{8,9},{9,8},{10,11... | collective-permute-start | bytes 294920 | tf_op jit(solution)/shard_map/ppermute | solution.py:231
  89.6 9.0 %collective-permute-start.6 = (bf16[384,128]{1,0:T(8,128)(2,1)S(1)}, bf16[384,128]{1,0:T(8,128)(2,1)S(1)}, u32[]{:S(2)}, u32[]{:S(2)}) collective-permute-start(bf16[384,128]{1,0:T(8,128)(2,1)S(1)} %get-tuple-element.13), channel_id=1, source_target_pairs={{0,2},{2,0},{1,3},{3,1},{4,6},{6,4},{5,7},{7,5},{8,10},{10,8},{9,1... | collective-permute-start | bytes 294920 | tf_op jit(solution)/shard_map/ppermute | solution.py:231
  94.5 8.4 %collective-permute-start.7 = (bf16[384,128]{1,0:T(8,128)(2,1)S(1)}, bf16[384,128]{1,0:T(8,128)(2,1)S(1)}, u32[]{:S(2)}, u32[]{:S(2)}) collective-permute-start(bf16[384,128]{1,0:T(8,128)(2,1)S(1)} %get-tuple-element.14), channel_id=1, source_target_pairs={{0,3},{1,2},{2,1},{3,0},{4,7},{5,6},{6,5},{7,4},{8,11},{9,10},{10,... | collective-permute-start | bytes 294920 | tf_op jit(solution)/shard_map/ppermute | solution.py:231

commit v4 on v3

--- a/solution.py
+++ b/solution.py
@@ -164,7 +164,7 @@
 
 
 def gram_kernel(
-    place_ref, own_ref, core_ref, half_ref, both_ref, f_ref, out_ref, to_core, to_half, to_both
+    place_ref, own_ref, core_ref, half_ref, both_ref, f_ref, out_ref, to_half
 ):
     pieces, height, _ = out_ref.shape
     here, core = place_ref[2], place_ref[3]
@@ -175,8 +175,8 @@
             f_ref[at], dual[...], (((0,), (0,)), ((), ())), preferred_element_type=f32
         )
     out_ref[...] = part.T.astype(bf16).reshape(pieces, height, LANES)
-    for at, send in zip(layers[1:], (to_core, to_half, to_both)):
-        send[...] = f_ref[at]
+    first = 2 * (1 - here)
+    to_half[...] = f_ref[pl.ds(first, 2)]
 
 
 def spots(here, core):
@@ -193,26 +193,53 @@
         out_ref[k] = piece
 
 
-def rotate_kernel(scale, place_ref, f_ref, core_ref, half_ref, both_ref, g_ref, gram_ref, out_ref):
-    blocks = out_ref.shape[1] // LANES
+def far_sum_kernel(place_ref, in_ref, f_ref, half_ref, out_ref, to_core):
+    sum_kernel(in_ref, out_ref)
+    here, core = place_ref[2], place_ref[3]
+    to_core[0] = f_ref[2 * here + 1 - core]
+    to_core[1] = half_ref[1 - core]
+
+
+def rows_of(g_ref, half, at):
     pieces, height, _ = g_ref.shape
-    each = pieces // blocks
-    own = each // blocks
+    each = pieces // 2
+    own = LANES // height
+    return g_ref[pl.ds(half * each + at * own, own)].reshape(LANES, LANES)
+
+
+def rotated_half(scale, place_ref, f_ref, half_ref, core_ref, g_ref):
     here, core = place_ref[2], place_ref[3]
-    places = [2 * a + b for a, b in spots(here, core)]
-    cols = side_by_side([f_ref[places[0]], core_ref[...], half_ref[...], both_ref[...]])
-
-    def rows_of(k, at):
-        return g_ref[pl.ds(k * each + at * own, own)].reshape(own * height, LANES)
-
-    for b in range(0, blocks, 2):
-        turn = side_by_side(
-            [jnp.concatenate([rows_of(k, at) for at in places], axis=0) for k in (b, b + 1)]
-        )
-        turned = jnp.dot(cols, turn, preferred_element_type=f32) * scale
-        out_ref[:, b * LANES : (b + 2) * LANES] = turned.astype(bf16)
-        for k in (b, b + 1):
-            gram_ref[:, k * LANES : (k + 1) * LANES] = rows_of(k, places[0]).astype(f32)
+    places = [
+        2 * here + core,
+        2 * (1 - here) + core,
+        2 * here + 1 - core,
+        2 * (1 - here) + 1 - core,
+    ]
+    cols = side_by_side([f_ref[places[0]], half_ref[core], core_ref[0], core_ref[1]])
+    turn = side_by_side(
+        [jnp.concatenate([rows_of(g_ref, k, at) for at in places], axis=0) for k in range(2)]
+    )
+    return (jnp.dot(cols, turn, preferred_element_type=f32) * scale).astype(bf16)
+
+
+def rotate_half_kernel(scale, place_ref, f_ref, half_ref, core_ref, g_ref, out_ref):
+    out_ref[...] = rotated_half(scale, place_ref, f_ref, half_ref, core_ref, g_ref)
+
+
+def rotate_kernel(
+    scale, place_ref, f_ref, half_ref, core_ref, g_ref, far_ref, done_ref, gram_ref, out_ref
+):
+    here, core = place_ref[2], place_ref[3]
+    other = rotated_half(scale, place_ref, f_ref, half_ref, core_ref, far_ref)
+    for k in range(2):
+        cut = slice(k * LANES, (k + 1) * LANES)
+        mine = pl.ds(pl.multiple_of((2 * k + core) * LANES, LANES), LANES)
+        theirs = pl.ds(pl.multiple_of((2 * k + 1 - core) * LANES, LANES), LANES)
+        out_ref[:, mine] = done_ref[:, cut]
+        out_ref[:, theirs] = other[:, cut]
+        at = 2 * here + core
+        gram_ref[:, mine] = rows_of(g_ref, k, at).astype(f32)
+        gram_ref[:, theirs] = rows_of(far_ref, k, at).astype(f32)
 
 
 def shards(vectors, node_shift, coupling, dual_basis):
@@ -264,35 +291,43 @@
         ],
         compiler_params=room(16), name="filter",
     )(coupling, place, v, low, high, shift_tile)
-    layer = jax.ShapeDtypeStruct((rows, width), bf16)
-    terms, to_core, to_half, to_both = pl.pallas_call(
+    two = jax.ShapeDtypeStruct((2, rows, width), bf16)
+    terms, to_half = pl.pallas_call(
         gram_kernel,
-        out_shape=(jax.ShapeDtypeStruct((near, height, LANES), bf16), layer, layer, layer),
-        in_specs=smem(1) + vmem(5), out_specs=tuple(vmem(4)), compiler_params=room(12), name="gram",
+        out_shape=(jax.ShapeDtypeStruct((near, height, LANES), bf16), two),
+        in_specs=smem(1) + vmem(5), out_specs=tuple(vmem(2)), compiler_params=room(12), name="gram",
     )(place, dual_basis, dual_core, dual_half, dual_both, own)
+    from_half = swap(to_half, HALVES)
+    pieces = spread(terms, NEAR)
+    part = pl.pallas_call(
+        sum_kernel,
+        out_shape=jax.ShapeDtypeStruct((far, height, LANES), bf16),
+        in_specs=vmem(1), out_specs=vmem(1)[0], compiler_params=room(8), name="near_sum",
+    )(pieces)
+    pieces = spread(part, FAR)
+    full, to_core = pl.pallas_call(
+        far_sum_kernel,
+        out_shape=(jax.ShapeDtypeStruct((2 * near, height, LANES), bf16), two),
+        in_specs=smem(1) + vmem(3), out_specs=tuple(vmem(2)), compiler_params=room(8), name="far_sum",
+    )(place, pieces, own, from_half)
     from_core = swap(to_core, "core")
-    from_half = swap(to_half, HALVES)
-    from_both = swap(to_both, COLS)
-
-    def summed(pieces, copies):
-        return pl.pallas_call(
-            sum_kernel,
-            out_shape=jax.ShapeDtypeStruct((copies, height, LANES), bf16),
-            in_specs=vmem(1), out_specs=vmem(1)[0], compiler_params=room(8),
-        )(pieces)
-
-    pieces = spread(terms, NEAR)
-    part = summed(pieces, far)
-    pieces = spread(part, FAR)
-    pieces = spread(summed(pieces, near * blocks), COLS + NEAR)
+    pieces = spread(full, (HALVES,) + NEAR)
+    other = swap(pieces, "core")
+    scale = cols ** (-0.5)
+    half = pl.pallas_call(
+        functools.partial(rotate_half_kernel, scale),
+        out_shape=jax.ShapeDtypeStruct((rows, cols // 2), bf16),
+        in_specs=smem(1) + vmem(4), out_specs=vmem(1)[0], compiler_params=room(8),
+        name="rotate_half",
+    )(place, own, from_half, from_core, pieces)
     gram, rotated = pl.pallas_call(
-        functools.partial(rotate_kernel, cols ** (-0.5)),
+        functools.partial(rotate_kernel, scale),
         out_shape=(
             jax.ShapeDtypeStruct((cols // blocks, cols), f32),
             jax.ShapeDtypeStruct((rows, cols), bf16),
         ),
-        in_specs=smem(1) + vmem(5), out_specs=tuple(vmem(2)), compiler_params=room(12), name="rotate",
-    )(place, own, from_core, from_half, from_both, pieces)
+        in_specs=smem(1) + vmem(6), out_specs=tuple(vmem(2)), compiler_params=room(12), name="rotate",
+    )(place, own, from_half, from_core, pieces, other, half)
     return gram, rotated
 
 

time: 105 us -> 105 us (level)
  blocking collectives: 37.5 us -> 29.6 us
  starting transfers between devices: 41.5 us -> 45.3 us
  waiting for transfers between devices: 16 us -> 19 us
  Pallas kernels: 7.04 us -> 8.13 us
    all_to_all x2, blocking collectives: 37.5 us -> 29.6 us  [spread(): return lax.all_to_all(array, axes, split_axis=0, concat_axis=0, tiled=True)]
    ppermute x6, starting transfers between devices: 28.9 us -> 33.7 us  [swap(): return lax.ppermute(array, axes, [(i, many - 1 - i) for i in range(many)])]
    all_to_all x1, waiting for transfers between devices: 0.01 us -> 4.3 us  [spread(): return lax.all_to_all(array, axes, split_axis=0, concat_axis=0, tiled=True)]
    ppermute x6, waiting for transfers between devices: 6.74 us -> 5.42 us  [swap(): return lax.ppermute(array, axes, [(i, many - 1 - i) for i in range(many)])]
    pallas_call x3 -> x4, Pallas kernels: 2.57 us -> 3.66 us  [the longest x1 1.62 us: shards(): pl.pallas_call(functools.partial(rotate_kernel, scale), out_shape=(jax.Sh...]
  transfers between devices with their start and end apart: 9 -> 9, of which waited for: 5 -> 6; matrix products, arithmetic and copies ran while one was open for 0% -> 0% of each run, Pallas kernels for 3% -> 4%
where the time goes in v4:
time: 105 us
  starting transfers between devices  45.3 us (43%)
  blocking collectives  29.6 us (28%)
  waiting for transfers between devices  19 us (18%)
  Pallas kernels  8.13 us (8%)
  local copies, waits for them, and re-layouts  1.69 us (2%)
    ppermute x6, starting transfers between devices, swap(): return lax.ppermute(array, axes, [(i, many - 1 - i) for i in range(many)])  33.7 us
    all_to_all x2, blocking collectives, spread(): return lax.all_to_all(array, axes, split_axis=0, concat_axis=0, tiled=True)  29.6 us
    all_to_all x1, starting transfers between devices, spread(): return lax.all_to_all(array, axes, split_axis=0, concat_axis=0, tiled=True)  9.02 us
    ppermute x6, waiting for transfers between devices, swap(): return lax.ppermute(array, axes, [(i, many - 1 - i) for i in range(many)])  5.42 us
    ppermute x1, waiting for transfers between devices, shards(): low = lax.ppermute(up, NODES, [(i, i + 1) for i in range(count - 1)])  5.11 us
    all_to_all x1, waiting for transfers between devices, spread(): return lax.all_to_all(array, axes, split_axis=0, concat_axis=0, tiled=True)  4.3 us
    ppermute x1, waiting for transfers between devices, shards(): high = lax.ppermute(down, NODES, [(i + 1, i) for i in range(count - 1)])  4.16 us
    pallas_call x1, Pallas kernels, shards(): pl.pallas_call(functools.partial(filter_kernel, gy, dofs), out_shape=jax....  3.24 us
  transfers between devices with their start and end apart: 9, of which 6 were waited for; matrix products, arithmetic and copies ran while one was open for 0% of the time, Pallas kernels for 4%

profile of v4, /device:TPU:1, one launch (start us, length us, event | category | flops | bytes accessed | tf_op | source)
XLA Modules:
  0.0 104.6 jit_solution(11572974055686304282)
XLA Ops:
  0.6 5.5 %collective-permute-start.3 = (bf16[384,512]{1,0:T(8,128)(2,1)}, bf16[384,512]{1,0:T(8,128)(2,1)S(1)}, u32[]{:S(2)}, u32[]{:S(2)}) collective-permute-start(bf16[384,512]{1,0:T(8,128)(2,1)} %own_ref.1), channel_id=1, source_target_pairs={{0,2},{2,0},{1,3},{3,1},{4,6},{6,4},{5,7},{7,5},{8,10},{10,8},{9,1... | collective-permute-start | bytes 1179656 | tf_op jit(solution)/shard_map/ppermute | solution.py:258
  6.1 5.2 %collective-permute-start.2 = (bf16[384,512]{1,0:T(8,128)(2,1)}, bf16[384,512]{1,0:T(8,128)(2,1)S(1)}, u32[]{:S(2)}, u32[]{:S(2)}) collective-permute-start(bf16[384,512]{1,0:T(8,128)(2,1)} %own_ref.1), channel_id=1, source_target_pairs={{0,1},{1,0},{2,3},{3,2},{4,5},{5,4},{6,7},{7,6},{8,9},{9,8},{10,11... | collective-permute-start | bytes 1179656 | tf_op jit(solution)/shard_map/ppermute | solution.py:258
  11.3 0.5 collective-permute-done.3.half_ref
  11.9 8.9 %collective-permute-start.4 = (bf16[384,512]{1,0:T(8,128)(2,1)S(1)}, bf16[384,512]{1,0:T(8,128)(2,1)S(1)}, u32[]{:S(2)}, u32[]{:S(2)}) collective-permute-start(bf16[384,512]{1,0:T(8,128)(2,1)S(1)} %collective-permute-done.3.half_ref), channel_id=1, source_target_pairs={{0,1},{1,0},{2,3},{3,2},{4,5},{5,4},{6,7},{7,6},{8,9},{9,8},{10,11... | collective-permute-start | bytes 1179656 | tf_op jit(solution)/shard_map/ppermute | solution.py:258
  20.8 0.0 copy-start
  20.8 1.0 copy-done
  21.8 0.7 copy-done.3
  22.5 0.1 pack.1
  22.6 1.3 %collective-permute-start = (bf16[1184,128]{1,0:T(8,128)(2,1)S(1)}, bf16[1184,128]{1,0:T(8,128)(2,1)S(1)}, u32[]{:S(2)}, u32[]{:S(2)}) collective-permute-start(bf16[1184,128]{1,0:T(8,128)(2,1)S(1)} %get-tuple-element.9), channel_id=1, source_target_pairs={{0,4},{4,8},{8,12},{12,16},{16,20},{20,24},{24,28},{28,32},{32,36}... | collective-permute-start | bytes 909320 | tf_op jit(solution)/shard_map/ppermute | solution.py:273
  23.9 1.3 %collective-permute-start.1 = (bf16[1184,128]{1,0:T(8,128)(2,1)S(1)}, bf16[1184,128]{1,0:T(8,128)(2,1)S(1)}, u32[]{:S(2)}, u32[]{:S(2)}) collective-permute-start(bf16[1184,128]{1,0:T(8,128)(2,1)S(1)} %get-tuple-element.10), channel_id=1, source_target_pairs={{4,0},{8,4},{12,8},{16,12},{20,16},{24,20},{28,24},{32,28},{36,32}... | collective-permute-start | bytes 909320 | tf_op jit(solution)/shard_map/ppermute | solution.py:274
  25.2 0.1 pad_add_fusion.place_ref
  25.3 5.1 %collective-permute-done.low_ref = bf16[1184,128]{1,0:T(8,128)(2,1)S(1)} collective-permute-done((bf16[1184,128]{1,0:T(8,128)(2,1)S(1)}, bf16[1184,128]{1,0:T(8,128)(2,1)S(1)}, u32[]{:S(2)}, u32[]{:S(2)}) %collective-permute-start) | collective-permute-done | bytes 303136 | tf_op jit(solution)/shard_map/ppermute | solution.py:273
  30.4 4.2 %collective-permute-done.1.high_ref = bf16[1184,128]{1,0:T(8,128)(2,1)S(1)} collective-permute-done((bf16[1184,128]{1,0:T(8,128)(2,1)S(1)}, bf16[1184,128]{1,0:T(8,128)(2,1)S(1)}, u32[]{:S(2)}, u32[]{:S(2)}) %collective-permute-start.1) | collective-permute-done | bytes 303136 | tf_op jit(solution)/shard_map/ppermute | solution.py:274
  34.6 3.2 %filter.1.f_ref = bf16[4,384,128]{2,1,0:T(8,128)(2,1)S(1)} custom-call(f32[4,4]{1,0:T(4,128)S(1)} %copy-done.4, s32[4]{0:T(128)S(1)} %pad_add_fusion.place_ref, bf16[4,384,128]{2,1,0:T(8,128)(2,1)S(1)} %bitcast.8, bf16[1184,128]{1,0:T(8,128)(2,1)S(1)} %collective-permute-done.low_ref, bf16[1184,128]{1,0:T(8,128)(2,1)S(1)} %collective-permute-done.1.high_ref, ...), custom_call_target="tpu_custom_call" | custom-call | tf_op jit(solution)/shard_map/filter/pallas_call | solution.py:281
  37.8 0.0 collective-permute-done.2.core_ref
  37.9 0.0 collective-permute-done.4.both_ref
  37.9 0.0 copy-done.2
  37.9 1.1 %gram.1 = (bf16[16,32,128]{2,1,0:T(8,128)(2,1)S(1)}, bf16[2,384,128]{2,1,0:T(8,128)(2,1)S(1)}) custom-call(s32[4]{0:T(128)S(1)} %pad_add_fusion.place_ref, bf16[384,512]{1,0:T(8,128)(2,1)S(1)} %copy-done.2, bf16[384,512]{1,0:T(8,128)(2,1)S(1)} %collective-permute-done.2.core_ref, bf16[384,512]{1,0:T(8,128)(2,1)S(1)} %collective-permute-done.3.half_ref, ...), custom_call_target="tpu_custom_call" | custom-call | tf_op jit(solution)/shard_map/gram/pallas_call | solution.py:295
  39.0 16.3 %all_to_all.15.in_ref = bf16[16,32,128]{2,1,0:T(8,128)(2,1)S(1)} all-to-all(bf16[16,32,128]{2,1,0:T(8,128)(2,1)S(1)} %get-tuple-element.13), channel_id=1, replica_groups=mesh['x_lo'=2,'y'=4,'z_hi'=8,'z_lo'=2,'x_hi'=2,'core'=2] {'x_lo','y','z_..., dimensions={0} | all-to-all | bytes 262144 | tf_op jit(solution)/shard_map/all_to_all | solution.py:261
  55.3 0.7 near_sum.1
  55.9 9.0 %all-to-all-start.1 = ((bf16[8,32,128]{2,1,0:T(8,128)(2,1)}), bf16[8,32,128]{2,1,0:T(8,128)(2,1)S(1)}, u32[]{:S(2)}, u32[]{:S(2)}) async-start(bf16[8,32,128]{2,1,0:T(8,128)(2,1)} %near_sum.1), calls=%async_computation.1 | async-start | bytes 131072 | tf_op jit(solution)/shard_map/all_to_all | solution.py:261
  65.0 4.4 %collective-permute-start.5 = (bf16[2,384,128]{2,1,0:T(8,128)(2,1)S(1)}, bf16[2,384,128]{2,1,0:T(8,128)(2,1)S(1)}, u32[]{:S(2)}, u32[]{:S(2)}) collective-permute-start(bf16[2,384,128]{2,1,0:T(8,128)(2,1)S(1)} %get-tuple-element.12), channel_id=1, source_target_pairs={{0,2},{2,0},{1,3},{3,1},{4,6},{6,4},{5,7},{7,5},{8,10},{10,8},{9,1... | collective-permute-start | bytes 589832 | tf_op jit(solution)/shard_map/ppermute | solution.py:258
  69.4 3.5 %collective-permute-done.5.half_ref = bf16[2,384,128]{2,1,0:T(8,128)(2,1)S(1)} collective-permute-done((bf16[2,384,128]{2,1,0:T(8,128)(2,1)S(1)}, bf16[2,384,128]{2,1,0:T(8,128)(2,1)S(1)}, u32[]{:S(2)}, u32[]{:S(2)}) %collective-permute-start.5) | collective-permute-done | bytes 196640 | tf_op jit(solution)/shard_map/ppermute | solution.py:258
  72.9 4.3 %all-to-all-done.1.in_ref = bf16[8,32,128]{2,1,0:T(8,128)(2,1)S(1)} async-done(((bf16[8,32,128]{2,1,0:T(8,128)(2,1)}), bf16[8,32,128]{2,1,0:T(8,128)(2,1)S(1)}, u32[]{:S(2)}, u32[]{:S(2)}) %all-to-all-start.1) | async-done | bytes 65568 | tf_op jit(solution)/shard_map/all_to_all | solution.py:261
  77.2 0.6 far_sum.1
  77.7 13.3 %all_to_all.16.g_ref = bf16[32,32,128]{2,1,0:T(8,128)(2,1)S(1)} all-to-all(bf16[32,32,128]{2,1,0:T(8,128)(2,1)S(1)} %get-tuple-element.15), channel_id=1, replica_groups=mesh['x_lo'=2,'y'=4,'z_hi'=8,'z_lo'=2,'x_hi'=2,'core'=2] {'x_hi','x_lo',..., dimensions={0} | all-to-all | bytes 524288 | tf_op jit(solution)/shard_map/all_to_all | solution.py:261
  91.0 7.8 %collective-permute-start.7 = (bf16[32,32,128]{2,1,0:T(8,128)(2,1)S(1)}, bf16[32,32,128]{2,1,0:T(8,128)(2,1)S(1)}, u32[]{:S(2)}, u32[]{:S(2)}) collective-permute-start(bf16[32,32,128]{2,1,0:T(8,128)(2,1)S(1)} %all_to_all.16.g_ref), channel_id=1, source_target_pairs={{0,1},{1,0},{2,3},{3,2},{4,5},{5,4},{6,7},{7,6},{8,9},{9,8},{10,11... | collective-permute-start | bytes 786440 | tf_op jit(solution)/shard_map/ppermute | solution.py:258
  98.8 1.9 %collective-permute-start.6 = (bf16[2,384,128]{2,1,0:T(8,128)(2,1)S(1)}, bf16[2,384,128]{2,1,0:T(8,128)(2,1)S(1)}, u32[]{:S(2)}, u32[]{:S(2)}) collective-permute-start(bf16[2,384,128]{2,1,0:T(8,128)(2,1)S(1)} %get-tuple-element.14), channel_id=1, source_target_pairs={{0,1},{1,0},{2,3},{3,2},{4,5},{5,4},{6,7},{7,6},{8,9},{9,8},{10,11... | collective-permute-start | bytes 589832 | tf_op jit(solution)/shard_map/ppermute | solution.py:258
  100.8 1.4 %collective-permute-done.6.core_ref = bf16[2,384,128]{2,1,0:T(8,128)(2,1)S(1)} collective-permute-done((bf16[2,384,128]{2,1,0:T(8,128)(2,1)S(1)}, bf16[2,384,128]{2,1,0:T(8,128)(2,1)S(1)}, u32[]{:S(2)}, u32[]{:S(2)}) %collective-permute-start.6) | collective-permute-done | bytes 196640 | tf_op jit(solution)/shard_map/ppermute | solution.py:258
  102.2 0.8 rotate_half.1.done_ref
  103.0 0.0 collective-permute-done.7.far_ref
  103.0 1.6 %rotate.1 = (f32[128,512]{1,0:T(8,128)}, bf16[384,512]{1,0:T(8,128)(2,1)}) custom-call(s32[4]{0:T(128)S(1)} %pad_add_fusion.place_ref, bf16[4,384,128]{2,1,0:T(8,128)(2,1)S(1)} %filter.1.f_ref, bf16[2,384,128]{2,1,0:T(8,128)(2,1)S(1)} %collective-permute-done.5.half_ref, bf16[2,384,128]{2,1,0:T(8,128)(2,1)S(1)} %collective-permute-done.6.core_ref, ...), custom_call_target="tpu_custom_call" | custom-call | tf_op jit(solution)/shard_map/rotate/pallas_call | solution.py:323
  (6 shorter events, 0.0 us)
Async XLA Ops:
  0.6 11.2 %collective-permute-start.3 = (bf16[384,512]{1,0:T(8,128)(2,1)}, bf16[384,512]{1,0:T(8,128)(2,1)S(1)}, u32[]{:S(2)}, u32[]{:S(2)}) collective-permute-start(bf16[384,512]{1,0:T(8,128)(2,1)} %own_ref.1), channel_id=1, source_target_pairs={{0,2},{2,0},{1,3},{3,1},{4,6},{6,4},{5,7},{7,5},{8,10},{10,8},{9,1... | collective-permute-start | bytes 1179656 | tf_op jit(solution)/shard_map/ppermute | solution.py:258
  6.1 31.7 %collective-permute-start.2 = (bf16[384,512]{1,0:T(8,128)(2,1)}, bf16[384,512]{1,0:T(8,128)(2,1)S(1)}, u32[]{:S(2)}, u32[]{:S(2)}) collective-permute-start(bf16[384,512]{1,0:T(8,128)(2,1)} %own_ref.1), channel_id=1, source_target_pairs={{0,1},{1,0},{2,3},{3,2},{4,5},{5,4},{6,7},{7,6},{8,9},{9,8},{10,11... | collective-permute-start | bytes 1179656 | tf_op jit(solution)/shard_map/ppermute | solution.py:258
  11.9 26.0 %collective-permute-start.4 = (bf16[384,512]{1,0:T(8,128)(2,1)S(1)}, bf16[384,512]{1,0:T(8,128)(2,1)S(1)}, u32[]{:S(2)}, u32[]{:S(2)}) collective-permute-start(bf16[384,512]{1,0:T(8,128)(2,1)S(1)} %collective-permute-done.3.half_ref), channel_id=1, source_target_pairs={{0,1},{1,0},{2,3},{3,2},{4,5},{5,4},{6,7},{7,6},{8,9},{9,8},{10,11... | collective-permute-start | bytes 1179656 | tf_op jit(solution)/shard_map/ppermute | solution.py:258
  20.8 1.0 copy-start
  21.8 0.7 copy-start.3
  22.4 12.1 %copy-start.1 = (bf16[4,4,6,16,128]{4,3,2,1,0:T(8,128)(2,1)S(1)}, bf16[4,4,6,16,128]{4,3,2,1,0:T(8,128)(2,1)}, u32[]{:S(2)}) copy-start(bf16[4,4,6,16,128]{4,3,2,1,0:T(8,128)(2,1)} %param.4) | copy-start | bytes 1179652
  22.6 7.8 %collective-permute-start = (bf16[1184,128]{1,0:T(8,128)(2,1)S(1)}, bf16[1184,128]{1,0:T(8,128)(2,1)S(1)}, u32[]{:S(2)}, u32[]{:S(2)}) collective-permute-start(bf16[1184,128]{1,0:T(8,128)(2,1)S(1)} %get-tuple-element.9), channel_id=1, source_target_pairs={{0,4},{4,8},{8,12},{12,16},{16,20},{20,24},{24,28},{28,32},{32,36}... | collective-permute-start | bytes 909320 | tf_op jit(solution)/shard_map/ppermute | solution.py:273
  23.9 10.7 %collective-permute-start.1 = (bf16[1184,128]{1,0:T(8,128)(2,1)S(1)}, bf16[1184,128]{1,0:T(8,128)(2,1)S(1)}, u32[]{:S(2)}, u32[]{:S(2)}) collective-permute-start(bf16[1184,128]{1,0:T(8,128)(2,1)S(1)} %get-tuple-element.10), channel_id=1, source_target_pairs={{4,0},{8,4},{12,8},{16,12},{20,16},{24,20},{28,24},{32,28},{36,32}... | collective-permute-start | bytes 909320 | tf_op jit(solution)/shard_map/ppermute | solution.py:274
  25.3 9.3 %copy-start.4 = (f32[4,4]{1,0:T(4,128)S(1)}, f32[4,4]{1,0:T(4,128)}, u32[]{:S(2)}) copy-start(f32[4,4]{1,0:T(4,128)} %coup_ref.1) | copy-start | bytes 196
  34.6 3.3 %copy-start.2 = (bf16[384,512]{1,0:T(8,128)(2,1)S(1)}, bf16[384,512]{1,0:T(8,128)(2,1)}, u32[]{:S(2)}) copy-start(bf16[384,512]{1,0:T(8,128)(2,1)} %own_ref.1) | copy-start | bytes 1179652
  55.9 21.2 %all-to-all-start.1 = ((bf16[8,32,128]{2,1,0:T(8,128)(2,1)}), bf16[8,32,128]{2,1,0:T(8,128)(2,1)S(1)}, u32[]{:S(2)}, u32[]{:S(2)}) async-start(bf16[8,32,128]{2,1,0:T(8,128)(2,1)} %near_sum.1), calls=%async_computation.1 | async-start | bytes 131072 | tf_op jit(solution)/shard_map/all_to_all | solution.py:261
  65.0 7.9 %collective-permute-start.5 = (bf16[2,384,128]{2,1,0:T(8,128)(2,1)S(1)}, bf16[2,384,128]{2,1,0:T(8,128)(2,1)S(1)}, u32[]{:S(2)}, u32[]{:S(2)}) collective-permute-start(bf16[2,384,128]{2,1,0:T(8,128)(2,1)S(1)} %get-tuple-element.12), channel_id=1, source_target_pairs={{0,2},{2,0},{1,3},{3,1},{4,6},{6,4},{5,7},{7,5},{8,10},{10,8},{9,1... | collective-permute-start | bytes 589832 | tf_op jit(solution)/shard_map/ppermute | solution.py:258
  91.0 11.9 %collective-permute-start.7 = (bf16[32,32,128]{2,1,0:T(8,128)(2,1)S(1)}, bf16[32,32,128]{2,1,0:T(8,128)(2,1)S(1)}, u32[]{:S(2)}, u32[]{:S(2)}) collective-permute-start(bf16[32,32,128]{2,1,0:T(8,128)(2,1)S(1)} %all_to_all.16.g_ref), channel_id=1, source_target_pairs={{0,1},{1,0},{2,3},{3,2},{4,5},{5,4},{6,7},{7,6},{8,9},{9,8},{10,11... | collective-permute-start | bytes 786440 | tf_op jit(solution)/shard_map/ppermute | solution.py:258
  98.8 3.3 %collective-permute-start.6 = (bf16[2,384,128]{2,1,0:T(8,128)(2,1)S(1)}, bf16[2,384,128]{2,1,0:T(8,128)(2,1)S(1)}, u32[]{:S(2)}, u32[]{:S(2)}) collective-permute-start(bf16[2,384,128]{2,1,0:T(8,128)(2,1)S(1)} %get-tuple-element.14), channel_id=1, source_target_pairs={{0,1},{1,0},{2,3},{3,2},{4,5},{5,4},{6,7},{7,6},{8,9},{9,8},{10,11... | collective-permute-start | bytes 589832 | tf_op jit(solution)/shard_map/ppermute | solution.py:258

commit v5 on v3

--- a/solution.py
+++ b/solution.py
@@ -164,7 +164,7 @@
 
 
 def gram_kernel(
-    place_ref, own_ref, core_ref, half_ref, both_ref, f_ref, out_ref, to_core, to_half, to_both
+    place_ref, own_ref, core_ref, half_ref, both_ref, f_ref, out_ref, to_half
 ):
     pieces, height, _ = out_ref.shape
     here, core = place_ref[2], place_ref[3]
@@ -175,8 +175,8 @@
             f_ref[at], dual[...], (((0,), (0,)), ((), ())), preferred_element_type=f32
         )
     out_ref[...] = part.T.astype(bf16).reshape(pieces, height, LANES)
-    for at, send in zip(layers[1:], (to_core, to_half, to_both)):
-        send[...] = f_ref[at]
+    first = 2 * (1 - here)
+    to_half[...] = f_ref[pl.ds(first, 2)]
 
 
 def spots(here, core):
@@ -193,14 +193,25 @@
         out_ref[k] = piece
 
 
-def rotate_kernel(scale, place_ref, f_ref, core_ref, half_ref, both_ref, g_ref, gram_ref, out_ref):
+def pick_kernel(place_ref, f_ref, half_ref, to_core):
+    here, core = place_ref[2], place_ref[3]
+    to_core[0] = f_ref[2 * here + 1 - core]
+    to_core[1] = half_ref[1 - core]
+
+
+def rotate_kernel(scale, place_ref, f_ref, half_ref, core_ref, g_ref, gram_ref, out_ref):
     blocks = out_ref.shape[1] // LANES
     pieces, height, _ = g_ref.shape
     each = pieces // blocks
     own = each // blocks
     here, core = place_ref[2], place_ref[3]
-    places = [2 * a + b for a, b in spots(here, core)]
-    cols = side_by_side([f_ref[places[0]], core_ref[...], half_ref[...], both_ref[...]])
+    places = [
+        2 * here + core,
+        2 * (1 - here) + core,
+        2 * here + 1 - core,
+        2 * (1 - here) + 1 - core,
+    ]
+    cols = side_by_side([f_ref[places[0]], half_ref[core], core_ref[0], core_ref[1]])
 
     def rows_of(k, at):
         return g_ref[pl.ds(k * each + at * own, own)].reshape(own * height, LANES)
@@ -264,15 +275,20 @@
         ],
         compiler_params=room(16), name="filter",
     )(coupling, place, v, low, high, shift_tile)
-    layer = jax.ShapeDtypeStruct((rows, width), bf16)
-    terms, to_core, to_half, to_both = pl.pallas_call(
+    two = jax.ShapeDtypeStruct((2, rows, width), bf16)
+    terms, to_half = pl.pallas_call(
         gram_kernel,
-        out_shape=(jax.ShapeDtypeStruct((near, height, LANES), bf16), layer, layer, layer),
-        in_specs=smem(1) + vmem(5), out_specs=tuple(vmem(4)), compiler_params=room(12), name="gram",
+        out_shape=(jax.ShapeDtypeStruct((near, height, LANES), bf16), two),
+        in_specs=smem(1) + vmem(5), out_specs=tuple(vmem(2)), compiler_params=room(12), name="gram",
     )(place, dual_basis, dual_core, dual_half, dual_both, own)
+    from_half = swap(to_half, HALVES)
+    pieces = spread(terms, NEAR)
+    to_core = pl.pallas_call(
+        pick_kernel,
+        out_shape=two,
+        in_specs=smem(1) + vmem(2), out_specs=vmem(1)[0], compiler_params=room(8), name="pick",
+    )(place, own, from_half)
     from_core = swap(to_core, "core")
-    from_half = swap(to_half, HALVES)
-    from_both = swap(to_both, COLS)
 
     def summed(pieces, copies):
         return pl.pallas_call(
@@ -281,9 +297,7 @@
             in_specs=vmem(1), out_specs=vmem(1)[0], compiler_params=room(8),
         )(pieces)
 
-    pieces = spread(terms, NEAR)
-    part = summed(pieces, far)
-    pieces = spread(part, FAR)
+    pieces = spread(summed(pieces, far), FAR)
     pieces = spread(summed(pieces, near * blocks), COLS + NEAR)
     gram, rotated = pl.pallas_call(
         functools.partial(rotate_kernel, cols ** (-0.5)),
@@ -291,8 +305,8 @@
             jax.ShapeDtypeStruct((cols // blocks, cols), f32),
             jax.ShapeDtypeStruct((rows, cols), bf16),
         ),
-        in_specs=smem(1) + vmem(5), out_specs=tuple(vmem(2)), compiler_params=room(12), name="rotate",
-    )(place, own, from_core, from_half, from_both, pieces)
+        in_specs=smem(1) + vmem(4), out_specs=tuple(vmem(2)), compiler_params=room(12), name="rotate",
+    )(place, own, from_half, from_core, pieces)
     return gram, rotated
 
 

time: 105 us -> 107 us (1.019)
  waiting for transfers between devices: 16 us -> 19.4 us
  starting transfers between devices: 41.5 us -> 40 us
    ppermute x6 -> x5, waiting for transfers between devices: 6.74 us -> 10.1 us  [swap(): return lax.ppermute(array, axes, [(i, many - 1 - i) for i in range(many)])]
    ppermute x6 -> x5, starting transfers between devices: 28.9 us -> 27.3 us  [swap(): return lax.ppermute(array, axes, [(i, many - 1 - i) for i in range(many)])]
  transfers between devices with their start and end apart: 9 -> 8, of which waited for: 5 -> 5; matrix products, arithmetic and copies ran while one was open for 0% -> 0% of each run, Pallas kernels for 3% -> 4%
where the time goes in v5:
time: 107 us
  starting transfers between devices  40 us (37%)
  blocking collectives  37.3 us (35%)
  waiting for transfers between devices  19.4 us (18%)
  Pallas kernels  7.59 us (7%)
  local copies, waits for them, and re-layouts  1.69 us (2%)
    all_to_all x2, blocking collectives, spread(): return lax.all_to_all(array, axes, split_axis=0, concat_axis=0, tiled=True)  37.3 us
    ppermute x5, starting transfers between devices, swap(): return lax.ppermute(array, axes, [(i, many - 1 - i) for i in range(many)])  27.3 us
    ppermute x5, waiting for transfers between devices, swap(): return lax.ppermute(array, axes, [(i, many - 1 - i) for i in range(many)])  10.1 us
    all_to_all x1, starting transfers between devices, spread(): return lax.all_to_all(array, axes, split_axis=0, concat_axis=0, tiled=True)  10.1 us
    ppermute x1, waiting for transfers between devices, shards(): low = lax.ppermute(up, NODES, [(i, i + 1) for i in range(count - 1)])  5.11 us
    ppermute x1, waiting for transfers between devices, shards(): high = lax.ppermute(down, NODES, [(i + 1, i) for i in range(count - 1)])  4.16 us
    pallas_call x1, Pallas kernels, shards(): pl.pallas_call(functools.partial(filter_kernel, gy, dofs), out_shape=jax....  3.24 us
  transfers between devices with their start and end apart: 8, of which 5 were waited for; matrix products, arithmetic and copies ran while one was open for 0% of the time, Pallas kernels for 4%

profile of v5, /device:TPU:1, one launch (start us, length us, event | category | flops | bytes accessed | tf_op | source)
XLA Modules:
  0.0 106.9 jit_solution(13012940246994661808)
XLA Ops:
  0.6 5.5 %collective-permute-start.3 = (bf16[384,512]{1,0:T(8,128)(2,1)}, bf16[384,512]{1,0:T(8,128)(2,1)S(1)}, u32[]{:S(2)}, u32[]{:S(2)}) collective-permute-start(bf16[384,512]{1,0:T(8,128)(2,1)} %own_ref.1), channel_id=1, source_target_pairs={{0,2},{2,0},{1,3},{3,1},{4,6},{6,4},{5,7},{7,5},{8,10},{10,8},{9,1... | collective-permute-start | bytes 1179656 | tf_op jit(solution)/shard_map/ppermute | solution.py:242
  6.1 5.2 %collective-permute-start.2 = (bf16[384,512]{1,0:T(8,128)(2,1)}, bf16[384,512]{1,0:T(8,128)(2,1)S(1)}, u32[]{:S(2)}, u32[]{:S(2)}) collective-permute-start(bf16[384,512]{1,0:T(8,128)(2,1)} %own_ref.1), channel_id=1, source_target_pairs={{0,1},{1,0},{2,3},{3,2},{4,5},{5,4},{6,7},{7,6},{8,9},{9,8},{10,11... | collective-permute-start | bytes 1179656 | tf_op jit(solution)/shard_map/ppermute | solution.py:242
  11.3 0.5 collective-permute-done.3.half_ref
  11.9 8.9 %collective-permute-start.4 = (bf16[384,512]{1,0:T(8,128)(2,1)S(1)}, bf16[384,512]{1,0:T(8,128)(2,1)S(1)}, u32[]{:S(2)}, u32[]{:S(2)}) collective-permute-start(bf16[384,512]{1,0:T(8,128)(2,1)S(1)} %collective-permute-done.3.half_ref), channel_id=1, source_target_pairs={{0,1},{1,0},{2,3},{3,2},{4,5},{5,4},{6,7},{7,6},{8,9},{9,8},{10,11... | collective-permute-start | bytes 1179656 | tf_op jit(solution)/shard_map/ppermute | solution.py:242
  20.8 0.0 copy-start
  20.8 1.0 copy-done
  21.8 0.0 copy-start.3
  21.8 0.7 copy-done.3
  22.5 0.1 pack.1
  22.6 1.3 %collective-permute-start = (bf16[1184,128]{1,0:T(8,128)(2,1)S(1)}, bf16[1184,128]{1,0:T(8,128)(2,1)S(1)}, u32[]{:S(2)}, u32[]{:S(2)}) collective-permute-start(bf16[1184,128]{1,0:T(8,128)(2,1)S(1)} %get-tuple-element.7), channel_id=1, source_target_pairs={{0,4},{4,8},{8,12},{12,16},{16,20},{20,24},{24,28},{28,32},{32,36}... | collective-permute-start | bytes 909320 | tf_op jit(solution)/shard_map/ppermute | solution.py:257
  23.9 1.3 %collective-permute-start.1 = (bf16[1184,128]{1,0:T(8,128)(2,1)S(1)}, bf16[1184,128]{1,0:T(8,128)(2,1)S(1)}, u32[]{:S(2)}, u32[]{:S(2)}) collective-permute-start(bf16[1184,128]{1,0:T(8,128)(2,1)S(1)} %get-tuple-element.8), channel_id=1, source_target_pairs={{4,0},{8,4},{12,8},{16,12},{20,16},{24,20},{28,24},{32,28},{36,32}... | collective-permute-start | bytes 909320 | tf_op jit(solution)/shard_map/ppermute | solution.py:258
  25.2 0.1 pad_add_fusion.place_ref
  25.3 5.1 %collective-permute-done.low_ref = bf16[1184,128]{1,0:T(8,128)(2,1)S(1)} collective-permute-done((bf16[1184,128]{1,0:T(8,128)(2,1)S(1)}, bf16[1184,128]{1,0:T(8,128)(2,1)S(1)}, u32[]{:S(2)}, u32[]{:S(2)}) %collective-permute-start) | collective-permute-done | bytes 303136 | tf_op jit(solution)/shard_map/ppermute | solution.py:257
  30.4 4.2 %collective-permute-done.1.high_ref = bf16[1184,128]{1,0:T(8,128)(2,1)S(1)} collective-permute-done((bf16[1184,128]{1,0:T(8,128)(2,1)S(1)}, bf16[1184,128]{1,0:T(8,128)(2,1)S(1)}, u32[]{:S(2)}, u32[]{:S(2)}) %collective-permute-start.1) | collective-permute-done | bytes 303136 | tf_op jit(solution)/shard_map/ppermute | solution.py:258
  34.6 0.0 copy-done.1
  34.6 0.0 copy-done.4
  34.6 3.2 %filter.1.f_ref = bf16[4,384,128]{2,1,0:T(8,128)(2,1)S(1)} custom-call(f32[4,4]{1,0:T(4,128)S(1)} %copy-done.4, s32[4]{0:T(128)S(1)} %pad_add_fusion.place_ref, bf16[4,384,128]{2,1,0:T(8,128)(2,1)S(1)} %bitcast.8, bf16[1184,128]{1,0:T(8,128)(2,1)S(1)} %collective-permute-done.low_ref, bf16[1184,128]{1,0:T(8,128)(2,1)S(1)} %collective-permute-done.1.high_ref, ...), custom_call_target="tpu_custom_call" | custom-call | tf_op jit(solution)/shard_map/filter/pallas_call | solution.py:265
  37.8 0.0 collective-permute-done.2.core_ref
  37.9 0.0 collective-permute-done.4.both_ref
  37.9 0.0 copy-done.2
  37.9 1.1 %gram.1 = (bf16[16,32,128]{2,1,0:T(8,128)(2,1)S(1)}, bf16[2,384,128]{2,1,0:T(8,128)(2,1)S(1)}) custom-call(s32[4]{0:T(128)S(1)} %pad_add_fusion.place_ref, bf16[384,512]{1,0:T(8,128)(2,1)S(1)} %copy-done.2, bf16[384,512]{1,0:T(8,128)(2,1)S(1)} %collective-permute-done.2.core_ref, bf16[384,512]{1,0:T(8,128)(2,1)S(1)} %collective-permute-done.3.half_ref, ...), custom_call_target="tpu_custom_call" | custom-call | tf_op jit(solution)/shard_map/gram/pallas_call | solution.py:279
  39.0 16.3 %all_to_all.15.in_ref = bf16[16,32,128]{2,1,0:T(8,128)(2,1)S(1)} all-to-all(bf16[16,32,128]{2,1,0:T(8,128)(2,1)S(1)} %get-tuple-element.11), channel_id=1, replica_groups=mesh['x_lo'=2,'y'=4,'z_hi'=8,'z_lo'=2,'x_hi'=2,'core'=2] {'x_lo','y','z_..., dimensions={0} | all-to-all | bytes 262144 | tf_op jit(solution)/shard_map/all_to_all | solution.py:245
  55.3 21.0 %all_to_all.16.in_ref = bf16[8,32,128]{2,1,0:T(8,128)(2,1)S(1)} all-to-all(bf16[8,32,128]{2,1,0:T(8,128)(2,1)S(1)} %shard_map.59), channel_id=1, replica_groups=mesh['x_lo'=2,'y'=4,'z_hi'=8,'z_lo'=2,'x_hi'=2,'core'=2] {'z_hi'}, dimensions={0} | all-to-all | bytes 131072 | tf_op jit(solution)/shard_map/all_to_all | solution.py:245
  76.3 0.8 shard_map.60
  77.2 10.1 %all-to-all-start.2 = ((bf16[64,32,128]{2,1,0:T(8,128)(2,1)}), bf16[64,32,128]{2,1,0:T(8,128)(2,1)S(1)}, u32[]{:S(2)}, u32[]{:S(2)}) async-start(bf16[64,32,128]{2,1,0:T(8,128)(2,1)} %shard_map.60), calls=%async_computation.2 | async-start | bytes 1048576 | tf_op jit(solution)/shard_map/all_to_all | solution.py:245
  87.3 5.0 %collective-permute-start.5 = (bf16[2,384,128]{2,1,0:T(8,128)(2,1)S(1)}, bf16[2,384,128]{2,1,0:T(8,128)(2,1)S(1)}, u32[]{:S(2)}, u32[]{:S(2)}) collective-permute-start(bf16[2,384,128]{2,1,0:T(8,128)(2,1)S(1)} %get-tuple-element.10), channel_id=1, source_target_pairs={{0,2},{2,0},{1,3},{3,1},{4,6},{6,4},{5,7},{7,5},{8,10},{10,8},{9,1... | collective-permute-start | bytes 589832 | tf_op jit(solution)/shard_map/ppermute | solution.py:242
  92.3 8.5 %collective-permute-done.5.half_ref = bf16[2,384,128]{2,1,0:T(8,128)(2,1)S(1)} collective-permute-done((bf16[2,384,128]{2,1,0:T(8,128)(2,1)S(1)}, bf16[2,384,128]{2,1,0:T(8,128)(2,1)S(1)}, u32[]{:S(2)}, u32[]{:S(2)}) %collective-permute-start.5) | collective-permute-done | bytes 196640 | tf_op jit(solution)/shard_map/ppermute | solution.py:242
  100.8 0.6 pick.1
  101.4 2.8 %collective-permute-start.6 = (bf16[2,384,128]{2,1,0:T(8,128)(2,1)S(1)}, bf16[2,384,128]{2,1,0:T(8,128)(2,1)S(1)}, u32[]{:S(2)}, u32[]{:S(2)}) collective-permute-start(bf16[2,384,128]{2,1,0:T(8,128)(2,1)S(1)} %pick.1), channel_id=1, source_target_pairs={{0,1},{1,0},{2,3},{3,2},{4,5},{5,4},{6,7},{7,6},{8,9},{9,8},{10,11... | collective-permute-start | bytes 589832 | tf_op jit(solution)/shard_map/ppermute | solution.py:242
  104.2 1.0 collective-permute-done.6.core_ref
  105.2 0.0 all-to-all-done.2.g_ref
  105.2 1.7 %rotate.1 = (f32[128,512]{1,0:T(8,128)}, bf16[384,512]{1,0:T(8,128)(2,1)}) custom-call(s32[4]{0:T(128)S(1)} %pad_add_fusion.place_ref, bf16[4,384,128]{2,1,0:T(8,128)(2,1)S(1)} %filter.1.f_ref, bf16[2,384,128]{2,1,0:T(8,128)(2,1)S(1)} %collective-permute-done.5.half_ref, bf16[2,384,128]{2,1,0:T(8,128)(2,1)S(1)} %collective-permute-done.6.core_ref, ...), custom_call_target="tpu_custom_call" | custom-call | tf_op jit(solution)/shard_map/rotate/pallas_call | solution.py:302
  (4 shorter events, 0.0 us)
Async XLA Ops:
  0.6 11.2 %collective-permute-start.3 = (bf16[384,512]{1,0:T(8,128)(2,1)}, bf16[384,512]{1,0:T(8,128)(2,1)S(1)}, u32[]{:S(2)}, u32[]{:S(2)}) collective-permute-start(bf16[384,512]{1,0:T(8,128)(2,1)} %own_ref.1), channel_id=1, source_target_pairs={{0,2},{2,0},{1,3},{3,1},{4,6},{6,4},{5,7},{7,5},{8,10},{10,8},{9,1... | collective-permute-start | bytes 1179656 | tf_op jit(solution)/shard_map/ppermute | solution.py:242
  6.1 31.7 %collective-permute-start.2 = (bf16[384,512]{1,0:T(8,128)(2,1)}, bf16[384,512]{1,0:T(8,128)(2,1)S(1)}, u32[]{:S(2)}, u32[]{:S(2)}) collective-permute-start(bf16[384,512]{1,0:T(8,128)(2,1)} %own_ref.1), channel_id=1, source_target_pairs={{0,1},{1,0},{2,3},{3,2},{4,5},{5,4},{6,7},{7,6},{8,9},{9,8},{10,11... | collective-permute-start | bytes 1179656 | tf_op jit(solution)/shard_map/ppermute | solution.py:242
  11.9 26.0 %collective-permute-start.4 = (bf16[384,512]{1,0:T(8,128)(2,1)S(1)}, bf16[384,512]{1,0:T(8,128)(2,1)S(1)}, u32[]{:S(2)}, u32[]{:S(2)}) collective-permute-start(bf16[384,512]{1,0:T(8,128)(2,1)S(1)} %collective-permute-done.3.half_ref), channel_id=1, source_target_pairs={{0,1},{1,0},{2,3},{3,2},{4,5},{5,4},{6,7},{7,6},{8,9},{9,8},{10,11... | collective-permute-start | bytes 1179656 | tf_op jit(solution)/shard_map/ppermute | solution.py:242
  20.8 1.0 copy-start
  21.8 0.7 copy-start.3
  22.4 12.1 %copy-start.1 = (bf16[4,4,6,16,128]{4,3,2,1,0:T(8,128)(2,1)S(1)}, bf16[4,4,6,16,128]{4,3,2,1,0:T(8,128)(2,1)}, u32[]{:S(2)}) copy-start(bf16[4,4,6,16,128]{4,3,2,1,0:T(8,128)(2,1)} %param.4) | copy-start | bytes 1179652
  22.6 7.8 %collective-permute-start = (bf16[1184,128]{1,0:T(8,128)(2,1)S(1)}, bf16[1184,128]{1,0:T(8,128)(2,1)S(1)}, u32[]{:S(2)}, u32[]{:S(2)}) collective-permute-start(bf16[1184,128]{1,0:T(8,128)(2,1)S(1)} %get-tuple-element.7), channel_id=1, source_target_pairs={{0,4},{4,8},{8,12},{12,16},{16,20},{20,24},{24,28},{28,32},{32,36}... | collective-permute-start | bytes 909320 | tf_op jit(solution)/shard_map/ppermute | solution.py:257
  23.9 10.7 %collective-permute-start.1 = (bf16[1184,128]{1,0:T(8,128)(2,1)S(1)}, bf16[1184,128]{1,0:T(8,128)(2,1)S(1)}, u32[]{:S(2)}, u32[]{:S(2)}) collective-permute-start(bf16[1184,128]{1,0:T(8,128)(2,1)S(1)} %get-tuple-element.8), channel_id=1, source_target_pairs={{4,0},{8,4},{12,8},{16,12},{20,16},{24,20},{28,24},{32,28},{36,32}... | collective-permute-start | bytes 909320 | tf_op jit(solution)/shard_map/ppermute | solution.py:258
  25.3 9.3 %copy-start.4 = (f32[4,4]{1,0:T(4,128)S(1)}, f32[4,4]{1,0:T(4,128)}, u32[]{:S(2)}) copy-start(f32[4,4]{1,0:T(4,128)} %coup_ref.1) | copy-start | bytes 196
  34.6 3.3 %copy-start.2 = (bf16[384,512]{1,0:T(8,128)(2,1)S(1)}, bf16[384,512]{1,0:T(8,128)(2,1)}, u32[]{:S(2)}) copy-start(bf16[384,512]{1,0:T(8,128)(2,1)} %own_ref.1) | copy-start | bytes 1179652
  77.2 28.0 %all-to-all-start.2 = ((bf16[64,32,128]{2,1,0:T(8,128)(2,1)}), bf16[64,32,128]{2,1,0:T(8,128)(2,1)S(1)}, u32[]{:S(2)}, u32[]{:S(2)}) async-start(bf16[64,32,128]{2,1,0:T(8,128)(2,1)} %shard_map.60), calls=%async_computation.2 | async-start | bytes 1048576 | tf_op jit(solution)/shard_map/all_to_all | solution.py:245
  87.3 13.5 %collective-permute-start.5 = (bf16[2,384,128]{2,1,0:T(8,128)(2,1)S(1)}, bf16[2,384,128]{2,1,0:T(8,128)(2,1)S(1)}, u32[]{:S(2)}, u32[]{:S(2)}) collective-permute-start(bf16[2,384,128]{2,1,0:T(8,128)(2,1)S(1)} %get-tuple-element.10), channel_id=1, source_target_pairs={{0,2},{2,0},{1,3},{3,1},{4,6},{6,4},{5,7},{7,5},{8,10},{10,8},{9,1... | collective-permute-start | bytes 589832 | tf_op jit(solution)/shard_map/ppermute | solution.py:242
  101.4 3.9 %collective-permute-start.6 = (bf16[2,384,128]{2,1,0:T(8,128)(2,1)S(1)}, bf16[2,384,128]{2,1,0:T(8,128)(2,1)S(1)}, u32[]{:S(2)}, u32[]{:S(2)}) collective-permute-start(bf16[2,384,128]{2,1,0:T(8,128)(2,1)S(1)} %pick.1), channel_id=1, source_target_pairs={{0,1},{1,0},{2,3},{3,2},{4,5},{5,4},{6,7},{7,6},{8,9},{9,8},{10,11... | collective-permute-start | bytes 589832 | tf_op jit(solution)/shard_map/ppermute | solution.py:242

commit v6 on v4

--- a/solution.py
+++ b/solution.py
@@ -163,20 +163,25 @@
     return jnp.concatenate(parts, axis=1)
 
 
-def gram_kernel(
-    place_ref, own_ref, core_ref, half_ref, both_ref, f_ref, out_ref, to_half
-):
-    pieces, height, _ = out_ref.shape
+def gram_kernel(place_ref, own_ref, core_ref, half_ref, f_ref, part_ref, to_half):
     here, core = place_ref[2], place_ref[3]
-    layers = [2 * a + b for a, b in spots(here, core)]
     part = 0.0
-    for at, dual in zip(layers, (own_ref, core_ref, half_ref, both_ref)):
+    for (a, b), dual in zip(spots(here, core), (own_ref, core_ref, half_ref)):
         part = part + lax.dot_general(
-            f_ref[at], dual[...], (((0,), (0,)), ((), ())), preferred_element_type=f32
+            f_ref[2 * a + b], dual[...], (((0,), (0,)), ((), ())), preferred_element_type=f32
         )
-    out_ref[...] = part.T.astype(bf16).reshape(pieces, height, LANES)
+    part_ref[...] = part
     first = 2 * (1 - here)
     to_half[...] = f_ref[pl.ds(first, 2)]
+
+
+def last_gram_kernel(place_ref, both_ref, f_ref, part_ref, out_ref):
+    pieces, height, _ = out_ref.shape
+    a, b = spots(place_ref[2], place_ref[3])[3]
+    part = part_ref[...] + lax.dot_general(
+        f_ref[2 * a + b], both_ref[...], (((0,), (0,)), ((), ())), preferred_element_type=f32
+    )
+    out_ref[...] = part.T.astype(bf16).reshape(pieces, height, LANES)
 
 
 def spots(here, core):
@@ -193,8 +198,7 @@
         out_ref[k] = piece
 
 
-def far_sum_kernel(place_ref, in_ref, f_ref, half_ref, out_ref, to_core):
-    sum_kernel(in_ref, out_ref)
+def pick_kernel(place_ref, f_ref, half_ref, to_core):
     here, core = place_ref[2], place_ref[3]
     to_core[0] = f_ref[2 * here + 1 - core]
     to_core[1] = half_ref[1 - core]
@@ -292,26 +296,35 @@
         compiler_params=room(16), name="filter",
     )(coupling, place, v, low, high, shift_tile)
     two = jax.ShapeDtypeStruct((2, rows, width), bf16)
-    terms, to_half = pl.pallas_call(
+    part, to_half = pl.pallas_call(
         gram_kernel,
-        out_shape=(jax.ShapeDtypeStruct((near, height, LANES), bf16), two),
-        in_specs=smem(1) + vmem(5), out_specs=tuple(vmem(2)), compiler_params=room(12), name="gram",
-    )(place, dual_basis, dual_core, dual_half, dual_both, own)
+        out_shape=(jax.ShapeDtypeStruct((width, cols), f32), two),
+        in_specs=smem(1) + vmem(4), out_specs=tuple(vmem(2)), compiler_params=room(12),
+        name="gram",
+    )(place, dual_basis, dual_core, dual_half, own)
+    terms = pl.pallas_call(
+        last_gram_kernel,
+        out_shape=jax.ShapeDtypeStruct((near, height, LANES), bf16),
+        in_specs=smem(1) + vmem(3), out_specs=vmem(1)[0], compiler_params=room(12), name="last_gram",
+    )(place, dual_both, own, part)
     from_half = swap(to_half, HALVES)
     pieces = spread(terms, NEAR)
-    part = pl.pallas_call(
-        sum_kernel,
-        out_shape=jax.ShapeDtypeStruct((far, height, LANES), bf16),
-        in_specs=vmem(1), out_specs=vmem(1)[0], compiler_params=room(8), name="near_sum",
-    )(pieces)
-    pieces = spread(part, FAR)
-    full, to_core = pl.pallas_call(
-        far_sum_kernel,
-        out_shape=(jax.ShapeDtypeStruct((2 * near, height, LANES), bf16), two),
-        in_specs=smem(1) + vmem(3), out_specs=tuple(vmem(2)), compiler_params=room(8), name="far_sum",
-    )(place, pieces, own, from_half)
+    to_core = pl.pallas_call(
+        pick_kernel,
+        out_shape=two,
+        in_specs=smem(1) + vmem(2), out_specs=vmem(1)[0], compiler_params=room(8), name="pick",
+    )(place, own, from_half)
     from_core = swap(to_core, "core")
-    pieces = spread(full, (HALVES,) + NEAR)
+
+    def summed(pieces, copies):
+        return pl.pallas_call(
+            sum_kernel,
+            out_shape=jax.ShapeDtypeStruct((copies, height, LANES), bf16),
+            in_specs=vmem(1), out_specs=vmem(1)[0], compiler_params=room(8),
+        )(pieces)
+
+    pieces = spread(summed(pieces, far), FAR)
+    pieces = spread(summed(pieces, 2 * near), (HALVES,) + NEAR)
     other = swap(pieces, "core")
     scale = cols ** (-0.5)
     half = pl.pallas_call(

time: 105 us -> 106 us (level)
  blocking collectives: 29.6 us -> 37.3 us
  waiting for transfers between devices: 19 us -> 14.9 us
  starting transfers between devices: 45.3 us -> 41.7 us
    all_to_all x2, blocking collectives: 29.6 us -> 37.3 us  [spread(): return lax.all_to_all(array, axes, split_axis=0, concat_axis=0, tiled=True)]
    all_to_all x1, starting transfers between devices: 9.02 us -> 5.2 us  [spread(): return lax.all_to_all(array, axes, split_axis=0, concat_axis=0, tiled=True)]
    ppermute x6, waiting for transfers between devices: 5.42 us -> 1.97 us  [swap(): return lax.ppermute(array, axes, [(i, many - 1 - i) for i in range(many)])]
    pallas_call x3 -> x5, Pallas kernels: 2.31 us -> 3.11 us  [the longest x1 0.93 us: shards(): pl.pallas_call(gram_kernel, out_shape=(jax.ShapeDtypeStruct((width, cols)...]
  transfers between devices with their start and end apart: 9 -> 9, of which waited for: 6 -> 5; matrix products, arithmetic and copies ran while one was open for 0% -> 0% of each run, Pallas kernels for 4% -> 5%
where the time goes in v6:
time: 106 us; the launch traced here: 105 us
  starting transfers between devices  41.7 us (39%)
  blocking collectives  37.3 us (35%)
  waiting for transfers between devices  14.9 us (14%)
  Pallas kernels  8.93 us (8%)
  local copies, waits for them, and re-layouts  1.69 us (2%)
    all_to_all x2, blocking collectives, spread(): return lax.all_to_all(array, axes, split_axis=0, concat_axis=0, tiled=True)  37.3 us
    ppermute x6, starting transfers between devices, swap(): return lax.ppermute(array, axes, [(i, many - 1 - i) for i in range(many)])  33.9 us
    all_to_all x1, starting transfers between devices, spread(): return lax.all_to_all(array, axes, split_axis=0, concat_axis=0, tiled=True)  5.2 us
    ppermute x1, waiting for transfers between devices, shards(): low = lax.ppermute(up, NODES, [(i, i + 1) for i in range(count - 1)])  5.11 us
    ppermute x1, waiting for transfers between devices, shards(): high = lax.ppermute(down, NODES, [(i + 1, i) for i in range(count - 1)])  4.16 us
    all_to_all x1, waiting for transfers between devices, spread(): return lax.all_to_all(array, axes, split_axis=0, concat_axis=0, tiled=True)  3.63 us
    pallas_call x1, Pallas kernels, shards(): pl.pallas_call(functools.partial(filter_kernel, gy, dofs), out_shape=jax....  3.24 us
  transfers between devices with their start and end apart: 9, of which 5 were waited for; matrix products, arithmetic and copies ran while one was open for 0% of the time, Pallas kernels for 5%

profile of v6, /device:TPU:1, one launch (start us, length us, event | category | flops | bytes accessed | tf_op | source)
XLA Modules:
  0.0 105.4 jit_solution(16542941382656774571)
XLA Ops:
  0.6 5.5 %collective-permute-start.3 = (bf16[384,512]{1,0:T(8,128)(2,1)}, bf16[384,512]{1,0:T(8,128)(2,1)S(1)}, u32[]{:S(2)}, u32[]{:S(2)}) collective-permute-start(bf16[384,512]{1,0:T(8,128)(2,1)} %own_ref.1), channel_id=1, source_target_pairs={{0,2},{2,0},{1,3},{3,1},{4,6},{6,4},{5,7},{7,5},{8,10},{10,8},{9,1... | collective-permute-start | bytes 1179656 | tf_op jit(solution)/shard_map/ppermute | solution.py:262
  6.1 5.2 %collective-permute-start.2 = (bf16[384,512]{1,0:T(8,128)(2,1)}, bf16[384,512]{1,0:T(8,128)(2,1)S(1)}, u32[]{:S(2)}, u32[]{:S(2)}) collective-permute-start(bf16[384,512]{1,0:T(8,128)(2,1)} %own_ref.1), channel_id=1, source_target_pairs={{0,1},{1,0},{2,3},{3,2},{4,5},{5,4},{6,7},{7,6},{8,9},{9,8},{10,11... | collective-permute-start | bytes 1179656 | tf_op jit(solution)/shard_map/ppermute | solution.py:262
  11.3 0.5 collective-permute-done.3.half_ref
  11.9 8.9 %collective-permute-start.6 = (bf16[384,512]{1,0:T(8,128)(2,1)S(1)}, bf16[384,512]{1,0:T(8,128)(2,1)S(1)}, u32[]{:S(2)}, u32[]{:S(2)}) collective-permute-start(bf16[384,512]{1,0:T(8,128)(2,1)S(1)} %collective-permute-done.3.half_ref), channel_id=1, source_target_pairs={{0,1},{1,0},{2,3},{3,2},{4,5},{5,4},{6,7},{7,6},{8,9},{9,8},{10,11... | collective-permute-start | bytes 1179656 | tf_op jit(solution)/shard_map/ppermute | solution.py:262
  20.8 0.0 copy-start
  20.8 1.0 copy-done
  21.8 0.7 copy-done.3
  22.5 0.1 pack.1
  22.6 1.3 %collective-permute-start = (bf16[1184,128]{1,0:T(8,128)(2,1)S(1)}, bf16[1184,128]{1,0:T(8,128)(2,1)S(1)}, u32[]{:S(2)}, u32[]{:S(2)}) collective-permute-start(bf16[1184,128]{1,0:T(8,128)(2,1)S(1)} %get-tuple-element.7), channel_id=1, source_target_pairs={{0,4},{4,8},{8,12},{12,16},{16,20},{20,24},{24,28},{28,32},{32,36}... | collective-permute-start | bytes 909320 | tf_op jit(solution)/shard_map/ppermute | solution.py:277
  23.9 1.3 %collective-permute-start.1 = (bf16[1184,128]{1,0:T(8,128)(2,1)S(1)}, bf16[1184,128]{1,0:T(8,128)(2,1)S(1)}, u32[]{:S(2)}, u32[]{:S(2)}) collective-permute-start(bf16[1184,128]{1,0:T(8,128)(2,1)S(1)} %get-tuple-element.8), channel_id=1, source_target_pairs={{4,0},{8,4},{12,8},{16,12},{20,16},{24,20},{28,24},{32,28},{36,32}... | collective-permute-start | bytes 909320 | tf_op jit(solution)/shard_map/ppermute | solution.py:278
  25.2 0.1 pad_add_fusion.place_ref
  25.3 5.1 %collective-permute-done.low_ref = bf16[1184,128]{1,0:T(8,128)(2,1)S(1)} collective-permute-done((bf16[1184,128]{1,0:T(8,128)(2,1)S(1)}, bf16[1184,128]{1,0:T(8,128)(2,1)S(1)}, u32[]{:S(2)}, u32[]{:S(2)}) %collective-permute-start) | collective-permute-done | bytes 303136 | tf_op jit(solution)/shard_map/ppermute | solution.py:277
  30.4 4.2 %collective-permute-done.1.high_ref = bf16[1184,128]{1,0:T(8,128)(2,1)S(1)} collective-permute-done((bf16[1184,128]{1,0:T(8,128)(2,1)S(1)}, bf16[1184,128]{1,0:T(8,128)(2,1)S(1)}, u32[]{:S(2)}, u32[]{:S(2)}) %collective-permute-start.1) | collective-permute-done | bytes 303136 | tf_op jit(solution)/shard_map/ppermute | solution.py:278
  34.6 3.2 %filter.1.f_ref = bf16[4,384,128]{2,1,0:T(8,128)(2,1)S(1)} custom-call(f32[4,4]{1,0:T(4,128)S(1)} %copy-done.4, s32[4]{0:T(128)S(1)} %pad_add_fusion.place_ref, bf16[4,384,128]{2,1,0:T(8,128)(2,1)S(1)} %bitcast.8, bf16[1184,128]{1,0:T(8,128)(2,1)S(1)} %collective-permute-done.low_ref, bf16[1184,128]{1,0:T(8,128)(2,1)S(1)} %collective-permute-done.1.high_ref, ...), custom_call_target="tpu_custom_call" | custom-call | tf_op jit(solution)/shard_map/filter/pallas_call | solution.py:285
  37.8 0.0 collective-permute-done.2.core_ref
  37.9 0.9 gram.1
  38.8 0.0 collective-permute-done.6.both_ref
  38.8 0.9 last_gram.1
  39.7 16.3 %all_to_all.15.in_ref = bf16[16,32,128]{2,1,0:T(8,128)(2,1)S(1)} all-to-all(bf16[16,32,128]{2,1,0:T(8,128)(2,1)S(1)} %last_gram.1), channel_id=1, replica_groups=mesh['x_lo'=2,'y'=4,'z_hi'=8,'z_lo'=2,'x_hi'=2,'core'=2] {'x_lo','y','z_..., dimensions={0} | all-to-all | bytes 262144 | tf_op jit(solution)/shard_map/all_to_all | solution.py:265
  56.0 21.0 %all_to_all.16.in_ref = bf16[8,32,128]{2,1,0:T(8,128)(2,1)S(1)} all-to-all(bf16[8,32,128]{2,1,0:T(8,128)(2,1)S(1)} %shard_map.59), channel_id=1, replica_groups=mesh['x_lo'=2,'y'=4,'z_hi'=8,'z_lo'=2,'x_hi'=2,'core'=2] {'z_hi'}, dimensions={0} | all-to-all | bytes 131072 | tf_op jit(solution)/shard_map/all_to_all | solution.py:265
  77.1 0.7 shard_map.60
  77.8 5.2 %all-to-all-start.2 = ((bf16[32,32,128]{2,1,0:T(8,128)(2,1)}), bf16[32,32,128]{2,1,0:T(8,128)(2,1)S(1)}, u32[]{:S(2)}, u32[]{:S(2)}) async-start(bf16[32,32,128]{2,1,0:T(8,128)(2,1)} %shard_map.60), calls=%async_computation.2 | async-start | bytes 524288 | tf_op jit(solution)/shard_map/all_to_all | solution.py:265
  83.0 4.7 %collective-permute-start.4 = (bf16[2,384,128]{2,1,0:T(8,128)(2,1)S(1)}, bf16[2,384,128]{2,1,0:T(8,128)(2,1)S(1)}, u32[]{:S(2)}, u32[]{:S(2)}) collective-permute-start(bf16[2,384,128]{2,1,0:T(8,128)(2,1)S(1)} %get-tuple-element.10), channel_id=1, source_target_pairs={{0,2},{2,0},{1,3},{3,1},{4,6},{6,4},{5,7},{7,5},{8,10},{10,8},{9,1... | collective-permute-start | bytes 589832 | tf_op jit(solution)/shard_map/ppermute | solution.py:262
  87.7 3.6 %all-to-all-done.2.g_ref = bf16[32,32,128]{2,1,0:T(8,128)(2,1)S(1)} async-done(((bf16[32,32,128]{2,1,0:T(8,128)(2,1)}), bf16[32,32,128]{2,1,0:T(8,128)(2,1)S(1)}, u32[]{:S(2)}, u32[]{:S(2)}) %all-to-all-start.2) | async-done | bytes 262176 | tf_op jit(solution)/shard_map/all_to_all | solution.py:265
  91.3 7.8 %collective-permute-start.7 = (bf16[32,32,128]{2,1,0:T(8,128)(2,1)S(1)}, bf16[32,32,128]{2,1,0:T(8,128)(2,1)S(1)}, u32[]{:S(2)}, u32[]{:S(2)}) collective-permute-start(bf16[32,32,128]{2,1,0:T(8,128)(2,1)S(1)} %all-to-all-done.2.g_ref), channel_id=1, source_target_pairs={{0,1},{1,0},{2,3},{3,2},{4,5},{5,4},{6,7},{7,6},{8,9},{9,8},{10,11... | collective-permute-start | bytes 786440 | tf_op jit(solution)/shard_map/ppermute | solution.py:262
  99.1 0.0 collective-permute-done.4.half_ref
  99.1 0.6 pick.1
  99.7 1.9 %collective-permute-start.5 = (bf16[2,384,128]{2,1,0:T(8,128)(2,1)S(1)}, bf16[2,384,128]{2,1,0:T(8,128)(2,1)S(1)}, u32[]{:S(2)}, u32[]{:S(2)}) collective-permute-start(bf16[2,384,128]{2,1,0:T(8,128)(2,1)S(1)} %pick.1), channel_id=1, source_target_pairs={{0,1},{1,0},{2,3},{3,2},{4,5},{5,4},{6,7},{7,6},{8,9},{9,8},{10,11... | collective-permute-start | bytes 589832 | tf_op jit(solution)/shard_map/ppermute | solution.py:262
  101.6 1.4 %collective-permute-done.5.core_ref = bf16[2,384,128]{2,1,0:T(8,128)(2,1)S(1)} collective-permute-done((bf16[2,384,128]{2,1,0:T(8,128)(2,1)S(1)}, bf16[2,384,128]{2,1,0:T(8,128)(2,1)S(1)}, u32[]{:S(2)}, u32[]{:S(2)}) %collective-permute-start.5) | collective-permute-done | bytes 196640 | tf_op jit(solution)/shard_map/ppermute | solution.py:262
  103.0 0.8 rotate_half.1.done_ref
  103.8 0.0 collective-permute-done.7.far_ref
  103.8 1.6 %rotate.1 = (f32[128,512]{1,0:T(8,128)}, bf16[384,512]{1,0:T(8,128)(2,1)}) custom-call(s32[4]{0:T(128)S(1)} %pad_add_fusion.place_ref, bf16[4,384,128]{2,1,0:T(8,128)(2,1)S(1)} %filter.1.f_ref, bf16[2,384,128]{2,1,0:T(8,128)(2,1)S(1)} %collective-permute-done.4.half_ref, bf16[2,384,128]{2,1,0:T(8,128)(2,1)S(1)} %collective-permute-done.5.core_ref, ...), custom_call_target="tpu_custom_call" | custom-call | tf_op jit(solution)/shard_map/rotate/pallas_call | solution.py:336
  (8 shorter events, 0.0 us)
Async XLA Ops:
  0.6 11.2 %collective-permute-start.3 = (bf16[384,512]{1,0:T(8,128)(2,1)}, bf16[384,512]{1,0:T(8,128)(2,1)S(1)}, u32[]{:S(2)}, u32[]{:S(2)}) collective-permute-start(bf16[384,512]{1,0:T(8,128)(2,1)} %own_ref.1), channel_id=1, source_target_pairs={{0,2},{2,0},{1,3},{3,1},{4,6},{6,4},{5,7},{7,5},{8,10},{10,8},{9,1... | collective-permute-start | bytes 1179656 | tf_op jit(solution)/shard_map/ppermute | solution.py:262
  6.1 31.7 %collective-permute-start.2 = (bf16[384,512]{1,0:T(8,128)(2,1)}, bf16[384,512]{1,0:T(8,128)(2,1)S(1)}, u32[]{:S(2)}, u32[]{:S(2)}) collective-permute-start(bf16[384,512]{1,0:T(8,128)(2,1)} %own_ref.1), channel_id=1, source_target_pairs={{0,1},{1,0},{2,3},{3,2},{4,5},{5,4},{6,7},{7,6},{8,9},{9,8},{10,11... | collective-permute-start | bytes 1179656 | tf_op jit(solution)/shard_map/ppermute | solution.py:262
  11.9 26.9 %collective-permute-start.6 = (bf16[384,512]{1,0:T(8,128)(2,1)S(1)}, bf16[384,512]{1,0:T(8,128)(2,1)S(1)}, u32[]{:S(2)}, u32[]{:S(2)}) collective-permute-start(bf16[384,512]{1,0:T(8,128)(2,1)S(1)} %collective-permute-done.3.half_ref), channel_id=1, source_target_pairs={{0,1},{1,0},{2,3},{3,2},{4,5},{5,4},{6,7},{7,6},{8,9},{9,8},{10,11... | collective-permute-start | bytes 1179656 | tf_op jit(solution)/shard_map/ppermute | solution.py:262
  20.8 1.0 copy-start
  21.8 0.7 copy-start.3
  22.4 12.1 %copy-start.1 = (bf16[4,4,6,16,128]{4,3,2,1,0:T(8,128)(2,1)S(1)}, bf16[4,4,6,16,128]{4,3,2,1,0:T(8,128)(2,1)}, u32[]{:S(2)}) copy-start(bf16[4,4,6,16,128]{4,3,2,1,0:T(8,128)(2,1)} %param.4) | copy-start | bytes 1179652
  22.6 7.8 %collective-permute-start = (bf16[1184,128]{1,0:T(8,128)(2,1)S(1)}, bf16[1184,128]{1,0:T(8,128)(2,1)S(1)}, u32[]{:S(2)}, u32[]{:S(2)}) collective-permute-start(bf16[1184,128]{1,0:T(8,128)(2,1)S(1)} %get-tuple-element.7), channel_id=1, source_target_pairs={{0,4},{4,8},{8,12},{12,16},{16,20},{20,24},{24,28},{28,32},{32,36}... | collective-permute-start | bytes 909320 | tf_op jit(solution)/shard_map/ppermute | solution.py:277
  23.9 10.7 %collective-permute-start.1 = (bf16[1184,128]{1,0:T(8,128)(2,1)S(1)}, bf16[1184,128]{1,0:T(8,128)(2,1)S(1)}, u32[]{:S(2)}, u32[]{:S(2)}) collective-permute-start(bf16[1184,128]{1,0:T(8,128)(2,1)S(1)} %get-tuple-element.8), channel_id=1, source_target_pairs={{4,0},{8,4},{12,8},{16,12},{20,16},{24,20},{28,24},{32,28},{36,32}... | collective-permute-start | bytes 909320 | tf_op jit(solution)/shard_map/ppermute | solution.py:278
  25.3 9.3 %copy-start.4 = (f32[4,4]{1,0:T(4,128)S(1)}, f32[4,4]{1,0:T(4,128)}, u32[]{:S(2)}) copy-start(f32[4,4]{1,0:T(4,128)} %coup_ref.1) | copy-start | bytes 196
  34.6 3.3 %copy-start.2 = (bf16[384,512]{1,0:T(8,128)(2,1)S(1)}, bf16[384,512]{1,0:T(8,128)(2,1)}, u32[]{:S(2)}) copy-start(bf16[384,512]{1,0:T(8,128)(2,1)} %own_ref.1) | copy-start | bytes 1179652
  77.8 13.5 %all-to-all-start.2 = ((bf16[32,32,128]{2,1,0:T(8,128)(2,1)}), bf16[32,32,128]{2,1,0:T(8,128)(2,1)S(1)}, u32[]{:S(2)}, u32[]{:S(2)}) async-start(bf16[32,32,128]{2,1,0:T(8,128)(2,1)} %shard_map.60), calls=%async_computation.2 | async-start | bytes 524288 | tf_op jit(solution)/shard_map/all_to_all | solution.py:265
  83.0 16.1 %collective-permute-start.4 = (bf16[2,384,128]{2,1,0:T(8,128)(2,1)S(1)}, bf16[2,384,128]{2,1,0:T(8,128)(2,1)S(1)}, u32[]{:S(2)}, u32[]{:S(2)}) collective-permute-start(bf16[2,384,128]{2,1,0:T(8,128)(2,1)S(1)} %get-tuple-element.10), channel_id=1, source_target_pairs={{0,2},{2,0},{1,3},{3,1},{4,6},{6,4},{5,7},{7,5},{8,10},{10,8},{9,1... | collective-permute-start | bytes 589832 | tf_op jit(solution)/shard_map/ppermute | solution.py:262
  91.3 12.5 %collective-permute-start.7 = (bf16[32,32,128]{2,1,0:T(8,128)(2,1)S(1)}, bf16[32,32,128]{2,1,0:T(8,128)(2,1)S(1)}, u32[]{:S(2)}, u32[]{:S(2)}) collective-permute-start(bf16[32,32,128]{2,1,0:T(8,128)(2,1)S(1)} %all-to-all-done.2.g_ref), channel_id=1, source_target_pairs={{0,1},{1,0},{2,3},{3,2},{4,5},{5,4},{6,7},{7,6},{8,9},{9,8},{10,11... | collective-permute-start | bytes 786440 | tf_op jit(solution)/shard_map/ppermute | solution.py:262
  99.7 3.3 %collective-permute-start.5 = (bf16[2,384,128]{2,1,0:T(8,128)(2,1)S(1)}, bf16[2,384,128]{2,1,0:T(8,128)(2,1)S(1)}, u32[]{:S(2)}, u32[]{:S(2)}) collective-permute-start(bf16[2,384,128]{2,1,0:T(8,128)(2,1)S(1)} %pick.1), channel_id=1, source_target_pairs={{0,1},{1,0},{2,3},{3,2},{4,5},{5,4},{6,7},{7,6},{8,9},{9,8},{10,11... | collective-permute-start | bytes 589832 | tf_op jit(solution)/shard_map/ppermute | solution.py:262

commit v7 on v4

--- a/solution.py
+++ b/solution.py
@@ -193,8 +193,7 @@
         out_ref[k] = piece
 
 
-def far_sum_kernel(place_ref, in_ref, f_ref, half_ref, out_ref, to_core):
-    sum_kernel(in_ref, out_ref)
+def pick_kernel(place_ref, f_ref, half_ref, to_core):
     here, core = place_ref[2], place_ref[3]
     to_core[0] = f_ref[2 * here + 1 - core]
     to_core[1] = half_ref[1 - core]
@@ -268,7 +267,7 @@
         out_shape=(message, message, jax.ShapeDtypeStruct((SHIFT_ROWS, width), bf16)),
         in_specs=[pl.BlockSpec(memory_space=pltpu.HBM)] + vmem(1), out_specs=tuple(vmem(3)),
         scratch_shapes=[pltpu.VMEM((SHIFT_ROWS, width), f32), pltpu.SemaphoreType.DMA((2,))],
-        compiler_params=room(8), name="pack",
+        compiler_params=room(60), name="pack",
     )(vectors.reshape(layers * rows, width), node_shift.transpose(1, 0, 2))
     low = lax.ppermute(up, NODES, [(i, i + 1) for i in range(count - 1)])
     high = lax.ppermute(down, NODES, [(i + 1, i) for i in range(count - 1)])
@@ -299,19 +298,22 @@
     )(place, dual_basis, dual_core, dual_half, dual_both, own)
     from_half = swap(to_half, HALVES)
     pieces = spread(terms, NEAR)
-    part = pl.pallas_call(
-        sum_kernel,
-        out_shape=jax.ShapeDtypeStruct((far, height, LANES), bf16),
-        in_specs=vmem(1), out_specs=vmem(1)[0], compiler_params=room(8), name="near_sum",
-    )(pieces)
-    pieces = spread(part, FAR)
-    full, to_core = pl.pallas_call(
-        far_sum_kernel,
-        out_shape=(jax.ShapeDtypeStruct((2 * near, height, LANES), bf16), two),
-        in_specs=smem(1) + vmem(3), out_specs=tuple(vmem(2)), compiler_params=room(8), name="far_sum",
-    )(place, pieces, own, from_half)
+    to_core = pl.pallas_call(
+        pick_kernel,
+        out_shape=two,
+        in_specs=smem(1) + vmem(2), out_specs=vmem(1)[0], compiler_params=room(8), name="pick",
+    )(place, own, from_half)
     from_core = swap(to_core, "core")
-    pieces = spread(full, (HALVES,) + NEAR)
+
+    def summed(pieces, copies):
+        return pl.pallas_call(
+            sum_kernel,
+            out_shape=jax.ShapeDtypeStruct((copies, height, LANES), bf16),
+            in_specs=vmem(1), out_specs=vmem(1)[0], compiler_params=room(8),
+        )(pieces)
+
+    pieces = spread(summed(pieces, far), FAR)
+    pieces = spread(summed(pieces, 2 * near), (HALVES,) + NEAR)
     other = swap(pieces, "core")
     scale = cols ** (-0.5)
     half = pl.pallas_call(

time: 105 us -> 106 us (level)
  blocking collectives: 29.6 us -> 37.4 us
  waiting for transfers between devices: 19 us -> 15.1 us
  starting transfers between devices: 45.3 us -> 41.7 us
  Pallas kernels: 8.13 us -> 10.6 us
  local copies, waits for them, and re-layouts: 1.69 us -> 0.02 us
    all_to_all x2, blocking collectives: 29.6 us -> 37.4 us  [spread(): return lax.all_to_all(array, axes, split_axis=0, concat_axis=0, tiled=True)]
    all_to_all x1, starting transfers between devices: 9.02 us -> 5.2 us  [spread(): return lax.all_to_all(array, axes, split_axis=0, concat_axis=0, tiled=True)]
    ppermute x6, waiting for transfers between devices: 5.42 us -> 1.97 us  [swap(): return lax.ppermute(array, axes, [(i, many - 1 - i) for i in range(many)])]
    pallas_call x1, Pallas kernels: 0.15 us -> 2.58 us  [shards(): pl.pallas_call(functools.partial(pack_kernel, rows), out_shape=(message,...]
    unnamed x10 -> x8, local copies, waits for them, and re-layouts: 1.69 us -> 0.02 us
  transfers between devices with their start and end apart: 9 -> 9, of which waited for: 6 -> 5; matrix products, arithmetic and copies ran while one was open for 0% -> 0% of each run, Pallas kernels for 4% -> 7%
where the time goes in v7:
time: 106 us
  starting transfers between devices  41.7 us (39%)
  blocking collectives  37.4 us (35%)
  waiting for transfers between devices  15.1 us (14%)
  Pallas kernels  10.6 us (10%)
    all_to_all x2, blocking collectives, spread(): return lax.all_to_all(array, axes, split_axis=0, concat_axis=0, tiled=True)  37.4 us
    ppermute x6, starting transfers between devices, swap(): return lax.ppermute(array, axes, [(i, many - 1 - i) for i in range(many)])  33.9 us
    ppermute x1, waiting for transfers between devices, shards(): low = lax.ppermute(up, NODES, [(i, i + 1) for i in range(count - 1)])  5.41 us
    all_to_all x1, starting transfers between devices, spread(): return lax.all_to_all(array, axes, split_axis=0, concat_axis=0, tiled=True)  5.2 us
    ppermute x1, waiting for transfers between devices, shards(): high = lax.ppermute(down, NODES, [(i + 1, i) for i in range(count - 1)])  4.05 us
    all_to_all x1, waiting for transfers between devices, spread(): return lax.all_to_all(array, axes, split_axis=0, concat_axis=0, tiled=True)  3.63 us
    pallas_call x1, Pallas kernels, shards(): pl.pallas_call(functools.partial(filter_kernel, gy, dofs), out_shape=jax....  3.25 us
    pallas_call x1, Pallas kernels, shards(): pl.pallas_call(functools.partial(pack_kernel, rows), out_shape=(message,...  2.58 us
  transfers between devices with their start and end apart: 9, of which 5 were waited for; matrix products, arithmetic and copies ran while one was open for 0% of the time, Pallas kernels for 7%

profile of v7, /device:TPU:1, one launch (start us, length us, event | category | flops | bytes accessed | tf_op | source)
XLA Modules:
  0.0 105.8 jit_solution(13410826890774286120)
XLA Ops:
  0.6 0.0 copy-start
  0.6 5.6 %collective-permute-start.3 = (bf16[384,512]{1,0:T(8,128)(2,1)}, bf16[384,512]{1,0:T(8,128)(2,1)S(1)}, u32[]{:S(2)}, u32[]{:S(2)}) collective-permute-start(bf16[384,512]{1,0:T(8,128)(2,1)} %own_ref.1), channel_id=1, source_target_pairs={{0,2},{2,0},{1,3},{3,1},{4,6},{6,4},{5,7},{7,5},{8,10},{10,8},{9,1... | collective-permute-start | bytes 1179656 | tf_op jit(solution)/shard_map/ppermute | solution.py:257
  6.3 5.2 %collective-permute-start.2 = (bf16[384,512]{1,0:T(8,128)(2,1)}, bf16[384,512]{1,0:T(8,128)(2,1)S(1)}, u32[]{:S(2)}, u32[]{:S(2)}) collective-permute-start(bf16[384,512]{1,0:T(8,128)(2,1)} %own_ref.1), channel_id=1, source_target_pairs={{0,1},{1,0},{2,3},{3,2},{4,5},{5,4},{6,7},{7,6},{8,9},{9,8},{10,11... | collective-permute-start | bytes 1179656 | tf_op jit(solution)/shard_map/ppermute | solution.py:257
  11.5 0.5 collective-permute-done.3.half_ref
  12.0 8.9 %collective-permute-start.4 = (bf16[384,512]{1,0:T(8,128)(2,1)S(1)}, bf16[384,512]{1,0:T(8,128)(2,1)S(1)}, u32[]{:S(2)}, u32[]{:S(2)}) collective-permute-start(bf16[384,512]{1,0:T(8,128)(2,1)S(1)} %collective-permute-done.3.half_ref), channel_id=1, source_target_pairs={{0,1},{1,0},{2,3},{3,2},{4,5},{5,4},{6,7},{7,6},{8,9},{9,8},{10,11... | collective-permute-start | bytes 1179656 | tf_op jit(solution)/shard_map/ppermute | solution.py:257
  20.9 2.6 %pack.1 = (bf16[1184,128]{1,0:T(8,128)(2,1)}, bf16[1184,128]{1,0:T(8,128)(2,1)}, bf16[32,128]{1,0:T(8,128)(2,1)}) custom-call(bf16[1536,128]{1,0:T(8,128)(2,1)} %bitcast.7, bf16[6,4,16]{2,1,0:T(4,128)(2,1)} %bitcast.9), custom_call_target="tpu_custom_call" | custom-call | tf_op jit(solution)/shard_map/pack/pallas_call | solution.py:265
  23.5 1.3 %collective-permute-start = (bf16[1184,128]{1,0:T(8,128)(2,1)}, bf16[1184,128]{1,0:T(8,128)(2,1)S(1)}, u32[]{:S(2)}, u32[]{:S(2)}) collective-permute-start(bf16[1184,128]{1,0:T(8,128)(2,1)} %get-tuple-element.7), channel_id=1, source_target_pairs={{0,4},{4,8},{8,12},{12,16},{16,20},{20,24},{24,28},{28,32},{32,36}... | collective-permute-start | bytes 909320 | tf_op jit(solution)/shard_map/ppermute | solution.py:272
  24.8 1.3 %collective-permute-start.1 = (bf16[1184,128]{1,0:T(8,128)(2,1)}, bf16[1184,128]{1,0:T(8,128)(2,1)S(1)}, u32[]{:S(2)}, u32[]{:S(2)}) collective-permute-start(bf16[1184,128]{1,0:T(8,128)(2,1)} %get-tuple-element.8), channel_id=1, source_target_pairs={{4,0},{8,4},{12,8},{16,12},{20,16},{24,20},{28,24},{32,28},{36,32}... | collective-permute-start | bytes 909320 | tf_op jit(solution)/shard_map/ppermute | solution.py:273
  26.1 0.0 copy-start.2
  26.1 0.1 pad_add_fusion.place_ref
  26.2 5.4 %collective-permute-done.low_ref = bf16[1184,128]{1,0:T(8,128)(2,1)S(1)} collective-permute-done((bf16[1184,128]{1,0:T(8,128)(2,1)}, bf16[1184,128]{1,0:T(8,128)(2,1)S(1)}, u32[]{:S(2)}, u32[]{:S(2)}) %collective-permute-start) | collective-permute-done | bytes 303136 | tf_op jit(solution)/shard_map/ppermute | solution.py:272
  31.6 4.1 %collective-permute-done.1.high_ref = bf16[1184,128]{1,0:T(8,128)(2,1)S(1)} collective-permute-done((bf16[1184,128]{1,0:T(8,128)(2,1)}, bf16[1184,128]{1,0:T(8,128)(2,1)S(1)}, u32[]{:S(2)}, u32[]{:S(2)}) %collective-permute-start.1) | collective-permute-done | bytes 303136 | tf_op jit(solution)/shard_map/ppermute | solution.py:273
  35.7 0.0 copy-done.2
  35.7 0.0 copy-start.1
  35.7 3.2 %filter.1.f_ref = bf16[4,384,128]{2,1,0:T(8,128)(2,1)S(1)} custom-call(f32[4,4]{1,0:T(4,128)S(1)} %copy-done.3, s32[4]{0:T(128)S(1)} %pad_add_fusion.place_ref, bf16[4,384,128]{2,1,0:T(8,128)(2,1)S(1)} %bitcast.8, bf16[1184,128]{1,0:T(8,128)(2,1)S(1)} %collective-permute-done.low_ref, bf16[1184,128]{1,0:T(8,128)(2,1)S(1)} %collective-permute-done.1.high_ref, ...), custom_call_target="tpu_custom_call" | custom-call | tf_op jit(solution)/shard_map/filter/pallas_call | solution.py:280
  39.0 0.0 collective-permute-done.2.core_ref
  39.0 0.0 collective-permute-done.4.both_ref
  39.0 1.1 %gram.1 = (bf16[16,32,128]{2,1,0:T(8,128)(2,1)S(1)}, bf16[2,384,128]{2,1,0:T(8,128)(2,1)S(1)}) custom-call(s32[4]{0:T(128)S(1)} %pad_add_fusion.place_ref, bf16[384,512]{1,0:T(8,128)(2,1)S(1)} %copy-done.1, bf16[384,512]{1,0:T(8,128)(2,1)S(1)} %collective-permute-done.2.core_ref, bf16[384,512]{1,0:T(8,128)(2,1)S(1)} %collective-permute-done.3.half_ref, ...), custom_call_target="tpu_custom_call" | custom-call | tf_op jit(solution)/shard_map/gram/pallas_call | solution.py:294
  40.1 16.4 %all_to_all.15.in_ref = bf16[16,32,128]{2,1,0:T(8,128)(2,1)S(1)} all-to-all(bf16[16,32,128]{2,1,0:T(8,128)(2,1)S(1)} %get-tuple-element.11), channel_id=1, replica_groups=mesh['x_lo'=2,'y'=4,'z_hi'=8,'z_lo'=2,'x_hi'=2,'core'=2] {'x_lo','y','z_..., dimensions={0} | all-to-all | bytes 262144 | tf_op jit(solution)/shard_map/all_to_all | solution.py:260
  56.5 21.0 %all_to_all.16.in_ref = bf16[8,32,128]{2,1,0:T(8,128)(2,1)S(1)} all-to-all(bf16[8,32,128]{2,1,0:T(8,128)(2,1)S(1)} %shard_map.59), channel_id=1, replica_groups=mesh['x_lo'=2,'y'=4,'z_hi'=8,'z_lo'=2,'x_hi'=2,'core'=2] {'z_hi'}, dimensions={0} | all-to-all | bytes 131072 | tf_op jit(solution)/shard_map/all_to_all | solution.py:260
  77.5 0.7 shard_map.60
  78.3 5.2 %all-to-all-start.2 = ((bf16[32,32,128]{2,1,0:T(8,128)(2,1)}), bf16[32,32,128]{2,1,0:T(8,128)(2,1)S(1)}, u32[]{:S(2)}, u32[]{:S(2)}) async-start(bf16[32,32,128]{2,1,0:T(8,128)(2,1)} %shard_map.60), calls=%async_computation.2 | async-start | bytes 524288 | tf_op jit(solution)/shard_map/all_to_all | solution.py:260
  83.5 4.7 %collective-permute-start.5 = (bf16[2,384,128]{2,1,0:T(8,128)(2,1)S(1)}, bf16[2,384,128]{2,1,0:T(8,128)(2,1)S(1)}, u32[]{:S(2)}, u32[]{:S(2)}) collective-permute-start(bf16[2,384,128]{2,1,0:T(8,128)(2,1)S(1)} %get-tuple-element.10), channel_id=1, source_target_pairs={{0,2},{2,0},{1,3},{3,1},{4,6},{6,4},{5,7},{7,5},{8,10},{10,8},{9,1... | collective-permute-start | bytes 589832 | tf_op jit(solution)/shard_map/ppermute | solution.py:257
  88.1 3.6 %all-to-all-done.2.g_ref = bf16[32,32,128]{2,1,0:T(8,128)(2,1)S(1)} async-done(((bf16[32,32,128]{2,1,0:T(8,128)(2,1)}), bf16[32,32,128]{2,1,0:T(8,128)(2,1)S(1)}, u32[]{:S(2)}, u32[]{:S(2)}) %all-to-all-start.2) | async-done | bytes 262176 | tf_op jit(solution)/shard_map/all_to_all | solution.py:260
  91.8 7.7 %collective-permute-start.7 = (bf16[32,32,128]{2,1,0:T(8,128)(2,1)S(1)}, bf16[32,32,128]{2,1,0:T(8,128)(2,1)S(1)}, u32[]{:S(2)}, u32[]{:S(2)}) collective-permute-start(bf16[32,32,128]{2,1,0:T(8,128)(2,1)S(1)} %all-to-all-done.2.g_ref), channel_id=1, source_target_pairs={{0,1},{1,0},{2,3},{3,2},{4,5},{5,4},{6,7},{7,6},{8,9},{9,8},{10,11... | collective-permute-start | bytes 786440 | tf_op jit(solution)/shard_map/ppermute | solution.py:257
  99.5 0.0 collective-permute-done.5.half_ref
  99.5 0.6 pick.1
  100.0 1.9 %collective-permute-start.6 = (bf16[2,384,128]{2,1,0:T(8,128)(2,1)S(1)}, bf16[2,384,128]{2,1,0:T(8,128)(2,1)S(1)}, u32[]{:S(2)}, u32[]{:S(2)}) collective-permute-start(bf16[2,384,128]{2,1,0:T(8,128)(2,1)S(1)} %pick.1), channel_id=1, source_target_pairs={{0,1},{1,0},{2,3},{3,2},{4,5},{5,4},{6,7},{7,6},{8,9},{9,8},{10,11... | collective-permute-start | bytes 589832 | tf_op jit(solution)/shard_map/ppermute | solution.py:257
  102.0 1.4 %collective-permute-done.6.core_ref = bf16[2,384,128]{2,1,0:T(8,128)(2,1)S(1)} collective-permute-done((bf16[2,384,128]{2,1,0:T(8,128)(2,1)S(1)}, bf16[2,384,128]{2,1,0:T(8,128)(2,1)S(1)}, u32[]{:S(2)}, u32[]{:S(2)}) %collective-permute-start.6) | collective-permute-done | bytes 196640 | tf_op jit(solution)/shard_map/ppermute | solution.py:257
  103.4 0.8 rotate_half.1.done_ref
  104.2 0.0 collective-permute-done.7.far_ref
  104.2 1.6 %rotate.1 = (f32[128,512]{1,0:T(8,128)}, bf16[384,512]{1,0:T(8,128)(2,1)}) custom-call(s32[4]{0:T(128)S(1)} %pad_add_fusion.place_ref, bf16[4,384,128]{2,1,0:T(8,128)(2,1)S(1)} %filter.1.f_ref, bf16[2,384,128]{2,1,0:T(8,128)(2,1)S(1)} %collective-permute-done.5.half_ref, bf16[2,384,128]{2,1,0:T(8,128)(2,1)S(1)} %collective-permute-done.6.core_ref, ...), custom_call_target="tpu_custom_call" | custom-call | tf_op jit(solution)/shard_map/rotate/pallas_call | solution.py:325
  (5 shorter events, 0.0 us)
Async XLA Ops:
  0.6 35.1 %copy-start = (bf16[4,4,6,16,128]{4,3,2,1,0:T(8,128)(2,1)S(1)}, bf16[4,4,6,16,128]{4,3,2,1,0:T(8,128)(2,1)}, u32[]{:S(2)}) copy-start(bf16[4,4,6,16,128]{4,3,2,1,0:T(8,128)(2,1)} %param.4) | copy-start | bytes 1179652
  0.6 11.4 %collective-permute-start.3 = (bf16[384,512]{1,0:T(8,128)(2,1)}, bf16[384,512]{1,0:T(8,128)(2,1)S(1)}, u32[]{:S(2)}, u32[]{:S(2)}) collective-permute-start(bf16[384,512]{1,0:T(8,128)(2,1)} %own_ref.1), channel_id=1, source_target_pairs={{0,2},{2,0},{1,3},{3,1},{4,6},{6,4},{5,7},{7,5},{8,10},{10,8},{9,1... | collective-permute-start | bytes 1179656 | tf_op jit(solution)/shard_map/ppermute | solution.py:257
  6.3 32.7 %collective-permute-start.2 = (bf16[384,512]{1,0:T(8,128)(2,1)}, bf16[384,512]{1,0:T(8,128)(2,1)S(1)}, u32[]{:S(2)}, u32[]{:S(2)}) collective-permute-start(bf16[384,512]{1,0:T(8,128)(2,1)} %own_ref.1), channel_id=1, source_target_pairs={{0,1},{1,0},{2,3},{3,2},{4,5},{5,4},{6,7},{7,6},{8,9},{9,8},{10,11... | collective-permute-start | bytes 1179656 | tf_op jit(solution)/shard_map/ppermute | solution.py:257
  12.0 27.0 %collective-permute-start.4 = (bf16[384,512]{1,0:T(8,128)(2,1)S(1)}, bf16[384,512]{1,0:T(8,128)(2,1)S(1)}, u32[]{:S(2)}, u32[]{:S(2)}) collective-permute-start(bf16[384,512]{1,0:T(8,128)(2,1)S(1)} %collective-permute-done.3.half_ref), channel_id=1, source_target_pairs={{0,1},{1,0},{2,3},{3,2},{4,5},{5,4},{6,7},{7,6},{8,9},{9,8},{10,11... | collective-permute-start | bytes 1179656 | tf_op jit(solution)/shard_map/ppermute | solution.py:257
  23.5 8.1 %collective-permute-start = (bf16[1184,128]{1,0:T(8,128)(2,1)}, bf16[1184,128]{1,0:T(8,128)(2,1)S(1)}, u32[]{:S(2)}, u32[]{:S(2)}) collective-permute-start(bf16[1184,128]{1,0:T(8,128)(2,1)} %get-tuple-element.7), channel_id=1, source_target_pairs={{0,4},{4,8},{8,12},{12,16},{16,20},{20,24},{24,28},{28,32},{32,36}... | collective-permute-start | bytes 909320 | tf_op jit(solution)/shard_map/ppermute | solution.py:272
  24.8 10.9 %collective-permute-start.1 = (bf16[1184,128]{1,0:T(8,128)(2,1)}, bf16[1184,128]{1,0:T(8,128)(2,1)S(1)}, u32[]{:S(2)}, u32[]{:S(2)}) collective-permute-start(bf16[1184,128]{1,0:T(8,128)(2,1)} %get-tuple-element.8), channel_id=1, source_target_pairs={{4,0},{8,4},{12,8},{16,12},{20,16},{24,20},{28,24},{32,28},{36,32}... | collective-permute-start | bytes 909320 | tf_op jit(solution)/shard_map/ppermute | solution.py:273
  26.1 9.6 %copy-start.2 = (bf16[32,128]{1,0:T(8,128)(2,1)S(1)}, bf16[32,128]{1,0:T(8,128)(2,1)}, u32[]{:S(2)}) copy-start(bf16[32,128]{1,0:T(8,128)(2,1)} %get-tuple-element.9.shift_ref) | copy-start | bytes 24580
  26.2 9.5 %copy-start.3 = (f32[4,4]{1,0:T(4,128)S(1)}, f32[4,4]{1,0:T(4,128)}, u32[]{:S(2)}) copy-start(f32[4,4]{1,0:T(4,128)} %coup_ref.1) | copy-start | bytes 196
  35.7 3.3 %copy-start.1 = (bf16[384,512]{1,0:T(8,128)(2,1)S(1)}, bf16[384,512]{1,0:T(8,128)(2,1)}, u32[]{:S(2)}) copy-start(bf16[384,512]{1,0:T(8,128)(2,1)} %own_ref.1) | copy-start | bytes 1179652
  78.3 13.5 %all-to-all-start.2 = ((bf16[32,32,128]{2,1,0:T(8,128)(2,1)}), bf16[32,32,128]{2,1,0:T(8,128)(2,1)S(1)}, u32[]{:S(2)}, u32[]{:S(2)}) async-start(bf16[32,32,128]{2,1,0:T(8,128)(2,1)} %shard_map.60), calls=%async_computation.2 | async-start | bytes 524288 | tf_op jit(solution)/shard_map/all_to_all | solution.py:260
  83.5 16.0 %collective-permute-start.5 = (bf16[2,384,128]{2,1,0:T(8,128)(2,1)S(1)}, bf16[2,384,128]{2,1,0:T(8,128)(2,1)S(1)}, u32[]{:S(2)}, u32[]{:S(2)}) collective-permute-start(bf16[2,384,128]{2,1,0:T(8,128)(2,1)S(1)} %get-tuple-element.10), channel_id=1, source_target_pairs={{0,2},{2,0},{1,3},{3,1},{4,6},{6,4},{5,7},{7,5},{8,10},{10,8},{9,1... | collective-permute-start | bytes 589832 | tf_op jit(solution)/shard_map/ppermute | solution.py:257
  91.8 12.4 %collective-permute-start.7 = (bf16[32,32,128]{2,1,0:T(8,128)(2,1)S(1)}, bf16[32,32,128]{2,1,0:T(8,128)(2,1)S(1)}, u32[]{:S(2)}, u32[]{:S(2)}) collective-permute-start(bf16[32,32,128]{2,1,0:T(8,128)(2,1)S(1)} %all-to-all-done.2.g_ref), channel_id=1, source_target_pairs={{0,1},{1,0},{2,3},{3,2},{4,5},{5,4},{6,7},{7,6},{8,9},{9,8},{10,11... | collective-permute-start | bytes 786440 | tf_op jit(solution)/shard_map/ppermute | solution.py:257
  100.0 3.3 %collective-permute-start.6 = (bf16[2,384,128]{2,1,0:T(8,128)(2,1)S(1)}, bf16[2,384,128]{2,1,0:T(8,128)(2,1)S(1)}, u32[]{:S(2)}, u32[]{:S(2)}) collective-permute-start(bf16[2,384,128]{2,1,0:T(8,128)(2,1)S(1)} %pick.1), channel_id=1, source_target_pairs={{0,1},{1,0},{2,3},{3,2},{4,5},{5,4},{6,7},{7,6},{8,9},{9,8},{10,11... | collective-permute-start | bytes 589832 | tf_op jit(solution)/shard_map/ppermute | solution.py:257
